TPU v7x, 32 devices: a whole 2x2x4 slice. The times are simulated.
32 devices in a mesh: rep: 4 (over y, x), grp: 8 (over z, core).
Axes of the slice: x: 2, y: 2, z: 4, core: 2. Of those that a mesh axis runs over, the one named last changes fastest.
Arguments:
- tokens: bfloat16 [4, 2048, 768], P('rep', 'grp'), may hold values from -6 to 6
- segments: int32 [4, 2048], P('rep', 'grp'), may hold values from 0 to 5, as said below
- block_sets: int32 [4, 16, 16], P('rep'), may hold values from 0 to 1, as said below
- routes: int32 [4, 2048, 2], P('rep', 'grp'), may hold values from 0 to 7, all different within a row; in each aligned block of 256 rows (0 to 255, 256 to 511, ..., all dimensions but the last counted through in order) at most 92 rows name the same one
- qkv_weight: bfloat16 [768, 2, 3, 768], P('grp'), may hold values from -0.21875 to 0.21875
- out_weight: bfloat16 [768, 2, 768], P('grp'), may hold values from -0.875 to 0.875
- ffn_in: bfloat16 [768, 3072], P('grp'), may hold values from -0.21875 to 0.21875
- ffn_out: bfloat16 [768, 3072], P('grp'), may hold values from -0.109375 to 0.109375
- norm_gains: float32 [2, 2, 768], replicated, may hold values from 0.5 to 1.5
- rel_bias: float32 [2, 12, 32], replicated, may hold values from -4 to 4
- router: bfloat16 [768, 8], replicated, may hold values from -0.4375 to 0.4375
- expert_in: bfloat16 [8, 768, 3072], P('grp'), may hold values from -0.21875 to 0.21875
- expert_out: bfloat16 [8, 3072, 768], P('grp'), may hold values from -0.109375 to 0.109375
- cotangent: bfloat16 [4, 2048, 768], P('rep', 'grp'), may hold values from -6 to 6
Outputs:
- final_out: float32 [4, 2048, 768], P('rep', 'grp')
- tokens_grad: float32 [4, 2048, 768], P('rep', 'grp')
- qkv_grad: float32 [768, 2, 3, 768], P('grp')
- out_grad: float32 [768, 2, 768], P('grp')
- ffn_in_grad: float32 [768, 3072], P('grp')
- ffn_out_grad: float32 [768, 3072], P('grp')
- gains_grad: float32 [2, 2, 768], replicated
- bias_grad: float32 [2, 12, 32], replicated
- router_grad: float32 [768, 8], replicated
- expert_in_grad: float32 [8, 768, 3072], P('grp')
- expert_out_grad: float32 [8, 3072, 768], P('grp')
Inputs may be any that keep to these rules, and one draw needn't show every extreme that they name: block_sets is 1 on the diagonal (i = j) and in the first column (j = 0), and 0 above the diagonal (j > i). segments never fall along a sequence. `routes`: each position names 2 different experts; within the 256 positions of one index of grp no expert is named more than 92 times, and some expert is named 92 times.
All inputs are finite; a program needn't handle non-finite values.
Results may differ from a plain program's by a relative error of at most 0.03.
Values may be sent and summed in bfloat16 or wider, within the bound.
No kernel may reach another device: no remote copies, remote signals or barrier semaphores. Data moves between devices by JAX's collectives and lax.ppermute only.
A program may use at most 256 MiB of HBM per device.

v0:
```python
from functools import partial

import jax
import jax.numpy as jnp
from jax import lax
from jax.sharding import PartitionSpec as P

D = 768
HEADS = 12
HEAD = 64
BLK = 128


BUCKET_EDGES = (18, 20, 23, 26, 30, 34, 39, 45, 51, 58, 66, 76, 86, 98, 112)
PRECISE = lax.Precision.HIGHEST
norm_eps = 1e-06
neg_fill = -1e30


def norm_rows(residual, gain_vec):
    return (
        residual
        * lax.rsqrt(jnp.mean(residual * residual, axis=-1, keepdims=True) + norm_eps)
        * gain_vec
    )


def bucket_of(pos_gap):
    clipped = jnp.maximum(pos_gap, 0)
    bucket = jnp.minimum(clipped, 16)
    for edge_at in BUCKET_EDGES:
        bucket = bucket + (clipped >= edge_at).astype(jnp.int32)
    return bucket


def bucket_table(pos_gap):
    return (
        bucket_of(pos_gap)[:, :, None] == jnp.arange(32, dtype=jnp.int32)[None, None, :]
    ).astype(jnp.float32)


def near_bias(bias_table, pos_gap):
    return jnp.einsum("hb,qkb->hqk", bias_table, bucket_table(pos_gap), precision=PRECISE)


def far_bias(bias_table, pos_gap):
    return jnp.broadcast_to(
        bias_table[:, 31][:, None, None], (bias_table.shape[0],) + pos_gap.shape
    )


def near_grad(dscores, pos_gap):
    return jnp.einsum("hqk,qkb->hb", dscores, bucket_table(pos_gap), precision=PRECISE)


def far_grad(dscores, pos_gap):
    column = jnp.sum(dscores, axis=(1, 2))
    return jnp.concatenate(
        [jnp.zeros((dscores.shape[0], 31), jnp.float32), column[:, None]], axis=1
    )


def is_far(pos_gap):
    return jnp.min(pos_gap) >= BUCKET_EDGES[-1]


def split_heads(row_block):
    return row_block.reshape(row_block.shape[0], HEADS, HEAD)


def block_scores(query_rows, key_rows, bias_table, query_pos, key_pos, query_seg, key_seg, blocks):
    pos_gap = query_pos[:, None] - key_pos[None, :]
    raw_scores = (
        jnp.einsum("qhd,khd->hqk", query_rows, key_rows, preferred_element_type=jnp.float32) * 0.125
    )
    bias_terms = lax.cond(is_far(pos_gap), far_bias, near_bias, bias_table, pos_gap)
    block_rows = jnp.take(blocks, query_pos // BLK, axis=0)
    block_hit = jnp.take(block_rows, key_pos // BLK, axis=1)
    allowed = (pos_gap >= 0) & (query_seg[:, None] == key_seg[None, :]) & (block_hit == 1)
    return (jnp.where(allowed[None], raw_scores + bias_terms, neg_fill), allowed, pos_gap)


def fold_keys(
    query_heads, bias_table, local_pos, local_seg, blocks, run_state, piece_all, start_at
):
    piece_keys, piece_values, piece_segs = piece_all
    step_rows = min(query_heads.shape[0], piece_keys.shape[0])

    def one_step(step_idx, inner_state):
        run_peak, run_total, run_accum = inner_state
        row_off = step_idx * step_rows
        keys_blk = split_heads(lax.dynamic_slice_in_dim(piece_keys, row_off, step_rows, 0))
        values_blk = split_heads(lax.dynamic_slice_in_dim(piece_values, row_off, step_rows, 0))
        seg_blk = lax.dynamic_slice_in_dim(piece_segs, row_off, step_rows, 0)
        key_pos = row_off + jnp.arange(step_rows, dtype=jnp.int32)
        scores, allowed, pos_gap = block_scores(
            query_heads, keys_blk, bias_table, local_pos, key_pos, local_seg, seg_blk, blocks
        )
        new_peak = jnp.maximum(run_peak, jnp.max(scores, axis=-1))
        shrink = jnp.exp(run_peak - new_peak)
        weights = jnp.where(allowed[None], jnp.exp(scores - new_peak[:, :, None]), 0.0)
        run_total = run_total * shrink + jnp.sum(weights, axis=-1)
        run_accum = run_accum * shrink[:, :, None] + jnp.einsum(
            "hqk,khd->hqd",
            weights.astype(jnp.bfloat16),
            values_blk,
            preferred_element_type=jnp.float32,
        )
        return (new_peak, run_total, run_accum)

    return lax.fori_loop(0, piece_keys.shape[0] // step_rows, one_step, run_state)


def fold_query_grad(
    query_heads,
    dctx_heads,
    log_norm,
    delta_rows,
    bias_table,
    local_pos,
    local_seg,
    blocks,
    grad_acc,
    piece_all,
    start_at,
):
    piece_keys, piece_values, piece_segs = piece_all
    step_rows = min(query_heads.shape[0], piece_keys.shape[0])

    def one_step(step_idx, inner_grad):
        row_off = step_idx * step_rows
        keys_blk = split_heads(lax.dynamic_slice_in_dim(piece_keys, row_off, step_rows, 0))
        values_blk = split_heads(lax.dynamic_slice_in_dim(piece_values, row_off, step_rows, 0))
        seg_blk = lax.dynamic_slice_in_dim(piece_segs, row_off, step_rows, 0)
        key_pos = row_off + jnp.arange(step_rows, dtype=jnp.int32)
        scores, allowed, pos_gap = block_scores(
            query_heads, keys_blk, bias_table, local_pos, key_pos, local_seg, seg_blk, blocks
        )
        prob_rows = jnp.where(allowed[None], jnp.exp(scores - log_norm[:, :, None]), 0.0)
        dprobs = jnp.einsum(
            "qhd,khd->hqk", dctx_heads, values_blk, preferred_element_type=jnp.float32
        )
        dscores = prob_rows * (dprobs - delta_rows[:, :, None])
        return inner_grad + 0.125 * jnp.einsum(
            "hqk,khd->qhd",
            dscores.astype(jnp.bfloat16),
            keys_blk,
            preferred_element_type=jnp.float32,
        )

    return lax.fori_loop(0, piece_keys.shape[0] // step_rows, one_step, grad_acc)


def fold_key_grad(
    key_heads,
    value_heads,
    local_pos,
    local_seg,
    stats_all,
    bias_table,
    blocks,
    grad_state,
    piece_all,
    start_at,
):
    piece_queries, piece_dctx, piece_segs = piece_all
    lse_all, delta_all = stats_all
    step_rows = min(key_heads.shape[0], piece_queries.shape[0])

    def one_step(step_idx, inner_state):
        key_grad, value_grad, table_grad = inner_state
        row_off = step_idx * step_rows
        query_blk = split_heads(lax.dynamic_slice_in_dim(piece_queries, row_off, step_rows, 0))
        dctx_blk = split_heads(lax.dynamic_slice_in_dim(piece_dctx, row_off, step_rows, 0))
        seg_blk = lax.dynamic_slice_in_dim(piece_segs, row_off, step_rows, 0)
        query_pos = row_off + jnp.arange(step_rows, dtype=jnp.int32)
        lse_blk = lax.dynamic_slice_in_dim(lse_all, row_off, step_rows, 0).T
        delta_blk = lax.dynamic_slice_in_dim(delta_all, row_off, step_rows, 0).T
        scores, allowed, pos_gap = block_scores(
            query_blk, key_heads, bias_table, query_pos, local_pos, seg_blk, local_seg, blocks
        )
        prob_rows = jnp.where(allowed[None], jnp.exp(scores - lse_blk[:, :, None]), 0.0)
        dprobs = jnp.einsum(
            "qhd,khd->hqk", dctx_blk, value_heads, preferred_element_type=jnp.float32
        )
        dscores = prob_rows * (dprobs - delta_blk[:, :, None])
        key_grad = key_grad + 0.125 * jnp.einsum(
            "hqk,qhd->khd",
            dscores.astype(jnp.bfloat16),
            query_blk,
            preferred_element_type=jnp.float32,
        )
        value_grad = value_grad + jnp.einsum(
            "hqk,qhd->khd",
            prob_rows.astype(jnp.bfloat16),
            dctx_blk,
            preferred_element_type=jnp.float32,
        )
        table_grad = table_grad + lax.cond(is_far(pos_gap), far_grad, near_grad, dscores, pos_gap)
        return (key_grad, value_grad, table_grad)

    return lax.fori_loop(0, piece_queries.shape[0] // step_rows, one_step, grad_state)


def attend_forward(residual, gain_vec, w_qkv, w_out, bias_table, local_pos, local_seg, blocks):
    normed = norm_rows(residual, gain_vec).astype(jnp.bfloat16)
    projected = jnp.einsum("td,dcf->tcf", normed, w_qkv, preferred_element_type=jnp.float32).astype(
        jnp.bfloat16
    )
    queries = projected[:, 0]
    keys_mine = projected[:, 1]
    values_mine = projected[:, 2]
    row_count = queries.shape[0]
    start_state = (
        jnp.full((HEADS, row_count), neg_fill, jnp.float32),
        jnp.zeros((HEADS, row_count), jnp.float32),
        jnp.zeros((HEADS, row_count, HEAD), jnp.float32),
    )
    fold_fn = partial(fold_keys, split_heads(queries), bias_table, local_pos, local_seg, blocks)
    run_peak, run_total, run_accum = fold_fn(
        start_state,
        (
            lax.all_gather(keys_mine, "grp", axis=0, tiled=True),
            lax.all_gather(values_mine, "grp", axis=0, tiled=True),
            lax.all_gather(local_seg, "grp", axis=0, tiled=True),
        ),
        jnp.int32(0),
    )
    log_norm = run_peak + jnp.log(run_total)
    context = jnp.transpose(run_accum / run_total[:, :, None], (1, 0, 2)).reshape(
        row_count, HEADS * HEAD
    )
    context_low = context.astype(jnp.bfloat16)
    branch = jnp.dot(context_low, w_out, preferred_element_type=jnp.float32)
    saved = (
        residual,
        normed,
        queries,
        keys_mine,
        values_mine,
        context,
        context_low,
        log_norm,
        None,
    )
    return (residual + branch, saved)


def attend_backward(
    grad_out, saved, gain_vec, w_qkv, w_out, bias_table, local_pos, local_seg, blocks
):
    residual, normed, queries, keys_mine, values_mine, context, context_low, log_norm, kept_kv = (
        saved
    )
    row_count = queries.shape[0]
    grad_low = grad_out.astype(jnp.bfloat16)
    out_part = jnp.einsum("td,te->de", context_low, grad_low, preferred_element_type=jnp.float32)
    dctx_low = jnp.einsum("te,de->td", grad_low, w_out, preferred_element_type=jnp.float32).astype(
        jnp.bfloat16
    )
    delta_rows = jnp.sum(
        (dctx_low.astype(jnp.float32) * context).reshape(row_count, HEADS, HEAD), axis=-1
    )
    query_fn = partial(
        fold_query_grad,
        split_heads(queries),
        split_heads(dctx_low),
        log_norm,
        delta_rows.T,
        bias_table,
        local_pos,
        local_seg,
        blocks,
    )
    zero_query = jnp.zeros((row_count, HEADS, HEAD), jnp.float32)
    query_grad = query_fn(
        zero_query,
        (
            lax.all_gather(keys_mine, "grp", axis=0, tiled=True),
            lax.all_gather(values_mine, "grp", axis=0, tiled=True),
            lax.all_gather(local_seg, "grp", axis=0, tiled=True),
        ),
        jnp.int32(0),
    )
    stats_all = (
        lax.all_gather(log_norm.T, "grp", axis=0, tiled=True),
        lax.all_gather(delta_rows, "grp", axis=0, tiled=True),
    )
    key_fn = partial(
        fold_key_grad,
        split_heads(keys_mine),
        split_heads(values_mine),
        local_pos,
        local_seg,
        stats_all,
        bias_table,
        blocks,
    )
    zero_keys = (
        jnp.zeros((row_count, HEADS, HEAD), jnp.float32),
        jnp.zeros((row_count, HEADS, HEAD), jnp.float32),
        jnp.zeros((HEADS, 32), jnp.float32),
    )
    key_grad, value_grad, table_grad = key_fn(
        zero_keys,
        (
            lax.all_gather(queries, "grp", axis=0, tiled=True),
            lax.all_gather(dctx_low, "grp", axis=0, tiled=True),
            lax.all_gather(local_seg, "grp", axis=0, tiled=True),
        ),
        jnp.int32(0),
    )
    proj_grad = (
        jnp.stack([query_grad, key_grad, value_grad], axis=1)
        .reshape(row_count, 3, HEADS * HEAD)
        .astype(jnp.bfloat16)
    )
    qkv_part = jnp.einsum("td,tcf->dcf", normed, proj_grad, preferred_element_type=jnp.float32)
    normed_grad = jnp.einsum("tcf,dcf->td", proj_grad, w_qkv, preferred_element_type=jnp.float32)
    unused_out, pull_back = jax.vjp(norm_rows, residual, gain_vec)
    residual_grad, gain_grad = pull_back(normed_grad)
    return (grad_out + residual_grad, qkv_part, out_part, gain_grad, table_grad)


def body(
    tokens,
    segments,
    block_sets,
    routes,
    qkv_weight,
    out_weight,
    ffn_in,
    ffn_out,
    norm_gains,
    rel_bias,
    router,
    expert_in,
    expert_out,
    cotangent,
):
    full_qkv, full_out, full_in, full_down = (
        lax.all_gather(qkv_weight, "grp", axis=0, tiled=True),
        lax.all_gather(out_weight, "grp", axis=0, tiled=True),
        lax.all_gather(ffn_in, "grp", axis=0, tiled=True),
        lax.all_gather(ffn_out, "grp", axis=0, tiled=True),
    )
    row_count = tokens.shape[1]
    local_pos = lax.axis_index("grp") * row_count + jnp.arange(row_count, dtype=jnp.int32)
    local_seg = segments[0]
    blocks = block_sets[0]
    stream_in = tokens[0].astype(jnp.float32)
    first_out, saved_first = attend_forward(
        stream_in,
        norm_gains[0, 0],
        full_qkv[:, 0],
        full_out[:, 0],
        rel_bias[0],
        local_pos,
        local_seg,
        blocks,
    )
    normed_ffn = norm_rows(first_out, norm_gains[0, 1]).astype(jnp.bfloat16)
    pre_ffn = jnp.dot(normed_ffn, full_in, preferred_element_type=jnp.float32)
    hidden_ffn = jax.nn.gelu(pre_ffn).astype(jnp.bfloat16)
    after_ffn = first_out + jnp.einsum(
        "tf,df->td", hidden_ffn, full_down, preferred_element_type=jnp.float32
    )
    second_out, saved_second = attend_forward(
        after_ffn,
        norm_gains[1, 0],
        full_qkv[:, 1],
        full_out[:, 1],
        rel_bias[1],
        local_pos,
        local_seg,
        blocks,
    )
    normed_moe = norm_rows(second_out, norm_gains[1, 1]).astype(jnp.bfloat16)
    normed_wide = normed_moe.astype(jnp.float32)
    router_wide = router.astype(jnp.float32)
    logits = jnp.dot(normed_wide, router_wide, precision=PRECISE)
    experts_all = router.shape[1]
    groups = lax.axis_size("grp")
    per_group = experts_all // groups
    capacity = row_count * 2 * 10 // (7 * experts_all) + 1
    chosen = routes[0]
    chosen_hot = (
        chosen[:, :, None] == jnp.arange(experts_all, dtype=jnp.int32)[None, None, :]
    ).astype(jnp.float32)
    selected = jnp.sum(logits[:, None, :] * chosen_hot, axis=-1)
    gate_probs = jax.nn.softmax(selected, axis=-1)
    flat_ids = chosen.reshape(-1)
    flat_hot = (flat_ids[:, None] == jnp.arange(experts_all, dtype=jnp.int32)[None, :]).astype(
        jnp.int32
    )
    slot_ids = jnp.sum((jnp.cumsum(flat_hot, axis=0) - 1) * flat_hot, axis=1)
    send_rows = (
        jnp.zeros((experts_all, capacity, D), jnp.bfloat16)
        .at[flat_ids, slot_ids]
        .set(jnp.repeat(normed_moe, 2, axis=0))
    )
    received = lax.all_to_all(
        send_rows.reshape(groups, per_group, capacity, D),
        "grp",
        split_axis=0,
        concat_axis=0,
        tiled=True,
    )
    pre_expert = jnp.einsum(
        "secd,edf->secf", received, expert_in, preferred_element_type=jnp.float32
    )
    hidden_expert = jax.nn.gelu(pre_expert).astype(jnp.bfloat16)
    made_rows = jnp.einsum(
        "secf,efd->secd", hidden_expert, expert_out, preferred_element_type=jnp.float32
    ).astype(jnp.bfloat16)
    returned = lax.all_to_all(made_rows, "grp", split_axis=0, concat_axis=0, tiled=True).reshape(
        experts_all, capacity, D
    )
    picked = returned[flat_ids, slot_ids].reshape(row_count, 2, D).astype(jnp.float32)
    final_out = second_out + jnp.sum(gate_probs[:, :, None] * picked, axis=1)
    grad_final = cotangent[0].astype(jnp.float32)
    gate_grad = jnp.sum(grad_final[:, None, :] * picked, axis=-1)
    select_grad = gate_probs * (gate_grad - jnp.sum(gate_probs * gate_grad, axis=-1, keepdims=True))
    logit_grad = jnp.sum(select_grad[:, :, None] * chosen_hot, axis=1)
    router_part = jnp.dot(normed_wide.T, logit_grad, precision=PRECISE)
    made_grad = (
        (gate_probs[:, :, None] * grad_final[:, None, :])
        .astype(jnp.bfloat16)
        .reshape(2 * row_count, D)
    )
    send_grad = (
        jnp.zeros((experts_all, capacity, D), jnp.bfloat16).at[flat_ids, slot_ids].set(made_grad)
    )
    recv_grad = lax.all_to_all(
        send_grad.reshape(groups, per_group, capacity, D),
        "grp",
        split_axis=0,
        concat_axis=0,
        tiled=True,
    )
    hidden_grad = jnp.einsum(
        "secd,efd->secf", recv_grad, expert_out, preferred_element_type=jnp.float32
    )
    unused_gelu, gelu_expert = jax.vjp(jax.nn.gelu, pre_expert)
    pre_grad = gelu_expert(hidden_grad)[0].astype(jnp.bfloat16)
    rows_grad = jnp.einsum(
        "secf,edf->secd", pre_grad, expert_in, preferred_element_type=jnp.float32
    ).astype(jnp.bfloat16)
    back_grad = lax.all_to_all(rows_grad, "grp", split_axis=0, concat_axis=0, tiled=True).reshape(
        experts_all, capacity, D
    )
    assign_grad = back_grad[flat_ids, slot_ids].reshape(row_count, 2, D).astype(jnp.float32)
    normed_moe_grad = jnp.dot(logit_grad, router_wide.T, precision=PRECISE) + jnp.sum(
        assign_grad, axis=1
    )
    unused_moe, pull_moe = jax.vjp(norm_rows, second_out, norm_gains[1, 1])
    moe_resid_grad, moe_gain_grad = pull_moe(normed_moe_grad)
    grad_second = grad_final + moe_resid_grad
    grad_ffn, qkv_part_b, out_part_b, gain_grad_b, table_grad_b = attend_backward(
        grad_second,
        saved_second,
        norm_gains[1, 0],
        full_qkv[:, 1],
        full_out[:, 1],
        rel_bias[1],
        local_pos,
        local_seg,
        blocks,
    )
    down_low = grad_ffn.astype(jnp.bfloat16)
    down_part = jnp.einsum("tf,td->df", hidden_ffn, down_low, preferred_element_type=jnp.float32)
    hidden_ffn_grad = jnp.einsum(
        "td,df->tf", down_low, full_down, preferred_element_type=jnp.float32
    )
    unused_dense, gelu_dense = jax.vjp(jax.nn.gelu, pre_ffn)
    pre_ffn_grad = gelu_dense(hidden_ffn_grad)[0].astype(jnp.bfloat16)
    in_part = jnp.einsum("td,tf->df", normed_ffn, pre_ffn_grad, preferred_element_type=jnp.float32)
    normed_ffn_grad = jnp.einsum(
        "tf,df->td", pre_ffn_grad, full_in, preferred_element_type=jnp.float32
    )
    unused_ffn, pull_ffn = jax.vjp(norm_rows, first_out, norm_gains[0, 1])
    ffn_resid_grad, ffn_gain_grad = pull_ffn(normed_ffn_grad)
    grad_first = grad_ffn + ffn_resid_grad
    grad_tokens, qkv_part_a, out_part_a, gain_grad_a, table_grad_a = attend_backward(
        grad_first,
        saved_first,
        norm_gains[0, 0],
        full_qkv[:, 0],
        full_out[:, 0],
        rel_bias[0],
        local_pos,
        local_seg,
        blocks,
    )
    qkv_all = jnp.stack([qkv_part_a, qkv_part_b], axis=1)
    out_all = jnp.stack([out_part_a, out_part_b], axis=1)
    qkv_shard, out_shard, in_shard, down_shard = (
        lax.psum_scatter(
            qkv_all.astype(jnp.bfloat16), "grp", scatter_dimension=0, tiled=True
        ).astype(jnp.float32),
        lax.psum_scatter(
            out_all.astype(jnp.bfloat16), "grp", scatter_dimension=0, tiled=True
        ).astype(jnp.float32),
        lax.psum_scatter(
            in_part.astype(jnp.bfloat16), "grp", scatter_dimension=0, tiled=True
        ).astype(jnp.float32),
        lax.psum_scatter(
            down_part.astype(jnp.bfloat16), "grp", scatter_dimension=0, tiled=True
        ).astype(jnp.float32),
    )
    expert_out_part = jnp.einsum(
        "secf,secd->efd", hidden_expert, recv_grad, preferred_element_type=jnp.float32
    )
    expert_in_part = jnp.einsum(
        "secd,secf->edf", received, pre_grad, preferred_element_type=jnp.float32
    )
    qkv_sum, out_sum, in_sum, down_sum, expert_in_sum, expert_out_sum = (
        lax.psum(qkv_shard.astype(jnp.bfloat16), "rep").astype(jnp.float32),
        lax.psum(out_shard.astype(jnp.bfloat16), "rep").astype(jnp.float32),
        lax.psum(in_shard.astype(jnp.bfloat16), "rep").astype(jnp.float32),
        lax.psum(down_shard.astype(jnp.bfloat16), "rep").astype(jnp.float32),
        lax.psum(expert_in_part.astype(jnp.bfloat16), "rep").astype(jnp.float32),
        lax.psum(expert_out_part.astype(jnp.bfloat16), "rep").astype(jnp.float32),
    )
    gain_all = jnp.stack(
        [jnp.stack([gain_grad_a, ffn_gain_grad]), jnp.stack([gain_grad_b, moe_gain_grad])]
    )
    table_all = jnp.stack([table_grad_a, table_grad_b])
    gain_sum, table_sum, router_sum = lax.psum((gain_all, table_all, router_part), ("rep", "grp"))
    return (
        final_out[None],
        grad_tokens[None],
        qkv_sum,
        out_sum,
        in_sum,
        down_sum,
        gain_sum,
        table_sum,
        router_sum,
        expert_in_sum,
        expert_out_sum,
    )


def solution(mesh):
    return jax.shard_map(
        body,
        mesh=mesh,
        in_specs=(
            P("rep", "grp", None),
            P("rep", "grp"),
            P("rep", None, None),
            P("rep", "grp", None),
            P("grp", None, None, None),
            P("grp", None, None),
            P("grp", None),
            P("grp", None),
            P(),
            P(),
            P(),
            P("grp", None, None),
            P("grp", None, None),
            P("rep", "grp", None),
        ),
        out_specs=(
            P("rep", "grp", None),
            P("rep", "grp", None),
            P("grp", None, None, None),
            P("grp", None, None),
            P("grp", None),
            P("grp", None),
            P(),
            P(),
            P(),
            P("grp", None, None),
            P("grp", None, None),
        ),
        check_vma=False,
    )
```

profile of v0, /device:TPU:0, one launch (start us, length us, event | category | flops | bytes accessed | tf_op | source)
XLA Modules:
  0.0 2221.6 jit_solution(17873094480550959390)
XLA Ops:
  12.1 72.1 %all-gather.20.cloned.1.call-done = bf16[768,2,3,768]{3,0,2,1:T(8,128)(2,1)} async-done(((bf16[96,2,3,768]{3,0,2,1:T(8,128)(2,1)}), bf16[768,2,3,768]{3,0,2,1:T(8,128)(2,1)}) %all-gather.20.cloned.1.call-update) | async-done | bytes 7077904 | tf_op jit(solution)/shard_map/all_gather | solution.py:342
  102.0 23.5 %all-gather.32.cloned.1.call-done = bf16[2048,1,768]{2,0,1:T(8,128)(2,1)} async-done(((bf16[256,1,768]{2,0,1:T(8,128)(2,1)}), bf16[2048,1,768]{2,0,1:T(8,128)(2,1)}) %all-gather.32.cloned.1.call-update) | async-done | bytes 3145744 | tf_op jit(solution)/shard_map/all_gather | solution.py:223
  130.3 34.6 %all-gather.34.cloned.1.call-done = bf16[2048,1,768]{2,0,1:T(8,128)(2,1)} async-done(((bf16[256,1,768]{2,0,1:T(8,128)(2,1)}), bf16[2048,1,768]{2,0,1:T(8,128)(2,1)}) %all-gather.34.cloned.1.call-update) | async-done | bytes 3145744 | tf_op jit(solution)/shard_map/all_gather | solution.py:224
  169.8 161.9 %while.130 = (s32[]{:T(128)}, f32[12,256]{1,0:T(8,128)S(1)}, f32[12,256]{1,0:T(8,128)S(1)}, f32[12,256,64]{1,2,0:T(8,128)}, s32[1,256]{1,0:T(1,128)S(1)}, /*inde...) while((s32[]{:T(128)}, f32[12,256]{1,0:T(8,128)S(1)}, ...), condition=%wide.region_7.10_spmd.clone.clone.clone, body=%wide.region_1.9_spmd.clone.clone.clone.sunk | while | flops 517580288 | bytes 49736588 | solution.py:111
  355.4 32.7 %all-gather.36.cloned.1.call-done = bf16[2048,1,768]{2,0,1:T(8,128)(2,1)} async-done(((bf16[256,1,768]{2,0,1:T(8,128)(2,1)}), bf16[2048,1,768]{2,0,1:T(8,128)(2,1)}) %all-gather.36.cloned.1.call-update) | async-done | bytes 3145744 | tf_op jit(solution)/shard_map/all_gather | solution.py:223
  392.8 34.1 %all-gather.38.cloned.1.call-done = bf16[2048,1,768]{2,0,1:T(8,128)(2,1)} async-done(((bf16[256,1,768]{2,0,1:T(8,128)(2,1)}), bf16[2048,1,768]{2,0,1:T(8,128)(2,1)}) %all-gather.38.cloned.1.call-update) | async-done | bytes 3145744 | tf_op jit(solution)/shard_map/all_gather | solution.py:224
  431.7 161.3 %while.131 = (s32[]{:T(128)}, f32[12,256]{1,0:T(8,128)S(1)}, f32[12,256]{1,0:T(8,128)S(1)}, f32[12,256,64]{1,2,0:T(8,128)}, s32[1,256]{1,0:T(1,128)S(1)}, /*inde...) while((s32[]{:T(128)}, f32[12,256]{1,0:T(8,128)S(1)}, ...), condition=%wide.region_16.19_spmd.clone.clone.clone, body=%wide.region_10.18_spmd.clone.clone.clone.sunk | while | flops 517580288 | bytes 49736588 | solution.py:111
  598.5 47.7 %scatter_fusion = bf16[8,92,768]{2,0,1:T(8,128)(2,1)S(1)} fusion(bf16[8,92,768]{2,0,1:T(8,128)(2,1)S(1)} %broadcast.1411.clone, s32[512]{0:T(512)S(1)} %bitcast.665, bf16[512,768]{1,0:T(8,128)(2,1)} %reshape.748), kind=kCustom, calls=%fused_computation.14 | custom fusion | bytes 2363392 | tf_op jit(solution)/shard_map/scatter | solution.py:400
  662.0 47.7 %scatter_fusion.1 = bf16[8,92,768]{2,0,1:T(8,128)(2,1)S(1)} fusion(bf16[8,92,768]{2,0,1:T(8,128)(2,1)S(1)} %broadcast.1411.clone.1, s32[512]{0:T(512)S(1)} %bitcast.666, bf16[512,768]{1,0:T(8,128)(2,1)} %multiply_convert_fusion.1), kind=kCustom, calls=%fused_computation.15 | custom fusion | bytes 2363392 | tf_op jit(solution)/shard_map/scatter | solution.py:432
  734.6 10.8 all-to-all-done.2
  749.8 12.2 fusion.166
  801.8 11.1 all-to-all-done.3
  834.7 16.3 all_gather.70
  852.3 15.6 all_gather.72
  867.8 182.0 %while.132 = (s32[]{:T(128)}, f32[256,12,64]{0,2,1:T(8,128)}, bf16[2048,768]{0,1:T(8,128)(2,1)}, s32[1,256]{1,0:T(1,128)S(1)}, s32[2048]{0:T(1024)S(1)}, /*index...) while((s32[]{:T(128)}, f32[256,12,64]{0,2,1:T(8,128)}, ...), condition=%wide.region_37.40_spmd.clone.clone.clone, body=%wide.region_33.39_spmd.clone.clone.clone.sunk | while | flops 616655360 | bytes 28199744 | solution.py:151
  1051.9 217.0 %while.133 = (s32[]{:T(128)}, f32[256,12,64]{0,2,1:T(8,128)}, f32[256,12,64]{0,2,1:T(8,128)}, f32[12,32]{1,0:T(8,128)S(1)}, bf16[2048,768]{1,0:T(8,128)(2,1)}, /...) while((s32[]{:T(128)}, f32[256,12,64]{0,2,1:T(8,128)}, ...), condition=%wide.region_45.48_spmd.clone.clone.clone, body=%wide.region_38.47_spmd.clone.clone.clone.sunk | while | flops 1025666304 | bytes 62595948 | solution.py:202
  1296.6 59.9 %all_gather.74 = f32[2048,12]{0,1:T(8,128)} all-gather(f32[256,12]{0,1:T(8,128)S(1)} %bitcast.732), channel_id=1, replica_groups=mesh['rep'=4,'grp'=8] {'grp'}, dimensions={0}, use_global_device_ids=true | all-gather | bytes 110592 | tf_op jit(solution)/shard_map/all_gather | solution.py:286
  1364.1 187.9 %while.134 = (s32[]{:T(128)}, f32[256,12,64]{0,2,1:T(8,128)}, bf16[2048,768]{0,1:T(8,128)(2,1)}, s32[1,256]{1,0:T(1,128)S(1)}, s32[2048]{0:T(1024)S(1)}, /*index...) while((s32[]{:T(128)}, f32[256,12,64]{0,2,1:T(8,128)}, ...), condition=%wide.region_53.56_spmd.clone.clone.clone, body=%wide.region_49.55_spmd.clone.clone.clone.sunk | while | flops 616655360 | bytes 28347284 | solution.py:151
  1554.1 15.4 all_gather.76
  1578.0 216.3 %while.135 = (s32[]{:T(128)}, f32[256,12,64]{0,2,1:T(8,128)}, f32[256,12,64]{0,2,1:T(8,128)}, f32[12,32]{1,0:T(8,128)S(1)}, bf16[2048,768]{1,0:T(8,128)(2,1)}, /...) while((s32[]{:T(128)}, f32[256,12,64]{0,2,1:T(8,128)}, ...), condition=%wide.region_61.64_spmd.clone.clone.clone, body=%wide.region_54.63_spmd.clone.clone.clone.sunk | while | flops 1025666304 | bytes 62595948 | solution.py:202
  1811.6 11.6 fusion.186
  1823.2 140.4 %reduce-scatter.5.cloned.1.call-done = bf16[96,2,3,768]{3,0,2,1:T(8,128)(2,1)} async-done(((bf16[768,2,3,768]{3,0,2,1:T(8,128)(2,1)}), bf16[96,2,3,768]{3,0,2,1:T(8,128)(2,1)}) %reduce-scatter.5.cloned.1.call-update) | async-done | bytes 884752 | tf_op jit(solution)/shard_map/reduce_scatter | solution.py:498
  1968.3 39.9 %all-reduce.2 = (f32[2,2,768]{2,1,0:T(2,128)}, f32[2,12,32]{2,1,0:T(8,128)S(1)}, f32[768,8]{0,1:T(8,128)}) all-reduce(f32[2,2,768]{2,1,0:T(2,128)S(1)} %pad_maximum_fusion.9, f32[2,12,32]{2,1,0:T(8,128)S(1)} %pad_maximum_fusion.8, f32[768,8]{0,1:T(8,128)S(1)} %fusion.304), channel_id=1, replica_groups=mesh['rep'=4,'grp'=8] {'rep','grp'}, use_global_device_ids=true, to_apply=%region_75.78 | all-reduce | flops 9984 | bytes 79872 | tf_op jit(solution)/shard_map/psum | solution.py:529
  2010.0 187.2 %all-reduce.6.cloned.1.call-done = (bf16[96,2,3,768]{3,0,2,1:T(8,128)(2,1)}, bf16[96,2,768]{2,0,1:T(8,128)(2,1)}, bf16[96,3072]{1,0:T(8,128)(2,1)}, bf16[96,3072...) async-done(((bf16[96,2,3,768]{3,0,2,1:T(8,128)(2,1)}, bf16[96,2,768]{2,0,1:T(8,128)(2,1)}, bf16[96,3072]{1,0:T(8,128)(2,1)}, ...) | async-done | bytes 11796496 | tf_op jit(solution)/shard_map/psum | solution.py:518
  (1845 shorter events, 1686.1 us)
Async XLA Ops:
  7.2 651.7 %copy-start = (bf16[768,8]{0,1:T(8,128)(2,1)S(1)}, bf16[768,8]{0,1:T(8,128)(2,1)}, u32[]{:S(2)}) copy-start(bf16[768,8]{0,1:T(8,128)(2,1)} %param.56) | copy-start | bytes 36868
  7.2 77.0 %all-gather.20.cloned.1.call-start = ((), (), s32[]{:S(2)}) async-start(), calls=%async_computation.8 | async-start | bytes 7962624 | tf_op jit(solution)/shard_map/all_gather | solution.py:342
  9.4 116.1 %all-gather.32.cloned.1.call-start = ((), (), s32[]{:S(2)}) async-start(), calls=%async_computation.18 | async-start | bytes 3538944 | tf_op jit(solution)/shard_map/all_gather | solution.py:223
  10.9 324.9 %copy-start.62 = (f32[768]{0:T(1024)}, f32[768]{0:T(1024)S(1)}, u32[]{:S(2)}) copy-start(f32[768]{0:T(1024)S(1)} %get-tuple-element.3685) | copy-start | bytes 9220
  88.5 76.5 %all-gather.34.cloned.1.call-start = ((), (), s32[]{:S(2)}) async-start(), calls=%async_computation.19 | async-start | bytes 3538944 | tf_op jit(solution)/shard_map/all_gather | solution.py:224
  89.2 244.6 %all-gather.22.cloned.1.call-start = ((), (), s32[]{:S(2)}) async-start(), calls=%async_computation.9 | async-start | bytes 2654208 | tf_op jit(solution)/shard_map/all_gather | solution.py:343
  90.0 245.8 %all-gather.24.cloned.1.call-start = ((), (), s32[]{:S(2)}) async-start(), calls=%async_computation.10 | async-start | bytes 5308416 | tf_op jit(solution)/shard_map/all_gather | solution.py:344
  90.6 251.0 %all-gather.26.cloned.1.call-start = ((), (), s32[]{:S(2)}) async-start(), calls=%async_computation.11 | async-start | bytes 5308416 | tf_op jit(solution)/shard_map/all_gather | solution.py:345
  91.2 296.9 %all-gather.36.cloned.1.call-start = ((), (), s32[]{:S(2)}) async-start(), calls=%async_computation.20 | async-start | bytes 3538944 | tf_op jit(solution)/shard_map/all_gather | solution.py:223
  351.5 75.4 %all-gather.38.cloned.1.call-start = ((), (), s32[]{:S(2)}) async-start(), calls=%async_computation.21 | async-start | bytes 3538944 | tf_op jit(solution)/shard_map/all_gather | solution.py:224
  594.2 189.5 %copy-start.25 = (f32[12,256,64]{1,2,0:T(8,128)}, f32[12,256,64]{1,2,0:T(8,128)S(1)}, u32[]{:S(2)}) copy-start(f32[12,256,64]{1,2,0:T(8,128)S(1)} %get-tuple-element.3864) | copy-start | bytes 2359300
  647.4 63.6 %all-to-all-start = ((bf16[8,1,92,768]{3,2,1,0:T(8,128)(2,1)}), bf16[8,1,92,768]{3,2,1,0:T(8,128)(2,1)}, u32[]{:S(2)}, u32[]{:S(2)}) async-start(bf16[8,1,92,768]{3,2,1,0:T(8,128)(2,1)} %copy.406), calls=%async_computation | async-start | bytes 2359296 | tf_op jit(solution)/shard_map/all_to_all | solution.py:402
  651.6 400.3 %all-gather.40.cloned.1.call-start = ((), (), s32[]{:S(2)}) async-start(), calls=%async_computation.22 | async-start | bytes 3538944 | tf_op jit(solution)/shard_map/all_gather | solution.py:307
  710.9 34.4 %all-to-all-start.2 = ((bf16[8,1,92,768]{3,2,1,0:T(8,128)(2,1)}), bf16[8,1,92,768]{3,2,1,0:T(8,128)(2,1)}, u32[]{:S(2)}, u32[]{:S(2)}) async-start(bf16[8,1,92,768]{3,2,1,0:T(8,128)(2,1)} %copy.412), calls=%async_computation.2 | async-start | bytes 2359296 | tf_op jit(solution)/shard_map/all_to_all | solution.py:434
  745.4 33.8 %all-to-all-start.1 = ((bf16[8,1,92,768]{3,2,1,0:T(8,128)(2,1)}), bf16[8,1,92,768]{3,2,1,0:T(8,128)(2,1)}, u32[]{:S(2)}, u32[]{:S(2)}) async-start(bf16[8,1,92,768]{3,2,1,0:T(8,128)(2,1)} %fusion.221), calls=%async_computation.1 | async-start | bytes 2359296 | tf_op jit(solution)/shard_map/all_to_all | solution.py:416
  779.2 33.7 %all-to-all-start.3 = ((bf16[8,1,92,768]{3,2,1,0:T(8,128)(2,1)}), bf16[8,1,92,768]{3,2,1,0:T(8,128)(2,1)}, u32[]{:S(2)}, u32[]{:S(2)}) async-start(bf16[8,1,92,768]{3,2,1,0:T(8,128)(2,1)} %fusion.216), calls=%async_computation.3 | async-start | bytes 2359296 | tf_op jit(solution)/shard_map/all_to_all | solution.py:449
  783.5 268.5 %all-gather.28.cloned.1.call-start = ((), (), s32[]{:S(2)}) async-start(), calls=%async_computation.12 | async-start | bytes 3538944 | tf_op jit(solution)/shard_map/all_gather | solution.py:308
  830.3 747.6 %all-gather.42.cloned.1.call-start = ((), (), s32[]{:S(2)}) async-start(), calls=%async_computation.23 | async-start | bytes 3538944 | tf_op jit(solution)/shard_map/all_gather | solution.py:307
  831.0 746.9 %all-gather.30.cloned.1.call-start = ((), (), s32[]{:S(2)}) async-start(), calls=%async_computation.13 | async-start | bytes 3538944 | tf_op jit(solution)/shard_map/all_gather | solution.py:308
  1290.8 532.4 %reduce-scatter.7.cloned.1.call-start = ((), (), s32[]{:S(2)}) async-start(), calls=%async_computation.15 | async-start | bytes 2654208 | tf_op jit(solution)/shard_map/reduce_scatter | solution.py:501
  1294.6 528.5 %reduce-scatter.9.cloned.1.call-start = ((), (), s32[]{:S(2)}) async-start(), calls=%async_computation.16 | async-start | bytes 5308416 | tf_op jit(solution)/shard_map/reduce_scatter | solution.py:504
  1363.4 459.7 %reduce-scatter.11.cloned.1.call-start = ((), (), s32[]{:S(2)}) async-start(), calls=%async_computation.17 | async-start | bytes 5308416 | tf_op jit(solution)/shard_map/reduce_scatter | solution.py:507
  1577.9 385.7 %reduce-scatter.5.cloned.1.call-start = ((), (), s32[]{:S(2)}) async-start(), calls=%async_computation.14 | async-start | bytes 7962624 | tf_op jit(solution)/shard_map/reduce_scatter | solution.py:498
  1802.7 394.5 %all-reduce.6.cloned.1.call-start = ((), (), s32[]{:S(2)}) async-start(), calls=%async_computation.24 | async-start | bytes 23592960 | tf_op jit(solution)/shard_map/psum | solution.py:518
  (208 other events, 1220.4 us)
Sparse Core Ops, SparseCore 0:
  10.2 73.9 all-gather.19
  88.6 36.9 all-gather.31
  127.8 37.1 all-gather.33
  167.0 30.4 all-gather.21
  199.0 50.8 all-gather.23
  251.3 50.5 all-gather.25
  351.6 36.4 all-gather.35
  389.7 37.1 all-gather.37
  659.0 48.9 all-gather.39
  830.4 38.9 all-gather.27
  871.1 37.1 all-gather.41
  1290.9 84.5 all-gather.29
  1377.9 35.4 reduce-scatter.6
  1415.5 54.1 reduce-scatter.8
  1578.0 53.2 reduce-scatter.10
  1802.8 160.6 reduce-scatter.4
  1967.9 229.2 all-reduce.5
where the time goes:
time: 2250 us; the launch traced here: 2220 us
  matrix products  663 us (29%)
  local copies, waits for them, and re-layouts  636 us (28%)
  waiting for transfers between devices  560 us (25%)
  blocking collectives  156 us (7%)
  other arithmetic  133 us (6%)
  loops' own time  38.5 us (2%)
    psum x1, waiting for transfers between devices, body(): lax.psum(qkv_shard.astype(jnp.bfloat16), 'rep').astype(jnp.float32)  187 us
    dot_general x48, matrix products, block_scores(): jnp.einsum('qhd,khd->hqk', query_rows, key_rows, preferred_element_type=j...  163 us
    dot_general x36, matrix products, near_bias(): jnp.einsum('hb,qkb->hqk', bias_table, bucket_table(pos_gap), precision=PR...  142 us
    reduce_scatter x1, waiting for transfers between devices, body(): lax.psum_scatter(qkv_all.astype(jnp.bfloat16), 'grp', scatter_dimension=0...  140 us
    cond x36, local copies, waits for them, and re-layouts, block_scores(): lax.cond(is_far(pos_gap), far_bias, near_bias, bias_table, pos_gap)  118 us
    dot_general x16, matrix products, one_step(): jnp.einsum('hqk,khd->qhd', dscores.astype(jnp.bfloat16), keys_blk, prefer...  79.6 us
    all_gather x2, blocking collectives, attend_backward(): lax.all_gather(log_norm.T, 'grp', axis=0, tiled=True)  76.1 us
    all_gather x1, waiting for transfers between devices, body(): lax.all_gather(qkv_weight, 'grp', axis=0, tiled=True)  72.1 us
  transfers between devices with their start and end apart: 21, of which 10 were waited for; matrix products, arithmetic and copies ran while one was open for 51% of the time, Pallas kernels for 0%

commit v1 on v0

v1 whole, which is shorter than its diff:
```python
from functools import partial

import jax
import jax.numpy as jnp
from jax import lax
from jax.experimental import pallas as pl
from jax.experimental.pallas import tpu as pltpu
from jax.sharding import PartitionSpec as P

D = 768
HEADS = 12
HEAD = 64
PAIRS = 6
BLK = 128
ROWS = 256

BUCKET_EDGES = (18, 20, 23, 26, 30, 34, 39, 45, 51, 58, 66, 76, 86, 98, 112)
PRECISE = lax.Precision.HIGHEST
norm_eps = 1e-06
NEG = -1e30
VMEM_LIMIT = 60 * 1024 * 1024
F32 = jnp.float32
BF16 = jnp.bfloat16


def mm(a, b, ca, cb):
    return lax.dot_general(a, b, (((ca,), (cb,)), ((), ())), preferred_element_type=F32)


def norm_rows(residual, gain_vec):
    return (
        residual
        * lax.rsqrt(jnp.mean(residual * residual, axis=-1, keepdims=True) + norm_eps)
        * gain_vec
    )


def bucket_of(pos_gap):
    clipped = jnp.maximum(pos_gap, 0)
    bucket = jnp.minimum(clipped, 16)
    for edge_at in BUCKET_EDGES:
        bucket = bucket + (clipped >= edge_at).astype(jnp.int32)
    return bucket


def gap_hot():
    gaps = jnp.arange(2 * BLK, dtype=jnp.int32)
    return (bucket_of(gaps)[:, None] == jnp.arange(32, dtype=jnp.int32)[None, :]).astype(F32)


def pair_diag(ref, p, off):
    x = ref[128 * p : 128 * p + 128, pl.ds(off, 128)]
    z = jnp.zeros((64, 128), x.dtype)
    top = jnp.concatenate([x[:64], z], axis=0)
    low = jnp.concatenate([z, x[64:]], axis=0)
    return jnp.concatenate([top, low], axis=1)


def fill_tiles(gap_ref, far_ref, tile_ref):
    rows = lax.broadcasted_iota(jnp.int32, (128, 128), 0)
    cols = lax.broadcasted_iota(jnp.int32, (128, 128), 1)
    causal = cols >= rows
    for h in range(HEADS):
        x = jnp.broadcast_to(gap_ref[h : h + 1, :], (128, 256))
        r = pltpu.roll(x, 0, 1, stride=1, stride_axis=0)
        tile_ref[h, :, 0:128] = jnp.where(causal, r[:, :128], NEG)
        tile_ref[h, :, 128:256] = r[:, 128:]
        half = 128 * (h % 2)
        tile_ref[h, :, 256:384] = jnp.broadcast_to(
            far_ref[h // 2 : h // 2 + 1, half : half + 128], (128, 128)
        )


def seg_ok(segc_ref, segr_ref, i, j):
    kcol = segc_ref[pl.ds(pl.multiple_of(j * 128, 128), 128), :]
    qrow = segr_ref[pl.ds(i, 1), :]
    ok = kcol == qrow
    return jnp.concatenate([ok, ok], axis=1)


def pair_tile(tile_ref, p, dd):
    off = pl.multiple_of(dd * 128, 128)
    return jnp.concatenate(
        [tile_ref[2 * p, :, pl.ds(off, 128)], tile_ref[2 * p + 1, :, pl.ds(off, 128)]], axis=1
    )


def fwd_kernel(
    code_ref, me_ref, qt_ref, k_ref, vt_ref, gap_ref, far_ref, segc_ref, segr_ref,
    ctxt_ref, ctxb_ref, lse_ref, tile_ref, m_ref, l_ref, acc_ref,
):
    fill_tiles(gap_ref, far_ref, tile_ref)
    me = me_ref[0]

    def one_query(qi, _):
        i = me * 2 + qi
        qoff = pl.multiple_of(qi * 128, 128)
        m_ref[...] = jnp.full_like(m_ref, NEG)
        l_ref[...] = jnp.zeros_like(l_ref)
        acc_ref[...] = jnp.zeros_like(acc_ref)

        def visit(j, near):
            koff = pl.multiple_of(j * 128, 128)
            if near:
                dd = jnp.minimum(i - j, 2)
                ok = seg_ok(segc_ref, segr_ref, i, j)
            for p in range(PAIRS):
                kb = k_ref[pl.ds(koff, 128), 128 * p : 128 * p + 128]
                s = mm(kb, pair_diag(qt_ref, p, qoff), 1, 0)
                if near:
                    s = jnp.where(ok, s + pair_tile(tile_ref, p, dd), NEG)
                else:
                    s = s + far_ref[p : p + 1, :]
                m_old = m_ref[p : p + 1, :]
                m_new = jnp.maximum(m_old, jnp.max(s, axis=0, keepdims=True))
                w = jnp.exp(s - m_new)
                shrink = jnp.exp(m_old - m_new)
                m_ref[p : p + 1, :] = m_new
                l_ref[p : p + 1, :] = l_ref[p : p + 1, :] * shrink + jnp.sum(
                    w, axis=0, keepdims=True
                )
                o = mm(vt_ref[128 * p : 128 * p + 128, pl.ds(koff, 128)], w.astype(BF16), 1, 0)
                o = jnp.concatenate([o[:64, :128], o[64:, 128:]], axis=1)
                acc_ref[p] = acc_ref[p] * shrink + o

        visit(i, True)

        def one_key(j, _):
            code = code_ref[i, j]

            @pl.when(code == 1)
            def _():
                visit(j, False)

            @pl.when(code == 2)
            def _():
                visit(j, True)

            return 0

        lax.fori_loop(0, i, one_key, 0)
        for p in range(PAIRS):
            total = l_ref[p : p + 1, :]
            ctx = acc_ref[p] * (1.0 / total)
            both = jnp.concatenate([ctx[:, :128], ctx[:, 128:]], axis=0)
            ctxt_ref[128 * p : 128 * p + 128, pl.ds(qoff, 128)] = both
            ctxb_ref[pl.ds(qoff, 128), 128 * p : 128 * p + 128] = both.T.astype(BF16)
            lse = m_ref[p : p + 1, :] + jnp.log(total)
            lse_ref[2 * p : 2 * p + 1, pl.ds(qoff, 128)] = lse[:, :128]
            lse_ref[2 * p + 1 : 2 * p + 2, pl.ds(qoff, 128)] = lse[:, 128:]
        return 0

    lax.fori_loop(0, 2, one_query, 0)


def bwd_kernel(
    code_ref, me_ref, qt_ref, dt_ref, k_ref, kt_ref, v_ref, lse_ref, delta_ref,
    gap_ref, far_ref, segc_ref, segr_ref,
    dqkv_ref, dgap_ref, dfar_ref,
    tile_ref, near_ref, facc_ref, dq_ref, dk_ref, dv_ref,
):
    fill_tiles(gap_ref, far_ref, tile_ref)
    near_ref[...] = jnp.zeros_like(near_ref)
    facc_ref[...] = jnp.zeros_like(facc_ref)
    me = me_ref[0]

    def lanes(ref, p, i):
        g = i // 2
        off = pl.multiple_of((i % 2) * 128, 128)
        return jnp.concatenate(
            [ref[g, 2 * p : 2 * p + 1, pl.ds(off, 128)], ref[g, 2 * p + 1 : 2 * p + 2, pl.ds(off, 128)]],
            axis=1,
        )

    def grads(i, j, p, near, dd, ok):
        qoff = pl.multiple_of(i * 128, 128)
        koff = pl.multiple_of(j * 128, 128)
        qd = pair_diag(qt_ref, p, qoff)
        dd_ = pair_diag(dt_ref, p, qoff)
        s = mm(k_ref[pl.ds(koff, 128), 128 * p : 128 * p + 128], qd, 1, 0)
        lse = lanes(lse_ref, p, i)
        if near:
            w = jnp.exp(jnp.where(ok, s + pair_tile(tile_ref, p, dd) - lse, NEG))
        else:
            w = jnp.exp(s + (far_ref[p : p + 1, :] - lse))
        dp = mm(v_ref[pl.ds(koff, 128), 128 * p : 128 * p + 128], dd_, 1, 0)
        ds = w * (dp - lanes(delta_ref, p, i))
        return w, ds, qd, dd_

    def visit_query(i, j, near):
        koff = pl.multiple_of(j * 128, 128)
        dd = jnp.minimum(i - j, 2) if near else None
        ok = seg_ok(segc_ref, segr_ref, i, j) if near else None
        for p in range(PAIRS):
            _, ds, _, _ = grads(i, j, p, near, dd, ok)
            if near:
                off = pl.multiple_of(dd * 128, 128)
                near_ref[2 * p, :, pl.ds(off, 128)] += ds[:, :128]
                near_ref[2 * p + 1, :, pl.ds(off, 128)] += ds[:, 128:]
            else:
                part = ds[0:8]
                for a in range(1, 16):
                    part = part + ds[8 * a : 8 * a + 8]
                facc_ref[p] += part
            o = mm(kt_ref[128 * p : 128 * p + 128, pl.ds(koff, 128)], ds.astype(BF16), 1, 0)
            dq_ref[p] += jnp.concatenate([o[:64, :128], o[64:, 128:]], axis=1)

    def one_query(qi, _):
        i = me * 2 + qi
        qoff = pl.multiple_of(qi * 128, 128)
        dq_ref[...] = jnp.zeros_like(dq_ref)

        def one_key(j, _):
            code = code_ref[i, j]

            @pl.when(code == 1)
            def _():
                visit_query(i, j, False)

            @pl.when(code == 2)
            def _():
                visit_query(i, j, True)

            return 0

        lax.fori_loop(0, i + 1, one_key, 0)
        for p in range(PAIRS):
            x = dq_ref[p] * 0.125
            both = jnp.concatenate([x[:, :128], x[:, 128:]], axis=0)
            dqkv_ref[pl.ds(qoff, 128), 128 * p : 128 * p + 128] = both.T.astype(BF16)
        return 0

    lax.fori_loop(0, 2, one_query, 0)

    def visit_key(i, j, near):
        dd = jnp.minimum(i - j, 2) if near else None
        ok = seg_ok(segc_ref, segr_ref, i, j) if near else None
        for p in range(PAIRS):
            w, ds, qd, dd_ = grads(i, j, p, near, dd, ok)
            dv_ref[p] += mm(w.astype(BF16), dd_, 1, 1)
            dk_ref[p] += mm(ds.astype(BF16), qd, 1, 1)

    def one_own(kj, _):
        j = me * 2 + kj
        koff = pl.multiple_of(kj * 128, 128)
        dk_ref[...] = jnp.zeros_like(dk_ref)
        dv_ref[...] = jnp.zeros_like(dv_ref)

        def one_block(i, _):
            code = code_ref[i, j]

            @pl.when(code == 1)
            def _():
                visit_key(i, j, False)

            @pl.when(code == 2)
            def _():
                visit_key(i, j, True)

            return 0

        lax.fori_loop(j, code_ref.shape[0], one_block, 0)
        for p in range(PAIRS):
            at = D + 128 * p
            dqkv_ref[pl.ds(koff, 128), at : at + 128] = dk_ref[p].astype(BF16)
            dqkv_ref[pl.ds(koff, 128), D + at : D + at + 128] = dv_ref[p].astype(BF16)
        return 0

    lax.fori_loop(0, 2, one_own, 0)

    for h in range(HEADS):
        x = near_ref[h, :, 0:256]
        g = x[0:8]
        for a in range(1, 16):
            g = g + pltpu.roll(x[8 * a : 8 * a + 8], 256 - 8 * a, 1)
        total = g[0:1]
        for b in range(1, 8):
            total = total + pltpu.roll(g, 256 - b, 1)[b : b + 1]
        dgap_ref[h : h + 1, :] = total
        half = 128 * (h % 2)
        far = jnp.sum(facc_ref[h // 2, :, half : half + 128], axis=0, keepdims=True)
        far = far + jnp.sum(near_ref[h, :, 256:384], axis=0, keepdims=True)
        dfar_ref[h : h + 1, :] = far


def vmem():
    return pl.BlockSpec(memory_space=pltpu.VMEM)


def smem():
    return pl.BlockSpec(memory_space=pltpu.SMEM)


def attention_forward(code, me, qt, keys, vt, gap, far, segc, segr):
    length = keys.shape[0]
    return pl.pallas_call(
        fwd_kernel,
        name="attention_forward",
        out_shape=[
            jax.ShapeDtypeStruct((D, ROWS), F32),
            jax.ShapeDtypeStruct((ROWS, D), BF16),
            jax.ShapeDtypeStruct((HEADS, ROWS), F32),
        ],
        in_specs=[smem(), smem()] + [vmem()] * 7,
        out_specs=[vmem()] * 3,
        scratch_shapes=[
            pltpu.VMEM((HEADS, 128, 384), F32),
            pltpu.VMEM((8, 256), F32),
            pltpu.VMEM((8, 256), F32),
            pltpu.VMEM((PAIRS, 64, 256), F32),
        ],
        compiler_params=pltpu.CompilerParams(vmem_limit_bytes=VMEM_LIMIT),
        cost_estimate=pl.CostEstimate(
            flops=8 * ROWS * length * D,
            bytes_accessed=4 * length * D,
            transcendentals=HEADS * ROWS * length // 2,
        ),
    )(code, me, qt, keys, vt, gap, far, segc, segr)


def attention_backward(code, me, qt, dt, keys, kt, values, lse, delta, gap, far, segc, segr):
    length = keys.shape[0]
    return pl.pallas_call(
        bwd_kernel,
        name="attention_backward",
        out_shape=[
            jax.ShapeDtypeStruct((ROWS, 3 * D), BF16),
            jax.ShapeDtypeStruct((HEADS, 256), F32),
            jax.ShapeDtypeStruct((HEADS, 128), F32),
        ],
        in_specs=[smem(), smem()] + [vmem()] * 11,
        out_specs=[vmem()] * 3,
        scratch_shapes=[
            pltpu.VMEM((HEADS, 128, 384), F32),
            pltpu.VMEM((HEADS, 128, 384), F32),
            pltpu.VMEM((PAIRS, 8, 256), F32),
            pltpu.VMEM((PAIRS, 64, 256), F32),
            pltpu.VMEM((PAIRS, 128, 128), F32),
            pltpu.VMEM((PAIRS, 128, 128), F32),
        ],
        compiler_params=pltpu.CompilerParams(vmem_limit_bytes=VMEM_LIMIT),
        cost_estimate=pl.CostEstimate(
            flops=14 * ROWS * length * D,
            bytes_accessed=10 * length * D,
            transcendentals=HEADS * ROWS * length,
        ),
    )(code, me, qt, dt, keys, kt, values, lse, delta, gap, far, segc, segr)


def block_codes(seg_all, blocks):
    count = blocks.shape[0]
    rows = seg_all.reshape(count, BLK)
    least, most = jnp.min(rows, axis=1), jnp.max(rows, axis=1)
    ids = jnp.arange(count, dtype=jnp.int32)
    gap = ids[:, None] - ids[None, :]
    meet = (most[None, :] >= least[:, None]) & (least[None, :] <= most[:, None])
    live = (gap >= 0) & (blocks == 1) & meet
    same = (
        (least == most)[:, None] & (least == most)[None, :] & (least[:, None] == least[None, :])
    )
    return jnp.where(live, jnp.where(same & (gap >= 2), 1, 2), 0).astype(jnp.int32)


def bias_inputs(table):
    gap = jnp.dot(table, gap_hot().T, precision=PRECISE)
    far = jnp.repeat(table[:, 31].reshape(PAIRS, 2), BLK, axis=1)
    return gap, far


def bias_back(dgap, dfar):
    near = jnp.dot(dgap, gap_hot(), precision=PRECISE)
    last = (jnp.arange(32) == 31).astype(F32)[None, :]
    return near + jnp.sum(dfar, axis=1, keepdims=True) * last


def body(
    tokens, segments, block_sets, routes, qkv_weight, out_weight, ffn_in, ffn_out,
    norm_gains, rel_bias, router, expert_in, expert_out, cotangent,
):
    gather = partial(lax.all_gather, axis_name="grp", axis=0, tiled=True)
    rows = tokens.shape[1]
    me = lax.axis_index("grp").astype(jnp.int32).reshape(1)
    seg_all = gather(segments[0])
    code = block_codes(seg_all, block_sets[0])
    segc = seg_all[:, None]
    segr = seg_all.reshape(-1, BLK)
    shared = (segc, segr)

    x_all = gather(tokens[0])
    w_qkv = [gather(qkv_weight[:, 0].reshape(-1, 3 * D)), None]
    w_out = [gather(out_weight[:, 0]), None]
    full_in, full_down = gather(ffn_in), gather(ffn_out)
    w_qkv[1] = gather(qkv_weight[:, 1].reshape(-1, 3 * D))
    w_out[1] = gather(out_weight[:, 1])

    def attend(residual, normed, normed_all, layer):
        w = w_qkv[layer]
        qt = mm(w[:, :D], normed, 0, 1).astype(BF16) * jnp.asarray(0.125, BF16)
        keys = mm(normed_all, w[:, D : 2 * D], 1, 0).astype(BF16)
        vt = mm(w[:, 2 * D :], normed_all, 0, 1).astype(BF16)
        gap, far = bias_inputs(rel_bias[layer])
        ctxt, ctxb, lse = attention_forward(code, me, qt, keys, vt, gap, far, *shared)
        branch = mm(ctxb, w_out[layer], 1, 0)
        lse_all = lax.all_gather(lse, "grp", axis=0)
        return residual + branch, (residual, normed, normed_all, keys, ctxt, ctxb, lse_all, gap, far)

    def attend_back(grad_out, saved, layer):
        residual, normed, normed_all, keys, ctxt, ctxb, lse_all, gap, far = saved
        w, wo = w_qkv[layer], w_out[layer]
        grad_low = grad_out.astype(BF16)
        grad_all = gather(grad_low)
        dctx_own = mm(wo, grad_low, 1, 1).astype(BF16)
        delta = jnp.sum((dctx_own.astype(F32) * ctxt).reshape(HEADS, HEAD, rows), axis=1)
        delta_all = lax.all_gather(delta, "grp", axis=0)
        qt_all = mm(w[:, :D], normed_all, 0, 1).astype(BF16) * jnp.asarray(0.125, BF16)
        kt = mm(w[:, D : 2 * D], normed_all, 0, 1).astype(BF16)
        values = mm(normed_all, w[:, 2 * D :], 1, 0).astype(BF16)
        dt_all = mm(wo, grad_all, 1, 1).astype(BF16)
        dqkv, dgap, dfar = attention_backward(
            code, me, qt_all, dt_all, keys, kt, values, lse_all, delta_all, gap, far, *shared
        )
        out_part = mm(ctxb, grad_low, 0, 0)
        qkv_part = mm(normed, dqkv, 0, 0)
        normed_grad = mm(dqkv, w, 1, 1)
        _, pull_back = jax.vjp(norm_rows, residual, norm_gains[layer, 0])
        residual_grad, gain_grad = pull_back(normed_grad)
        return grad_out + residual_grad, qkv_part, out_part, gain_grad, bias_back(dgap, dfar)

    stream = tokens[0].astype(F32)
    own_a = norm_rows(stream, norm_gains[0, 0]).astype(BF16)
    all_a = norm_rows(x_all.astype(F32), norm_gains[0, 0]).astype(BF16)
    first_out, saved_a = attend(stream, own_a, all_a, 0)
    normed_ffn = norm_rows(first_out, norm_gains[0, 1]).astype(BF16)
    pre_ffn = mm(normed_ffn, full_in, 1, 0)
    hidden_ffn = jax.nn.gelu(pre_ffn).astype(BF16)
    after_ffn = first_out + mm(hidden_ffn, full_down, 1, 1)

    own_b = norm_rows(after_ffn, norm_gains[1, 0]).astype(BF16)
    second_out, saved_b = attend(after_ffn, own_b, gather(own_b), 1)
    normed_moe = norm_rows(second_out, norm_gains[1, 1]).astype(BF16)
    normed_wide = normed_moe.astype(F32)
    router_wide = router.astype(F32)
    logits = jnp.dot(normed_wide, router_wide, precision=PRECISE)

    experts_all = router.shape[1]
    groups = lax.axis_size("grp")
    per_group = experts_all // groups
    capacity = rows * 2 * 10 // (7 * experts_all) + 1
    slots = (capacity + 16) // 16 * 16
    chosen = routes[0]
    ids = jnp.arange(experts_all, dtype=jnp.int32)
    chosen_hot = (chosen[:, :, None] == ids[None, None, :]).astype(F32)
    flat_hot = chosen_hot.reshape(2 * rows, experts_all)
    before = jnp.tril(jnp.ones((2 * rows, 2 * rows), BF16), -1)
    earlier = mm(before, flat_hot.astype(BF16), 1, 0)
    slot_ids = jnp.sum(earlier * flat_hot, axis=1).astype(jnp.int32)
    place = (chosen.reshape(-1) * slots + slot_ids).reshape(rows, 2)
    lanes = jnp.arange(experts_all * slots, dtype=jnp.int32)
    pick = [(place[:, k][:, None] == lanes[None, :]).astype(BF16) for k in range(2)]
    both = pick[0] + pick[1]

    def exchange(x):
        return lax.all_to_all(
            x.reshape(groups, per_group * slots, D), "grp", split_axis=0, concat_axis=0, tiled=True
        )

    grad_final = cotangent[0].astype(F32)
    selected = jnp.sum(logits[:, None, :] * chosen_hot, axis=-1)
    gate_probs = jax.nn.softmax(selected, axis=-1)
    received = exchange(mm(both, normed_moe, 0, 0).astype(BF16))
    made = [(gate_probs[:, k : k + 1] * grad_final).astype(BF16) for k in range(2)]
    send_grad = (mm(pick[0], made[0], 0, 0) + mm(pick[1], made[1], 0, 0)).astype(BF16)
    recv_grad = exchange(send_grad)

    def by_expert(x):
        return x.reshape(groups, per_group, slots, -1).swapaxes(0, 1).reshape(per_group, groups * slots, -1)

    def by_source(x):
        return x.reshape(per_group, groups, slots, -1).swapaxes(0, 1).reshape(groups, per_group * slots, -1)

    def each(a, b, ca, cb):
        return lax.dot_general(a, b, (((ca,), (cb,)), ((0,), (0,))), preferred_element_type=F32)

    rows_e, dye = by_expert(received), by_expert(recv_grad)
    pre_expert = each(rows_e, expert_in, 2, 1)
    hidden_expert, gelu_expert = jax.vjp(jax.nn.gelu, pre_expert)
    hidden_expert = hidden_expert.astype(BF16)
    made_rows = each(hidden_expert, expert_out, 2, 1).astype(BF16)
    returned = exchange(by_source(made_rows)).reshape(experts_all * slots, D)
    hidden_grad = each(dye, expert_out, 2, 2)
    pre_grad = gelu_expert(hidden_grad)[0].astype(BF16)
    rows_grad = each(pre_grad, expert_in, 2, 2).astype(BF16)
    back_grad = exchange(by_source(rows_grad)).reshape(experts_all * slots, D)
    picked = [mm(pick[k], returned, 1, 0) for k in range(2)]
    final_out = second_out + gate_probs[:, 0:1] * picked[0] + gate_probs[:, 1:2] * picked[1]
    gate_grad = jnp.stack([jnp.sum(grad_final * picked[k], axis=-1) for k in range(2)], axis=-1)
    select_grad = gate_probs * (gate_grad - jnp.sum(gate_probs * gate_grad, axis=-1, keepdims=True))
    logit_grad = jnp.sum(select_grad[:, :, None] * chosen_hot, axis=1)
    router_part = jnp.dot(normed_wide.T, logit_grad, precision=PRECISE)
    normed_moe_grad = jnp.dot(logit_grad, router_wide.T, precision=PRECISE) + mm(both, back_grad, 1, 0)
    _, pull_moe = jax.vjp(norm_rows, second_out, norm_gains[1, 1])
    moe_resid_grad, moe_gain_grad = pull_moe(normed_moe_grad)
    grad_second = grad_final + moe_resid_grad

    expert_out_part = each(hidden_expert, dye, 1, 1)
    expert_in_part = each(rows_e, pre_grad, 1, 1)

    grad_ffn, qkv_part_b, out_part_b, gain_grad_b, table_grad_b = attend_back(grad_second, saved_b, 1)
    down_low = grad_ffn.astype(BF16)
    down_part = mm(down_low, hidden_ffn, 0, 0)
    hidden_ffn_grad = mm(down_low, full_down, 1, 0)
    _, gelu_dense = jax.vjp(jax.nn.gelu, pre_ffn)
    pre_ffn_grad = gelu_dense(hidden_ffn_grad)[0].astype(BF16)
    in_part = mm(normed_ffn, pre_ffn_grad, 0, 0)
    normed_ffn_grad = mm(pre_ffn_grad, full_in, 1, 1)
    _, pull_ffn = jax.vjp(norm_rows, first_out, norm_gains[0, 1])
    ffn_resid_grad, ffn_gain_grad = pull_ffn(normed_ffn_grad)
    grad_first = grad_ffn + ffn_resid_grad
    grad_tokens, qkv_part_a, out_part_a, gain_grad_a, table_grad_a = attend_back(grad_first, saved_a, 0)

    def scatter(x):
        return lax.psum_scatter(x.astype(BF16), "grp", scatter_dimension=0, tiled=True)

    def total(x):
        return lax.psum(x.astype(BF16), "rep").astype(F32)

    qkv_sum = jnp.stack([total(scatter(x)) for x in (qkv_part_a, qkv_part_b)], axis=1)
    qkv_sum = qkv_sum.reshape(qkv_weight.shape)
    out_sum = jnp.stack([total(scatter(x)) for x in (out_part_a, out_part_b)], axis=1)
    in_sum, down_sum = total(scatter(in_part)), total(scatter(down_part))
    expert_in_sum, expert_out_sum = total(expert_in_part), total(expert_out_part)
    gain_all = jnp.stack(
        [jnp.stack([gain_grad_a, ffn_gain_grad]), jnp.stack([gain_grad_b, moe_gain_grad])]
    )
    table_all = jnp.stack([table_grad_a, table_grad_b])
    gain_sum, table_sum, router_sum = lax.psum((gain_all, table_all, router_part), ("rep", "grp"))
    return (
        final_out[None], grad_tokens[None], qkv_sum, out_sum, in_sum, down_sum,
        gain_sum, table_sum, router_sum, expert_in_sum, expert_out_sum,
    )


def solution(mesh):
    return jax.shard_map(
        body,
        mesh=mesh,
        in_specs=(
            P("rep", "grp", None),
            P("rep", "grp"),
            P("rep", None, None),
            P("rep", "grp", None),
            P("grp", None, None, None),
            P("grp", None, None),
            P("grp", None),
            P("grp", None),
            P(),
            P(),
            P(),
            P("grp", None, None),
            P("grp", None, None),
            P("rep", "grp", None),
        ),
        out_specs=(
            P("rep", "grp", None),
            P("rep", "grp", None),
            P("grp", None, None, None),
            P("grp", None, None),
            P("grp", None),
            P("grp", None),
            P(),
            P(),
            P(),
            P("grp", None, None),
            P("grp", None, None),
        ),
        check_vma=False,
    )
```

time: 2250 us -> 1220 us (0.54)
  local copies, waits for them, and re-layouts: 636 us -> 49.7 us
  matrix products: 663 us -> 170 us
  other arithmetic: 133 us -> 33.7 us
  Pallas kernels: 0 us -> 93.6 us
  waiting for transfers between devices: 560 us -> 653 us
  loops' own time: 38.5 us -> 0 us
  blocking collectives: 156 us -> 188 us
    dot_general x192 -> x43, matrix products: 661 us -> 166 us  [the longest x33 118 us: mm(): lax.dot_general(a, b, (((ca,), (cb,)), ((), ())), preferred_element_type=...]
    dynamic_slice x128 -> x0, local copies, waits for them, and re-layouts: 170 us -> none  [the longest x32 71.7 us: one_step(): lax.dynamic_slice_in_dim(piece_values, row_off, step_rows, 0)]
    cond x60 -> x0, local copies, waits for them, and re-layouts: 120 us -> none  [the longest x36 118 us: block_scores(): lax.cond(is_far(pos_gap), far_bias, near_bias, bias_table, pos_gap)]
    scatter x2 -> x0, local copies, waits for them, and re-layouts: 95.4 us -> none  [the longest x1 47.7 us: body(): jnp.zeros((experts_all, capacity, D), jnp.bfloat16).at[flat_ids, slot_ids]]
    pallas_call x0 -> x4, Pallas kernels: none -> 93.6 us  [the longest x2 80.1 us: attention_backward(): pl.pallas_call(bwd_kernel, name='attention_backward', out_shape=[jax.Shap...]
    gather x98 -> x0, local copies, waits for them, and re-layouts: 93.3 us -> none  [the longest x48 46.9 us: block_scores(): block_hit = jnp.take(block_rows, key_pos // BLK, axis=1)]
    all_to_all x0 -> x2, blocking collectives: none -> 72.4 us  [exchange(): lax.all_to_all(x.reshape(groups, per_group * slots, D), 'grp', split_axis...]
    reduce_scatter x4 -> x6, waiting for transfers between devices: 140 us -> 194 us  [scatter(): lax.psum_scatter(x.astype(BF16), 'grp', scatter_dimension=0, tiled=True)]
  transfers between devices with their start and end apart: 21 -> 19, of which waited for: 10 -> 15; matrix products, arithmetic and copies ran while one was open for 51% -> 13% of each run, Pallas kernels for 0% -> 4%
where the time goes in v1:
time: 1220 us; the launch traced here: 1210 us
  waiting for transfers between devices  653 us (54%)
  blocking collectives  188 us (15%)
  matrix products  170 us (14%)
  Pallas kernels  93.6 us (8%)
  local copies, waits for them, and re-layouts  49.7 us (4%)
  other arithmetic  33.7 us (3%)
  between operations  15.7 us (1%)
    reduce_scatter x6, waiting for transfers between devices, scatter(): lax.psum_scatter(x.astype(BF16), 'grp', scatter_dimension=0, tiled=True)  194 us
    psum x1, waiting for transfers between devices, total(): return lax.psum(x.astype(BF16), 'rep').astype(F32)  194 us
    dot_general x33, matrix products, mm(): lax.dot_general(a, b, (((ca,), (cb,)), ((), ())), preferred_element_type=...  118 us
    all_gather x2, waiting for transfers between devices, body(): full_in, full_down = (gather(ffn_in), gather(ffn_out))  89 us
    pallas_call x2, Pallas kernels, attention_backward(): pl.pallas_call(bwd_kernel, name='attention_backward', out_shape=[jax.Shap...  80.1 us
    all_to_all x2, blocking collectives, exchange(): lax.all_to_all(x.reshape(groups, per_group * slots, D), 'grp', split_axis...  72.4 us
    all_to_all x2, waiting for transfers between devices, exchange(): lax.all_to_all(x.reshape(groups, per_group * slots, D), 'grp', split_axis...  50.2 us
    dot_general x6, matrix products, each(): lax.dot_general(a, b, (((ca,), (cb,)), ((0,), (0,))), preferred_element_t...  45.3 us
  transfers between devices with their start and end apart: 19, of which 15 were waited for; matrix products, arithmetic and copies ran while one was open for 13% of the time, Pallas kernels for 4%

profile of v1, /device:TPU:0, one launch (start us, length us, event | category | flops | bytes accessed | tf_op | source)
XLA Modules:
  0.0 1213.0 jit_solution(1363490089550581971)
XLA Ops:
  18.9 13.6 %all-gather = s32[1,2048]{1,0:T(1,128)S(1)} all-gather(s32[1,256]{1,0:T(1,128)S(1)} %copy-done.92), channel_id=2, replica_groups=mesh['rep'=4,'grp'=8] {'grp'}, dimensions={1}, use_global_device_ids=true | all-gather | bytes 9216 | tf_op jit(solution)/shard_map/all_gather | solution.py:383
  35.9 14.8 %all-gather.37.cloned.1.call-done = bf16[1,2048,768]{2,1,0:T(8,128)(2,1)} async-done(((bf16[1,256,768]{2,1,0:T(8,128)(2,1)}), bf16[1,2048,768]{2,1,0:T(8,128)(2,1)}) %all-gather.37.cloned.1.call-update) | async-done | bytes 3145744 | tf_op jit(solution)/shard_map/all_gather | solution.py:389
  53.4 40.0 %all-gather.23.cloned.1.call-done = bf16[768,2304]{1,0:T(8,128)(2,1)} async-done(((bf16[96,2304]{1,0:T(8,128)(2,1)}), bf16[768,2304]{1,0:T(8,128)(2,1)}) %all-gather.23.cloned.1.call-update) | async-done | bytes 3538960 | tf_op jit(solution)/shard_map/all_gather | solution.py:390
  127.8 42.4 %all-gather.25.cloned.1.call-done = bf16[768,3072]{1,0:T(8,128)(2,1)} async-done(((bf16[96,3072]{1,0:T(8,128)(2,1)}), bf16[768,3072]{1,0:T(8,128)(2,1)}) %all-gather.25.cloned.1.call-update) | async-done | bytes 4718608 | tf_op jit(solution)/shard_map/all_gather | solution.py:392
  175.6 46.6 %all-gather.27.cloned.1.call-done = bf16[768,3072]{1,0:T(8,128)(2,1)} async-done(((bf16[96,3072]{1,0:T(8,128)(2,1)}), bf16[768,3072]{1,0:T(8,128)(2,1)}) %all-gather.27.cloned.1.call-update) | async-done | bytes 4718608 | tf_op jit(solution)/shard_map/all_gather | solution.py:392
  232.7 32.0 %all-gather.29.cloned.1.call-done = bf16[768,2304]{1,0:T(8,128)(2,1)} async-done(((bf16[96,2304]{1,0:T(8,128)(2,1)}), bf16[768,2304]{1,0:T(8,128)(2,1)}) %all-gather.29.cloned.1.call-update) | async-done | bytes 3538960 | tf_op jit(solution)/shard_map/all_gather | solution.py:393
  267.4 36.6 %all-gather.31.cloned.1.call-done = bf16[2048,768]{1,0:T(8,128)(2,1)} async-done(((bf16[256,768]{1,0:T(8,128)(2,1)}), bf16[2048,768]{1,0:T(8,128)(2,1)}) %all-gather.31.cloned.1.call-update) | async-done | bytes 3145744 | tf_op jit(solution)/shard_map/all_gather | solution.py:439
  337.7 40.3 %all_to_all.20 = bf16[8,96,768]{2,1,0:T(8,128)(2,1)S(1)} all-to-all(bf16[8,96,768]{2,1,0:T(8,128)(2,1)S(1)} %bitcast.231), channel_id=1, replica_groups=mesh['rep'=4,'grp'=8] {'grp'}, dimensions={0} | all-to-all | bytes 2359296 | tf_op jit(solution)/shard_map/all_to_all | solution.py:463
  401.5 22.9 %all-to-all-done.1 = bf16[8,96,768]{2,1,0:T(8,128)(2,1)S(1)} async-done(((bf16[8,96,768]{2,1,0:T(8,128)(2,1)}), bf16[8,96,768]{2,1,0:T(8,128)(2,1)S(1)}, u32[]{:S(2)}, u32[]{:S(2)}) %all-to-all-start.1) | async-done | bytes 1179680 | tf_op jit(solution)/shard_map/all_to_all | solution.py:463
  430.2 32.2 %all_to_all.21 = bf16[8,96,768]{2,1,0:T(8,128)(2,1)S(1)} all-to-all(bf16[8,96,768]{2,1,0:T(8,128)(2,1)S(1)} %bitcast.212), channel_id=1, replica_groups=mesh['rep'=4,'grp'=8] {'grp'}, dimensions={0} | all-to-all | bytes 2359296 | tf_op jit(solution)/shard_map/all_to_all | solution.py:463
  483.7 27.4 %all-to-all-done.3 = bf16[8,96,768]{2,1,0:T(8,128)(2,1)S(1)} async-done(((bf16[8,96,768]{2,1,0:T(8,128)(2,1)}), bf16[8,96,768]{2,1,0:T(8,128)(2,1)S(1)}, u32[]{:S(2)}, u32[]{:S(2)}) %all-to-all-start.3) | async-done | bytes 1179680 | tf_op jit(solution)/shard_map/all_to_all | solution.py:463
  516.4 15.2 %all-gather.8.lse_ref = f32[8,12,256]{2,1,0:T(8,128)} all-gather(f32[1,12,256]{2,1,0:T(8,128)S(1)} %bitcast.243), channel_id=6, replica_groups=mesh['rep'=4,'grp'=8] {'grp'}, dimensions={0}, use_global_device_ids=true | all-gather | bytes 110592 | tf_op jit(solution)/shard_map/all_gather | solution.py:404
  539.6 16.2 %all-gather.9.delta_ref = f32[8,12,256]{2,1,0:T(8,128)} all-gather(f32[1,12,256]{2,1,0:T(8,128)} %bitcast.240), channel_id=7, replica_groups=mesh['rep'=4,'grp'=8] {'grp'}, dimensions={0}, use_global_device_ids=true | all-gather | bytes 110592 | tf_op jit(solution)/shard_map/all_gather | solution.py:414
  563.0 40.0 %attention_backward.2 = (bf16[256,2304]{1,0:T(8,128)(2,1)}, f32[12,256]{1,0:T(8,128)}, f32[12,128]{1,0:T(8,128)}) custom-call(s32[16,16]{1,0:T(8,128)} %select_select_fusion.code_ref, s32[1]{0:T(128)} %bitcast.3.me_ref, bf16[768,2048]{1,0:T(8,128)(2,1)} %multiply_bitcast_fusion.1.qt_ref, bf16[768,2048]{1,0:T(8,128)(2,1)} %fusion.27.dt_ref, ...), custom_call_target="tpu_custom_call" | custom-call | flops 5637144576 | bytes 15728640 | tf_op jit(solution)/shard_map/attention_backward/pallas_call | solution.py:323
  623.1 15.2 %all-gather.10.lse_ref = f32[8,12,256]{2,1,0:T(8,128)} all-gather(f32[1,12,256]{2,1,0:T(8,128)S(1)} %bitcast.242), channel_id=8, replica_groups=mesh['rep'=4,'grp'=8] {'grp'}, dimensions={0}, use_global_device_ids=true | all-gather | bytes 110592 | tf_op jit(solution)/shard_map/all_gather | solution.py:404
  647.9 15.5 %all-gather.11.delta_ref = f32[8,12,256]{2,1,0:T(8,128)} all-gather(f32[1,12,256]{2,1,0:T(8,128)S(1)} %bitcast.241), channel_id=9, replica_groups=mesh['rep'=4,'grp'=8] {'grp'}, dimensions={0}, use_global_device_ids=true | all-gather | bytes 110592 | tf_op jit(solution)/shard_map/all_gather | solution.py:414
  669.3 40.1 %attention_backward.3 = (bf16[256,2304]{1,0:T(8,128)(2,1)}, f32[12,256]{1,0:T(8,128)}, f32[12,128]{1,0:T(8,128)}) custom-call(s32[16,16]{1,0:T(8,128)} %select_select_fusion.code_ref, s32[1]{0:T(128)} %bitcast.3.me_ref, bf16[768,2048]{1,0:T(8,128)(2,1)} %multiply_bitcast_fusion.qt_ref, bf16[768,2048]{1,0:T(8,128)(2,1)} %fusion.28.dt_ref, ...), custom_call_target="tpu_custom_call" | custom-call | flops 5637144576 | bytes 15728640 | tf_op jit(solution)/shard_map/attention_backward/pallas_call | solution.py:323
  749.4 17.5 %reduce-scatter.7.cloned.1.call-done = bf16[96,2304]{1,0:T(8,128)(2,1)} async-done(((bf16[768,2304]{1,0:T(8,128)(2,1)}), bf16[96,2304]{1,0:T(8,128)(2,1)}) %reduce-scatter.7.cloned.1.call-update) | async-done | bytes 442384 | tf_op jit(solution)/shard_map/reduce_scatter | solution.py:522
  769.2 31.8 %reduce-scatter.13.cloned.1.call-done = bf16[96,768]{1,0:T(8,128)(2,1)} async-done(((bf16[768,768]{1,0:T(8,128)(2,1)}), bf16[96,768]{1,0:T(8,128)(2,1)}) %reduce-scatter.13.cloned.1.call-update) | async-done | bytes 147472 | tf_op jit(solution)/shard_map/reduce_scatter | solution.py:522
  801.0 33.3 %reduce-scatter.11.cloned.1.call-done = bf16[96,768]{1,0:T(8,128)(2,1)} async-done(((bf16[768,768]{1,0:T(8,128)(2,1)}), bf16[96,768]{1,0:T(8,128)(2,1)}) %reduce-scatter.11.cloned.1.call-update) | async-done | bytes 147472 | tf_op jit(solution)/shard_map/reduce_scatter | solution.py:522
  834.3 55.3 %reduce-scatter.17.cloned.1.call-done = bf16[96,3072]{1,0:T(8,128)(2,1)} async-done(((bf16[768,3072]{1,0:T(8,128)(2,1)}), bf16[96,3072]{1,0:T(8,128)(2,1)}) %reduce-scatter.17.cloned.1.call-update) | async-done | bytes 589840 | tf_op jit(solution)/shard_map/reduce_scatter | solution.py:522
  889.5 56.1 %reduce-scatter.15.cloned.1.call-done = bf16[96,3072]{1,0:T(8,128)(2,1)} async-done(((bf16[768,3072]{1,0:T(8,128)(2,1)}), bf16[96,3072]{1,0:T(8,128)(2,1)}) %reduce-scatter.15.cloned.1.call-update) | async-done | bytes 589840 | tf_op jit(solution)/shard_map/reduce_scatter | solution.py:522
  951.8 40.0 %all-reduce = (f32[2,2,768]{2,1,0:T(2,128)}, f32[2,12,32]{2,1,0:T(8,128)S(1)}, f32[768,8]{0,1:T(8,128)}) all-reduce(f32[2,2,768]{2,1,0:T(2,128)S(1)} %pad_maximum_fusion.1, f32[2,12,32]{2,1,0:T(8,128)S(1)} %pad_maximum_fusion, f32[768,8]{0,1:T(8,128)S(1)} %fusion.159), channel_id=1, replica_groups=mesh['rep'=4,'grp'=8] {'rep','grp'}, use_global_device_ids=true, to_apply=%region_37.38 | all-reduce | flops 9984 | bytes 79872 | tf_op jit(solution)/shard_map/psum | solution.py:536
  993.6 193.6 %all-reduce.4.cloned.1.call-done = (bf16[96,1,3,768]{3,2,0,1:T(4,128)(2,1)}, bf16[96,1,3,768]{3,2,0,1:T(4,128)(2,1)}, bf16[96,1,768]{2,0,1:T(8,128)(2,1)}, bf16[...) async-done(((bf16[96,1,3,768]{3,2,0,1:T(4,128)(2,1)}, ...) | async-done | bytes 11796496 | tf_op jit(solution)/shard_map/psum | solution.py:525
  (396 shorter events, 278.7 us)
Async XLA Ops:
  7.2 389.4 %copy-start = (bf16[768,8]{0,1:T(8,128)(2,1)S(1)}, bf16[768,8]{0,1:T(8,128)(2,1)}, u32[]{:S(2)}) copy-start(bf16[768,8]{0,1:T(8,128)(2,1)} %param.24) | copy-start | bytes 36868
  7.2 43.6 %all-gather.37.cloned.1.call-start = ((), (), s32[]{:S(2)}) async-start(), calls=%async_computation.23 | async-start | bytes 3538944 | tf_op jit(solution)/shard_map/all_gather | solution.py:389
  7.9 85.5 %all-gather.23.cloned.1.call-start = ((), (), s32[]{:S(2)}) async-start(), calls=%async_computation.10 | async-start | bytes 3981312 | tf_op jit(solution)/shard_map/all_gather | solution.py:390
  14.7 111.0 %all-gather.39.cloned.1.call-start = ((), (), s32[]{:S(2)}) async-start(), calls=%async_computation.24 | async-start | bytes 1327104 | tf_op jit(solution)/shard_map/all_gather | solution.py:391
  15.9 154.3 %all-gather.25.cloned.1.call-start = ((), (), s32[]{:S(2)}) async-start(), calls=%async_computation.11 | async-start | bytes 5308416 | tf_op jit(solution)/shard_map/all_gather | solution.py:392
  16.4 205.8 %all-gather.27.cloned.1.call-start = ((), (), s32[]{:S(2)}) async-start(), calls=%async_computation.12 | async-start | bytes 5308416 | tf_op jit(solution)/shard_map/all_gather | solution.py:392
  17.0 247.7 %all-gather.29.cloned.1.call-start = ((), (), s32[]{:S(2)}) async-start(), calls=%async_computation.13 | async-start | bytes 3981312 | tf_op jit(solution)/shard_map/all_gather | solution.py:393
  17.9 286.2 %all-gather.31.cloned.1.call-start = ((), (), s32[]{:S(2)}) async-start(), calls=%async_computation.14 | async-start | bytes 3538944 | tf_op jit(solution)/shard_map/all_gather | solution.py:439
  34.1 197.7 %copy-start.93 = (s32[256]{0:T(256)}, s32[256]{0:T(256)S(1)}, u32[]{:S(2)}) copy-start(s32[256]{0:T(256)S(1)} %fusion.139) | copy-start | bytes 3076
  34.2 193.5 %copy-start.43 = (f32[768]{0:T(1024)}, f32[768]{0:T(1024)S(1)}, u32[]{:S(2)}) copy-start(f32[768]{0:T(1024)S(1)} %get-tuple-element.107) | copy-start | bytes 9220
  34.2 301.0 %copy-start.38 = (f32[768]{0:T(1024)}, f32[768]{0:T(1024)S(1)}, u32[]{:S(2)}) copy-start(f32[768]{0:T(1024)S(1)} %get-tuple-element.104) | copy-start | bytes 9220
  227.6 105.5 %copy-start.6 = (f32[256,768]{1,0:T(8,128)}, f32[256,768]{1,0:T(8,128)S(1)}, u32[]{:S(2)}) copy-start(f32[256,768]{1,0:T(8,128)S(1)} %get-tuple-element.136) | copy-start | bytes 2359300
  228.7 104.5 %all-gather.41.cloned.1.call-start = ((), (), s32[]{:S(2)}) async-start(), calls=%async_computation.25 | async-start | bytes 1327104 | tf_op jit(solution)/shard_map/all_gather | solution.py:394
  391.4 33.0 %all-to-all-start.1 = ((bf16[8,96,768]{2,1,0:T(8,128)(2,1)}), bf16[8,96,768]{2,1,0:T(8,128)(2,1)S(1)}, u32[]{:S(2)}, u32[]{:S(2)}) async-start(bf16[8,96,768]{2,1,0:T(8,128)(2,1)} %bitcast.230), calls=%async_computation.1 | async-start | bytes 2359296 | tf_op jit(solution)/shard_map/all_to_all | solution.py:463
  478.2 32.9 %all-to-all-start.3 = ((bf16[8,96,768]{2,1,0:T(8,128)(2,1)}), bf16[8,96,768]{2,1,0:T(8,128)(2,1)S(1)}, u32[]{:S(2)}, u32[]{:S(2)}) async-start(bf16[8,96,768]{2,1,0:T(8,128)(2,1)} %bitcast.229), calls=%async_computation.3 | async-start | bytes 2359296 | tf_op jit(solution)/shard_map/all_to_all | solution.py:463
  481.7 74.8 %all-gather.33.cloned.1.call-start = ((), (), s32[]{:S(2)}) async-start(), calls=%async_computation.15 | async-start | bytes 3538944 | tf_op jit(solution)/shard_map/all_gather | solution.py:411
  516.3 147.1 %all-gather.35.cloned.1.call-start = ((), (), s32[]{:S(2)}) async-start(), calls=%async_computation.16 | async-start | bytes 3538944 | tf_op jit(solution)/shard_map/all_gather | solution.py:411
  618.9 128.2 %reduce-scatter.9.cloned.1.call-start = ((), (), s32[]{:S(2)}) async-start(), calls=%async_computation.18 | async-start | bytes 3981312 | tf_op jit(solution)/shard_map/reduce_scatter | solution.py:522
  622.4 144.5 %reduce-scatter.7.cloned.1.call-start = ((), (), s32[]{:S(2)}) async-start(), calls=%async_computation.17 | async-start | bytes 3981312 | tf_op jit(solution)/shard_map/reduce_scatter | solution.py:522
  713.8 87.2 %reduce-scatter.13.cloned.1.call-start = ((), (), s32[]{:S(2)}) async-start(), calls=%async_computation.20 | async-start | bytes 1327104 | tf_op jit(solution)/shard_map/reduce_scatter | solution.py:522
  716.3 118.0 %reduce-scatter.11.cloned.1.call-start = ((), (), s32[]{:S(2)}) async-start(), calls=%async_computation.19 | async-start | bytes 1327104 | tf_op jit(solution)/shard_map/reduce_scatter | solution.py:522
  717.9 171.6 %reduce-scatter.17.cloned.1.call-start = ((), (), s32[]{:S(2)}) async-start(), calls=%async_computation.22 | async-start | bytes 5308416 | tf_op jit(solution)/shard_map/reduce_scatter | solution.py:522
  723.5 222.0 %reduce-scatter.15.cloned.1.call-start = ((), (), s32[]{:S(2)}) async-start(), calls=%async_computation.21 | async-start | bytes 5308416 | tf_op jit(solution)/shard_map/reduce_scatter | solution.py:522
  728.6 458.5 %all-reduce.4.cloned.1.call-start = ((), (), s32[]{:S(2)}) async-start(), calls=%async_computation.26 | async-start | bytes 24182784 | tf_op jit(solution)/shard_map/psum | solution.py:525
  (105 other events, 1763.4 us)
Sparse Core Ops, SparseCore 0:
  9.7 41.0 all-gather.36
  53.0 40.3 all-gather.22
  95.6 21.5 all-gather.38
  118.7 51.4 all-gather.24
  171.7 50.5 all-gather.26
  224.3 40.3 all-gather.28
  266.9 37.1 all-gather.30
  305.7 21.5 all-gather.40
  516.5 39.9 all-gather.32
  619.1 43.4 all-gather.34
  664.9 42.8 reduce-scatter.8
  713.9 53.0 reduce-scatter.6
  769.8 31.1 reduce-scatter.12
  803.1 31.0 reduce-scatter.10
  836.4 53.0 reduce-scatter.16
  892.2 53.2 reduce-scatter.14
  950.6 236.4 all-reduce.3

commit v2 on v1

v2 whole, which is shorter than its diff:
```python
from functools import partial

import jax
import jax.numpy as jnp
from jax import lax
from jax.experimental import pallas as pl
from jax.experimental.pallas import tpu as pltpu
from jax.sharding import PartitionSpec as P

D = 768
HEADS = 12
HEAD = 64
PAIRS = 6
BLK = 128
ROWS = 256

BUCKET_EDGES = (18, 20, 23, 26, 30, 34, 39, 45, 51, 58, 66, 76, 86, 98, 112)
PRECISE = lax.Precision.HIGHEST
norm_eps = 1e-06
GELU_SCALE = 0.7978845608028654
GELU_CUBE = 0.044715
NEG = -1e30
VMEM_LIMIT = 60 * 1024 * 1024
F32 = jnp.float32
BF16 = jnp.bfloat16


def mm(a, b, ca, cb):
    return lax.dot_general(a, b, (((ca,), (cb,)), ((), ())), preferred_element_type=F32)


def norm_rows(residual, gain_vec):
    return (
        residual
        * lax.rsqrt(jnp.mean(residual * residual, axis=-1, keepdims=True) + norm_eps)
        * gain_vec
    )


def bucket_of(pos_gap):
    clipped = jnp.maximum(pos_gap, 0)
    bucket = jnp.minimum(clipped, 16)
    for edge_at in BUCKET_EDGES:
        bucket = bucket + (clipped >= edge_at).astype(jnp.int32)
    return bucket


def gap_hot():
    gaps = jnp.arange(2 * BLK, dtype=jnp.int32)
    return (bucket_of(gaps)[:, None] == jnp.arange(32, dtype=jnp.int32)[None, :]).astype(F32)


def pair_diag(ref, p, off):
    x = ref[128 * p : 128 * p + 128, pl.ds(off, 128)]
    z = jnp.zeros((64, 128), x.dtype)
    top = jnp.concatenate([x[:64], z], axis=0)
    low = jnp.concatenate([z, x[64:]], axis=0)
    return jnp.concatenate([top, low], axis=1)


def fill_tiles(gap_ref, far_ref, tile_ref):
    rows = lax.broadcasted_iota(jnp.int32, (128, 128), 0)
    cols = lax.broadcasted_iota(jnp.int32, (128, 128), 1)
    causal = cols >= rows
    for h in range(HEADS):
        x = jnp.broadcast_to(gap_ref[h : h + 1, :], (128, 256))
        r = pltpu.roll(x, 0, 1, stride=1, stride_axis=0)
        tile_ref[h, :, 0:128] = jnp.where(causal, r[:, :128], NEG)
        tile_ref[h, :, 128:256] = r[:, 128:]
        half = 128 * (h % 2)
        tile_ref[h, :, 256:384] = jnp.broadcast_to(
            far_ref[h // 2 : h // 2 + 1, half : half + 128], (128, 128)
        )
    tile_ref[:, :, 384:512] = jnp.full((HEADS, 128, 128), NEG, F32)


def tile_ids(code_ref, i, j):
    pick = [jnp.where(code_ref[i, j + n] == 0, 3, jnp.clip(i - j - n, 0, 2)) for n in range(2)]
    return [pl.multiple_of(t * 128, 128) for t in pick]


def pair_tiles(tile_ref, p, offs):
    cols = [
        jnp.concatenate([tile_ref[2 * p + h, :, pl.ds(off, 128)] for off in offs], axis=0)
        for h in range(2)
    ]
    return jnp.concatenate(cols, axis=1)


def seg_ok(segc_ref, segr_ref, i, j, count):
    kcol = segc_ref[pl.ds(pl.multiple_of(j * 128, 128), count), :]
    ok = kcol == segr_ref[pl.ds(i, 1), :]
    return jnp.concatenate([ok, ok], axis=1)


def split_visit(code_ref, i, j, visit):
    one, two = code_ref[i, j], code_ref[i, j + 1]
    near = (one == 2) | (two == 2)

    @pl.when(near)
    def _():
        visit(j, 2, True)

    @pl.when(jnp.logical_not(near) & (one + two == 2))
    def _():
        visit(j, 2, False)

    @pl.when(jnp.logical_not(near) & (one + two == 1))
    def _():
        visit(j + two, 1, False)


def fwd_kernel(
    code_ref, me_ref, qt_ref, k_ref, v_ref, gap_ref, far_ref, segc_ref, segr_ref,
    ctxt_ref, ctxb_ref, lse_ref, tile_ref, m_ref, l_ref, acc_ref,
):
    fill_tiles(gap_ref, far_ref, tile_ref)
    me = me_ref[0]

    def one_query(qi, _):
        i = me * 2 + qi
        qoff = pl.multiple_of(qi * 128, 128)
        m_ref[...] = jnp.full_like(m_ref, NEG)
        l_ref[...] = jnp.zeros_like(l_ref)
        acc_ref[...] = jnp.zeros_like(acc_ref)

        def visit(j, near):
            keys = pl.ds(pl.multiple_of(j * 128, 128), 128)
            if near:
                off = pl.multiple_of(jnp.minimum(i - j, 2) * 128, 128)
                ok = seg_ok(segc_ref, segr_ref, i, j, 128)
            for p in range(PAIRS):
                cols = slice(128 * p, 128 * p + 128)
                s = mm(k_ref[keys, cols], pair_diag(qt_ref, p, qoff), 1, 0)
                if near:
                    s = jnp.where(ok, s + pair_tiles(tile_ref, p, [off]), NEG)
                else:
                    s = s + far_ref[p : p + 1, :]
                m_old = m_ref[p : p + 1, :]
                m_new = jnp.maximum(m_old, jnp.max(s, axis=0, keepdims=True))
                w = jnp.exp(s - m_new)
                shrink = jnp.exp(m_old - m_new)
                m_ref[p : p + 1, :] = m_new
                l_ref[p : p + 1, :] = l_ref[p : p + 1, :] * shrink + jnp.sum(
                    w, axis=0, keepdims=True
                )
                o = mm(v_ref[keys, cols], w.astype(BF16), 0, 0)
                o = jnp.concatenate([o[:64, :128], o[64:, 128:]], axis=1)
                acc_ref[p] = acc_ref[p] * shrink + o

        visit(i, True)

        def one_key(j, _):
            code = code_ref[i, j]

            @pl.when(code == 1)
            def _():
                visit(j, False)

            @pl.when(code == 2)
            def _():
                visit(j, True)

            return 0

        lax.fori_loop(0, i, one_key, 0)
        for p in range(PAIRS):
            total = l_ref[p : p + 1, :]
            ctx = acc_ref[p] * (1.0 / total)
            both = jnp.concatenate([ctx[:, :128], ctx[:, 128:]], axis=0)
            ctxt_ref[128 * p : 128 * p + 128, pl.ds(qoff, 128)] = both
            ctxb_ref[pl.ds(qoff, 128), 128 * p : 128 * p + 128] = both.T.astype(BF16)
            lse = m_ref[p : p + 1, :] + jnp.log(total)
            lse_ref[2 * p : 2 * p + 1, pl.ds(qoff, 128)] = lse[:, :128]
            lse_ref[2 * p + 1 : 2 * p + 2, pl.ds(qoff, 128)] = lse[:, 128:]
        return 0

    lax.fori_loop(0, 2, one_query, 0)


def bwd_kernel(
    code_ref, me_ref, qt_ref, dt_ref, k_ref, v_ref, stat_ref, gap_ref, far_ref, segc_ref, segr_ref,
    dqkv_ref, dgap_ref, dfar_ref,
    tile_ref, near_ref, facc_ref, dq_ref, dk_ref, dv_ref,
):
    fill_tiles(gap_ref, far_ref, tile_ref)
    near_ref[...] = jnp.zeros_like(near_ref)
    facc_ref[...] = jnp.zeros_like(facc_ref)
    dq_ref[...] = jnp.zeros_like(dq_ref)
    dk_ref[...] = jnp.zeros_like(dk_ref)
    dv_ref[...] = jnp.zeros_like(dv_ref)
    me = me_ref[0]

    def lanes(first, p, i):
        g, at = i // 2, first + 2 * p
        off = pl.multiple_of((i % 2) * 128, 128)
        return jnp.concatenate(
            [stat_ref[g, at : at + 1, pl.ds(off, 128)], stat_ref[g, at + 1 : at + 2, pl.ds(off, 128)]],
            axis=1,
        )

    def visit(i, j, blocks, near, by_query, by_key):
        keys = pl.ds(pl.multiple_of(j * 128, 128), 128 * blocks)
        own = pl.ds(pl.multiple_of((j - 2 * me) * 128, 128), 128 * blocks)
        qoff = pl.multiple_of(i * 128, 128)
        if near:
            offs = tile_ids(code_ref, i, j)
            ok = seg_ok(segc_ref, segr_ref, i, j, 256)
        for p in range(PAIRS):
            cols = slice(128 * p, 128 * p + 128)
            qd, od = pair_diag(qt_ref, p, qoff), pair_diag(dt_ref, p, qoff)
            s = mm(k_ref[keys, cols], qd, 1, 0)
            lse = lanes(0, p, i)
            if near:
                w = jnp.exp(jnp.where(ok, s + pair_tiles(tile_ref, p, offs) - lse, NEG))
            else:
                w = jnp.exp(s + (far_ref[p : p + 1, :] - lse))
            dp = mm(v_ref[keys, cols], od, 1, 0)
            ds = w * (dp - lanes(HEADS, p, i))
            dsb = ds.astype(BF16)
            if by_key:
                dv_ref[p, own] += mm(w.astype(BF16), od, 1, 1)
                dk_ref[p, own] += mm(dsb, qd, 1, 1)
            if by_query:
                qi = i - 2 * me
                o = mm(k_ref[keys, cols], dsb, 0, 0)
                dq_ref[qi, p] += jnp.concatenate([o[:64, :128], o[64:, 128:]], axis=1)
                if near:
                    for n in range(2):
                        for h in range(2):
                            part = ds[128 * n : 128 * n + 128, 128 * h : 128 * h + 128]
                            near_ref[2 * p + h, :, pl.ds(offs[n], 128)] += part
                else:
                    part = ds[0:8]
                    for a in range(1, 16 * blocks):
                        part = part + ds[8 * a : 8 * a + 8]
                    facc_ref[p] += part

    def one_query(qi, _):
        i = me * 2 + qi
        visit(i, 2 * me, 2, True, True, True)

        def two_keys(t, _):
            split_visit(code_ref, i, 2 * t, lambda j, blocks, near: visit(i, j, blocks, near, True, False))
            return 0

        lax.fori_loop(0, me, two_keys, 0)
        for p in range(PAIRS):
            x = dq_ref[qi, p] * 0.125
            both = jnp.concatenate([x[:, :128], x[:, 128:]], axis=0)
            dqkv_ref[pl.ds(pl.multiple_of(qi * 128, 128), 128), 128 * p : 128 * p + 128] = both.T.astype(BF16)
        return 0

    lax.fori_loop(0, 2, one_query, 0)

    def later(i, _):
        split_visit(code_ref, i, 2 * me, lambda j, blocks, near: visit(i, j, blocks, near, False, True))
        return 0

    lax.fori_loop(2 * me + 2, code_ref.shape[0], later, 0)
    for p in range(PAIRS):
        at = D + 128 * p
        dqkv_ref[:, at : at + 128] = dk_ref[p].astype(BF16)
        dqkv_ref[:, D + at : D + at + 128] = dv_ref[p].astype(BF16)

    for h in range(HEADS):
        x = near_ref[h, :, 0:256]
        g = x[0:8]
        for a in range(1, 16):
            g = g + pltpu.roll(x[8 * a : 8 * a + 8], 256 - 8 * a, 1)
        total = g[0:1]
        for b in range(1, 8):
            total = total + pltpu.roll(g, 256 - b, 1)[b : b + 1]
        dgap_ref[h : h + 1, :] = total
        half = 128 * (h % 2)
        far = jnp.sum(facc_ref[h // 2, :, half : half + 128], axis=0, keepdims=True)
        far = far + jnp.sum(near_ref[h, :, 256:384], axis=0, keepdims=True)
        dfar_ref[h : h + 1, :] = far


def vmem():
    return pl.BlockSpec(memory_space=pltpu.VMEM)


def smem():
    return pl.BlockSpec(memory_space=pltpu.SMEM)


def attention_forward(code, me, qt, keys, values, gap, far, segc, segr):
    length = keys.shape[0]
    return pl.pallas_call(
        fwd_kernel,
        name="attention_forward",
        out_shape=[
            jax.ShapeDtypeStruct((D, ROWS), F32),
            jax.ShapeDtypeStruct((ROWS, D), BF16),
            jax.ShapeDtypeStruct((HEADS, ROWS), F32),
        ],
        in_specs=[smem(), smem()] + [vmem()] * 7,
        out_specs=[vmem()] * 3,
        scratch_shapes=[
            pltpu.VMEM((HEADS, 128, 512), F32),
            pltpu.VMEM((8, 256), F32),
            pltpu.VMEM((8, 256), F32),
            pltpu.VMEM((PAIRS, 64, 256), F32),
        ],
        compiler_params=pltpu.CompilerParams(vmem_limit_bytes=VMEM_LIMIT),
        cost_estimate=pl.CostEstimate(
            flops=8 * ROWS * length * D,
            bytes_accessed=32 * length * D,
            transcendentals=HEADS * ROWS * length // 2,
        ),
    )(code, me, qt, keys, values, gap, far, segc, segr)


def attention_backward(code, me, qt, dt, keys, values, stats, gap, far, segc, segr):
    length = keys.shape[0]
    return pl.pallas_call(
        bwd_kernel,
        name="attention_backward",
        out_shape=[
            jax.ShapeDtypeStruct((ROWS, 3 * D), BF16),
            jax.ShapeDtypeStruct((HEADS, 256), F32),
            jax.ShapeDtypeStruct((HEADS, 128), F32),
        ],
        in_specs=[smem(), smem()] + [vmem()] * 9,
        out_specs=[vmem()] * 3,
        scratch_shapes=[
            pltpu.VMEM((HEADS, 128, 512), F32),
            pltpu.VMEM((HEADS, 128, 512), F32),
            pltpu.VMEM((PAIRS, 8, 256), F32),
            pltpu.VMEM((2, PAIRS, 64, 256), F32),
            pltpu.VMEM((PAIRS, 256, 128), F32),
            pltpu.VMEM((PAIRS, 256, 128), F32),
        ],
        compiler_params=pltpu.CompilerParams(vmem_limit_bytes=VMEM_LIMIT),
        cost_estimate=pl.CostEstimate(
            flops=14 * ROWS * length * D,
            bytes_accessed=64 * length * D,
            transcendentals=HEADS * ROWS * length,
        ),
    )(code, me, qt, dt, keys, values, stats, gap, far, segc, segr)


def ffn_kernel(x_ref, gain_ref, own_ref, peer_ref, other_ref, out_ref, norm_ref, hidden_ref, slope_ref):
    x = x_ref[...]
    normed = norm_rows(x, gain_ref[...]).astype(BF16)
    norm_ref[...] = normed
    total = x
    piece = own_ref.shape[2] // 2
    peers = peer_ref.shape[0]
    weights = [own_ref.at[0], own_ref.at[1]]
    for k in range(peers):
        weights += [peer_ref.at[k], other_ref.at[k]]
    for n, ref in enumerate(weights):
        at = slice(n * piece, n * piece + piece)
        hidden, slope = gelu_pair(mm(normed, ref[:, :piece], 1, 0))
        hidden = hidden.astype(BF16)
        hidden_ref[:, at] = hidden
        slope_ref[:, at] = slope
        total = total + mm(hidden, ref[:, piece:], 1, 1)
    out_ref[...] = total


def ffn_forward(x, gain, own, peers, others):
    count = x.shape[0]
    width = own.shape[2] // 2 * (2 + 2 * peers.shape[0])
    return pl.pallas_call(
        ffn_kernel,
        name="ffn_forward",
        in_specs=[vmem()] * 5,
        out_specs=[vmem()] * 4,
        out_shape=[
            jax.ShapeDtypeStruct((count, D), F32),
            jax.ShapeDtypeStruct((count, D), BF16),
            jax.ShapeDtypeStruct((count, width), BF16),
            jax.ShapeDtypeStruct((count, width), F32),
        ],
        compiler_params=pltpu.CompilerParams(vmem_limit_bytes=VMEM_LIMIT),
        cost_estimate=pl.CostEstimate(
            flops=4 * count * D * width, bytes_accessed=8 * D * width, transcendentals=count * width
        ),
    )(x, gain[None, :], own, peers, others)


def gelu_pair(u):
    t = jnp.tanh(GELU_SCALE * (u + GELU_CUBE * u * u * u))
    half = 0.5 * (1.0 + t)
    slope = half + 0.5 * u * (1.0 - t * t) * (GELU_SCALE * (1.0 + 3.0 * GELU_CUBE * u * u))
    return u * half, slope


def expert_rows_kernel(rows_ref, dye_ref, cot_ref, win_ref, wout_ref, made_ref, back_ref, gate_ref, made_acc, back_acc):
    step = pl.program_id(1)

    @pl.when(step == 0)
    def _():
        made_acc[...] = jnp.zeros_like(made_acc)
        back_acc[...] = jnp.zeros_like(back_acc)

    win, wout = win_ref[0], wout_ref[0]
    half = rows_ref.shape[1] // 2
    for c in range(2):
        at = slice(half * c, half * c + half)
        hidden, slope = gelu_pair(mm(rows_ref[0, at], win, 1, 0))
        made_acc[at] += mm(hidden.astype(BF16), wout, 1, 0)
        pre_back = (mm(dye_ref[0, at], wout, 1, 1) * slope).astype(BF16)
        back_acc[at] += mm(pre_back, win, 1, 1)

    @pl.when(step == pl.num_programs(1) - 1)
    def _():
        made = made_acc[...].astype(BF16)
        made_ref[0] = made
        back_ref[0] = back_acc[...]
        gate = jnp.sum(cot_ref[0].astype(F32) * made.astype(F32), axis=1, keepdims=True)
        gate_ref[0] = jnp.broadcast_to(gate, gate_ref.shape[1:])


def expert_rows(rows, dye, cot, w_in, w_out):
    count, total, _ = rows.shape
    width, block = w_in.shape[2], 512
    whole = pl.BlockSpec((1, total, D), lambda e, i: (e, 0, 0))
    return pl.pallas_call(
        expert_rows_kernel,
        name="expert_rows",
        grid=(count, width // block),
        in_specs=[
            whole,
            whole,
            whole,
            pl.BlockSpec((1, D, block), lambda e, i: (e, 0, i)),
            pl.BlockSpec((1, block, D), lambda e, i: (e, i, 0)),
        ],
        out_specs=[whole, whole, pl.BlockSpec((1, total, 128), lambda e, i: (e, 0, 0))],
        out_shape=[
            jax.ShapeDtypeStruct(rows.shape, BF16),
            jax.ShapeDtypeStruct(rows.shape, F32),
            jax.ShapeDtypeStruct((count, total, 128), F32),
        ],
        scratch_shapes=[pltpu.VMEM((total, D), F32), pltpu.VMEM((total, D), F32)],
        compiler_params=pltpu.CompilerParams(vmem_limit_bytes=VMEM_LIMIT),
        cost_estimate=pl.CostEstimate(
            flops=8 * count * total * D * width,
            bytes_accessed=16 * count * D * width,
            transcendentals=count * total * width,
        ),
    )(rows, dye, cot, w_in, w_out)


def expert_kernel(rows_ref, dye_ref, win_ref, wout_ref, *rest):
    in_ref, out_ref = rest[-2:]
    total = rows_ref.shape[1]
    step = total // 3
    win, wout = win_ref[0], wout_ref[0]
    for c in range(3):
        rows = rows_ref[0, step * c : step * c + step]
        dye = dye_ref[0, step * c : step * c + step]
        hidden, slope = gelu_pair(mm(rows, win, 1, 0))
        pre_back = (mm(dye, wout, 1, 1) * slope).astype(BF16)
        grad_in = mm(rows, pre_back, 0, 0)
        grad_out = mm(hidden.astype(BF16), dye, 0, 0)
        if c == 0:
            in_ref[0], out_ref[0] = grad_in, grad_out
        else:
            in_ref[0] += grad_in
            out_ref[0] += grad_out


def expert_gradients(rows, dye, w_in, w_out, part, earlier):
    count, total, _ = rows.shape
    width, block = w_in.shape[2], 512
    steps = width // block // 2
    whole = pl.BlockSpec((1, total, D), lambda e, i: (e, 0, 0))
    by_in = pl.BlockSpec((1, D, block), lambda e, i: (e, 0, i + part * steps))
    by_out = pl.BlockSpec((1, block, D), lambda e, i: (e, i + part * steps, 0))
    return pl.pallas_call(
        expert_kernel,
        name=f"expert_gradients_{part}",
        grid=(count, steps),
        in_specs=[whole, whole, by_in, by_out] + [pl.BlockSpec(memory_space=pl.ANY)] * len(earlier),
        out_specs=[by_in, by_out],
        out_shape=[
            jax.ShapeDtypeStruct(w_in.shape, F32),
            jax.ShapeDtypeStruct(w_out.shape, F32),
        ],
        input_output_aliases={4 + n: n for n in range(len(earlier))},
        compiler_params=pltpu.CompilerParams(vmem_limit_bytes=VMEM_LIMIT),
        cost_estimate=pl.CostEstimate(
            flops=4 * count * total * D * width,
            bytes_accessed=32 * count * D * width,
            transcendentals=count * total * width // 2,
        ),
    )(rows, dye, w_in, w_out, *earlier)


def three_parts(x):
    parts = []
    for _ in range(3):
        parts.append(lax.reduce_precision(x, 8, 7))
        x = x - parts[-1]
    return parts


def block_codes(seg_all, blocks):
    count = blocks.shape[0]
    rows = seg_all.reshape(count, BLK)
    least, most = jnp.min(rows, axis=1), jnp.max(rows, axis=1)
    ids = jnp.arange(count, dtype=jnp.int32)
    gap = ids[:, None] - ids[None, :]
    meet = (most[None, :] >= least[:, None]) & (least[None, :] <= most[:, None])
    live = (gap >= 0) & (blocks == 1) & meet
    same = (
        (least == most)[:, None] & (least == most)[None, :] & (least[:, None] == least[None, :])
    )
    return jnp.where(live, jnp.where(same & (gap >= 2), 1, 2), 0).astype(jnp.int32)


def bias_inputs(table):
    gap = jnp.dot(table, gap_hot().T, precision=PRECISE)
    far = jnp.repeat(table[:, 31].reshape(PAIRS, 2), BLK, axis=1)
    return gap, far


def bias_back(dgap, dfar):
    near = jnp.dot(dgap, gap_hot(), precision=PRECISE)
    last = (jnp.arange(32) == 31).astype(F32)[None, :]
    return near + jnp.sum(dfar, axis=1, keepdims=True) * last


def body(
    tokens, segments, block_sets, routes, qkv_weight, out_weight, ffn_in, ffn_out,
    norm_gains, rel_bias, router, expert_in, expert_out, cotangent,
):
    gather = partial(lax.all_gather, axis_name="grp", axis=0, tiled=True)
    rows = tokens.shape[1]
    me = lax.axis_index("grp").astype(jnp.int32).reshape(1)
    replicas, groups = lax.axis_size("rep"), lax.axis_size("grp")
    mine, core = lax.axis_index("rep"), lax.axis_index("grp") % 2

    def from_replica(x, k):
        return lax.ppermute(x, "rep", [(i, i ^ k) for i in range(replicas)])

    def from_sibling(x):
        return lax.ppermute(x, "grp", [(i, i ^ 1) for i in range(groups)])

    def swapped_cores(got):
        other = from_sibling(jnp.stack(got))
        return [other[k] for k in range(replicas - 1)]

    def layer_quarter(layer, after):
        count = qkv_weight.shape[0] // replicas
        part_qkv = lax.dynamic_slice(
            qkv_weight, (mine * count, layer, 0, 0), (count, 1) + qkv_weight.shape[2:]
        )
        part_out = lax.dynamic_slice(out_weight, (mine * count, layer, 0), (count, 1, D))
        part = jnp.concatenate([part_qkv.reshape(count, 3 * D), part_out.reshape(count, D)], axis=1)
        if after is not None:
            part, _ = lax.optimization_barrier((part, after))
        return lax.all_gather(part, "grp", axis=0)

    def layer_weights(quarter):
        width = quarter.shape[2] // 2
        half = lax.dynamic_slice_in_dim(quarter, core * width, width, 2)
        got = [from_replica(half, k) for k in range(1, replicas)]
        other = swapped_cores(got)
        full = jnp.zeros((groups, replicas) + quarter.shape[1:], BF16)
        full = lax.dynamic_update_slice(full, quarter[:, None], (0, mine, 0, 0))
        for k in range(1, replicas):
            for part, which in ((got[k - 1], core), (other[k - 1], 1 - core)):
                full = lax.dynamic_update_slice(full, part[:, None], (0, mine ^ k, 0, which * width))
        full = full.reshape(-1, 2 * width)
        return full[:, : 3 * D], full[:, 3 * D :]

    quarter_first = layer_quarter(0, None)
    w_first = layer_weights(quarter_first)

    span = ffn_in.shape[1] // replicas
    piece = span // 2
    ffn_own = [lax.dynamic_slice_in_dim(w, mine * span, span, 1) for w in (ffn_in, ffn_out)]
    ffn_own = jnp.concatenate([w[:, h * piece : h * piece + piece] for h in range(2) for w in ffn_own], axis=1)
    ffn_own, quarter_first = lax.optimization_barrier((ffn_own, quarter_first))
    ffn_quarter = gather(ffn_own)
    seg_row = jnp.pad(segments.astype(BF16), ((0, 7), (0, D - rows)))
    tokens_own = jnp.concatenate([tokens[0], seg_row], axis=0)
    tokens_own, ffn_quarter = lax.optimization_barrier((tokens_own, ffn_quarter))
    tokens_all = lax.all_gather(tokens_own, "grp", axis=0)
    ffn_mine = [lax.dynamic_slice_in_dim(ffn_quarter, n * span, span, 1) for n in (core, 1 - core)]
    ffn_peers = [from_replica(ffn_mine[0], k) for k in range(1, replicas)]

    quarter_second = layer_quarter(1, tokens_all)
    x_all = tokens_all[:, :rows].reshape(-1, D)
    seg_all = tokens_all[:, rows, :rows].astype(jnp.int32).reshape(-1)
    code = block_codes(seg_all, block_sets[0])
    shared = (seg_all[:, None], seg_all.reshape(-1, BLK))
    w_qkv, w_out = [w_first[0]], [w_first[1]]

    def attend(residual, normed, normed_all, layer):
        w = w_qkv[layer]
        qt = mm(w[:, :D], normed, 0, 1).astype(BF16) * jnp.asarray(0.125, BF16)
        keys = mm(normed_all, w[:, D : 2 * D], 1, 0).astype(BF16)
        values = mm(normed_all, w[:, 2 * D :], 1, 0).astype(BF16)
        gap, far = bias_inputs(rel_bias[layer])
        ctxt, ctxb, lse = attention_forward(code, me, qt, keys, values, gap, far, *shared)
        branch = mm(ctxb, w_out[layer], 1, 0)
        saved = (residual, normed, normed_all, keys, values, ctxt, ctxb, lse, gap, far)
        return residual + branch, saved

    def attend_back(grad_out, saved, layer, qt_all, held, cover):
        residual, normed, normed_all, keys, values, ctxt, ctxb, lse, gap, far = saved
        w, wo = w_qkv[layer], w_out[layer]
        grad_low = grad_out.astype(BF16)
        dctx_own = mm(wo, grad_low, 1, 1).astype(BF16)
        delta = jnp.sum((dctx_own.astype(F32) * ctxt).reshape(HEADS, HEAD, rows), axis=1)
        stats = jnp.stack(three_parts(jnp.concatenate([lse, delta], axis=0)), axis=1)
        stats = stats.reshape(2 * HEADS, 3 * rows).astype(BF16)
        sent = jnp.concatenate([grad_low, stats, jnp.zeros((8, D), BF16)], axis=0)
        got, covered = lax.optimization_barrier((lax.all_gather(sent, "grp", axis=0), cover(sent)))
        grad_all = got[:, :rows].reshape(-1, D)
        stats_all = got[:, rows : rows + 2 * HEADS].reshape(-1, 2 * HEADS, 3, rows)
        stats_all = jnp.sum(stats_all.astype(F32), axis=2)
        dt_all = mm(wo, grad_all, 1, 1).astype(BF16)
        dt_all, held = lax.optimization_barrier((dt_all, held))
        dqkv, dgap, dfar = attention_backward(
            code, me, qt_all, dt_all, keys, values, stats_all, gap, far, *shared
        )
        out_part = mm(ctxb, grad_low, 0, 0)
        qkv_part = mm(normed, dqkv, 0, 0)
        normed_grad = mm(dqkv, w, 1, 1)
        _, pull_back = jax.vjp(norm_rows, residual, norm_gains[layer, 0])
        residual_grad, gain_grad = pull_back(normed_grad)
        table_grad = bias_back(dgap, dfar)
        return grad_out + residual_grad, qkv_part, out_part, gain_grad, table_grad, grad_all, held, covered

    experts_all = router.shape[1]
    per_group = experts_all // groups
    capacity = rows * 2 * 10 // (7 * experts_all) + 1
    slots = (capacity + 16) // 16 * 16
    chosen = routes[0]
    ids = jnp.arange(experts_all, dtype=jnp.int32)
    chosen_hot = (chosen[:, :, None] == ids[None, None, :]).astype(F32)
    flat_hot = chosen_hot.reshape(2 * rows, experts_all)
    before = jnp.tril(jnp.ones((2 * rows, 2 * rows), BF16), -1)
    earlier = mm(before, flat_hot.astype(BF16), 1, 0)
    slot_ids = jnp.sum(earlier * flat_hot, axis=1).astype(jnp.int32)
    place = (chosen.reshape(-1) * slots + slot_ids).reshape(rows, 2)
    lanes = jnp.arange(experts_all * slots, dtype=jnp.int32)
    pick = [(place[:, k][:, None] == lanes[None, :]).astype(BF16) for k in range(2)]
    both = pick[0] + pick[1]

    def exchange(x):
        return lax.all_to_all(
            x.reshape(groups, per_group * slots, D), "grp", split_axis=0, concat_axis=0, tiled=True
        )

    def by_expert(x):
        return x.reshape(groups, per_group, slots, -1).swapaxes(0, 1).reshape(per_group, groups * slots, -1)

    def by_source(x):
        return x.reshape(per_group, groups, slots, -1).swapaxes(0, 1).reshape(groups, per_group * slots, -1)

    def all_replicas(x):
        return lax.all_gather(x, "rep", axis=1, tiled=True)

    stream = tokens[0].astype(F32)
    own_a = norm_rows(stream, norm_gains[0, 0]).astype(BF16)
    all_a = norm_rows(x_all.astype(F32), norm_gains[0, 0]).astype(BF16)
    first_out, saved_a = attend(stream, own_a, all_a, 0)
    first_out, quarter_second, ffn_peers = lax.optimization_barrier(
        (first_out, quarter_second, ffn_peers)
    )
    ffn_peers = jnp.stack(ffn_peers)
    ffn_others = from_sibling(ffn_peers)
    after_ffn, normed_ffn, hidden_ffn, slope_ffn = ffn_forward(
        first_out, norm_gains[0, 1], jnp.stack(ffn_mine), ffn_peers, ffn_others
    )

    w_second = layer_weights(quarter_second)
    w_qkv.append(w_second[0])
    w_out.append(w_second[1])
    own_b = norm_rows(after_ffn, norm_gains[1, 0]).astype(BF16)
    pieces = ffn_mine + [x[k] for k in range(replicas - 1) for x in (ffn_peers, ffn_others)]
    full_in = jnp.concatenate([x[:, :piece] for x in pieces], axis=1)
    full_down = jnp.concatenate([x[:, piece:] for x in pieces], axis=1)
    all_b, cot_own, full_in, full_down = lax.optimization_barrier(
        (gather(own_b), cotangent[0], full_in, full_down)
    )
    cot_rows = by_expert(exchange(mm(both, cot_own, 0, 0).astype(BF16)))
    second_out, saved_b = attend(after_ffn, own_b, all_b, 1)
    second_out, cot_rows = lax.optimization_barrier((second_out, cot_rows))
    cot_all = all_replicas(cot_rows)
    normed_moe = norm_rows(second_out, norm_gains[1, 1]).astype(BF16)
    normed_wide = normed_moe.astype(F32)
    router_wide = router.astype(F32)
    logits = jnp.dot(normed_wide, router_wide, precision=PRECISE)

    last_row = (jnp.arange(slots) == slots - 1)[None, :, None]

    def with_scalars(rows_in, values):
        parts = [jnp.pad(part, ((0, 0), (0, 128 - slots))) for part in three_parts(values)]
        info = jnp.concatenate(parts + [jnp.zeros((values.shape[0], D - 384), F32)], axis=1)
        return jnp.where(last_row, info[:, None, :], rows_in).astype(BF16)

    def scalars_of(rows_in):
        info = rows_in[:, slots - 1, :].astype(F32)
        total = info[:, 0:slots] + info[:, 128 : 128 + slots] + info[:, 256 : 256 + slots]
        return jnp.where(jnp.arange(slots)[None, :] == slots - 1, 0.0, total)

    grad_final = cotangent[0].astype(F32)
    selected = jnp.sum(logits[:, None, :] * chosen_hot, axis=-1)
    gate_probs = jax.nn.softmax(selected, axis=-1)
    gate_slots = jnp.sum(
        jnp.where(pick[0] == 1, gate_probs[:, 0:1], 0.0) + jnp.where(pick[1] == 1, gate_probs[:, 1:2], 0.0),
        axis=0,
    ).reshape(experts_all, slots)
    sent = mm(both, normed_moe, 0, 0).reshape(experts_all, slots, D)
    rows_e = by_expert(exchange(with_scalars(sent, gate_slots)))

    def gated(rows_in, cot):
        gates = scalars_of(rows_in.reshape(-1, slots, D)).reshape(per_group, -1, 1)
        return (gates * cot.astype(F32)).astype(BF16)

    dye = gated(rows_e, cot_rows)
    made_rows, rows_grad, gate_back = expert_rows(rows_e, dye, cot_rows, expert_in, expert_out)
    rows_grad = rows_grad.reshape(per_group * groups, slots, D)
    rows_grad = with_scalars(rows_grad, gate_back[:, :, 0].reshape(-1, slots))
    queries_all = [
        mm(w_qkv[n][:, :D], all_rows, 0, 1).astype(BF16) * jnp.asarray(0.125, BF16)
        for n, all_rows in enumerate((all_a, all_b))
    ]
    back_grad, rows_all, cot_all, queries_all = lax.optimization_barrier(
        (exchange(by_source(rows_grad)), all_replicas(rows_e), cot_all, queries_all)
    )
    back_slots = scalars_of(back_grad.reshape(experts_all, slots, D)).reshape(1, -1)
    back_grad = back_grad.reshape(experts_all * slots, D)
    gate_grad = jnp.stack(
        [jnp.sum(jnp.where(pick[k] == 1, back_slots, 0.0), axis=1) for k in range(2)], axis=-1
    )
    select_grad = gate_probs * (gate_grad - jnp.sum(gate_probs * gate_grad, axis=-1, keepdims=True))
    logit_grad = jnp.sum(select_grad[:, :, None] * chosen_hot, axis=1)
    normed_moe_grad = jnp.dot(logit_grad, router_wide.T, precision=PRECISE) + mm(both, back_grad, 1, 0)
    _, pull_moe = jax.vjp(norm_rows, second_out, norm_gains[1, 1])
    moe_resid_grad, moe_gain_grad = pull_moe(normed_moe_grad)
    grad_second = grad_final + moe_resid_grad
    router_part = jnp.dot(normed_wide.T, logit_grad, precision=PRECISE)

    def finish(made):
        returned = exchange(by_source(made)).reshape(experts_all * slots, D)
        picked = [mm(pick[k], returned, 1, 0) for k in range(2)]
        return second_out + gate_probs[:, 0:1] * picked[0] + gate_probs[:, 1:2] * picked[1]

    dye_all = gated(rows_all, cot_all)

    def expert_half(part, earlier):
        def run(sent):
            rows_in, _ = lax.optimization_barrier((rows_all, sent))
            return tuple(expert_gradients(rows_in, dye_all, expert_in, expert_out, part, earlier))

        return run

    back_b = attend_back(grad_second, saved_b, 1, queries_all[1], made_rows, expert_half(0, ()))
    grad_ffn, qkv_part_b, out_part_b, gain_grad_b, table_grad_b, _, made_held, expert_sums = back_b
    final_out = finish(made_held)
    grad_ffn, final_out = lax.optimization_barrier((grad_ffn, final_out))
    down_low = grad_ffn.astype(BF16)
    down_part = mm(down_low, hidden_ffn, 0, 0)
    hidden_ffn_grad = mm(down_low, full_down, 1, 0)
    pre_ffn_grad = (hidden_ffn_grad * slope_ffn).astype(BF16)
    in_part = mm(normed_ffn, pre_ffn_grad, 0, 0)
    normed_ffn_grad = mm(pre_ffn_grad, full_in, 1, 1)
    _, pull_ffn = jax.vjp(norm_rows, first_out, norm_gains[0, 1])
    ffn_resid_grad, ffn_gain_grad = pull_ffn(normed_ffn_grad)
    grad_first = grad_ffn + ffn_resid_grad
    def packed(parts):
        return jnp.concatenate([part.astype(BF16) for part in parts], axis=1)

    def halves(k, which):
        at = k * span + which * piece
        return packed([x[:, at : at + piece] for x in (down_part, in_part)])

    theirs = from_sibling(jnp.stack([halves(k, 1) for k in range(replicas)]))
    ffn_parts = [
        (halves(k, 0).astype(F32) + theirs[k].astype(F32)).astype(BF16) for k in range(replicas)
    ]
    ffn_got = [from_replica(ffn_parts[k], k) for k in range(1, replicas)]
    back_a = attend_back(grad_first, saved_a, 0, queries_all[0], (), expert_half(1, expert_sums))
    grad_tokens, qkv_part_a, out_part_a, gain_grad_a, table_grad_a, grad_all_a, _, expert_sums = back_a
    expert_in_sum, expert_out_sum = expert_sums
    parts_b, _ = lax.optimization_barrier((packed([qkv_part_b, out_part_b]), grad_all_a))
    parts_a = packed([qkv_part_a, out_part_a])
    shard_b = lax.psum_scatter(parts_b, "grp", scatter_dimension=0, tiled=True)
    parts_a, shard_b, ffn_got = lax.optimization_barrier((parts_a, shard_b, ffn_got))

    def scatter(x):
        return lax.psum_scatter(x, "grp", scatter_dimension=0, tiled=True)

    def over_replicas(x, cut):
        half = x.shape[0] // 2

        def add(v, mask):
            return (v.astype(F32) + from_replica(v, mask).astype(F32)).astype(BF16)

        first = [1 << b for b in range(replicas.bit_length() - 1)]
        top, low = x[:half], x[half:]
        for a, b in zip(first, first[::-1]):
            top, low = add(top, a), add(low, b)
        x = jnp.concatenate([top, low], axis=0).astype(F32)
        return x[:, :cut], x[:, cut:]

    shard_a = lax.psum_scatter(parts_a, "grp", scatter_dimension=0, tiled=True)
    ffn_total = ffn_parts[0].astype(F32)
    for x in ffn_got:
        ffn_total = ffn_total + x.astype(F32)
    down_half, in_half = ffn_total[:, :piece], ffn_total[:, piece:]
    ffn_total = jnp.concatenate(
        [jnp.where(core == h, x, 0.0) for x in (in_half, down_half) for h in range(2)], axis=1
    )
    shard_a, ffn_total = lax.optimization_barrier((shard_a, ffn_total.astype(BF16)))
    ffn_shard = scatter(ffn_total)
    ffn_sums = jnp.stack([ffn_shard] + [from_replica(ffn_shard, k) for k in range(1, replicas)])
    ffn_sums = [lax.dynamic_index_in_dim(ffn_sums, mine ^ q, 0, False).astype(F32) for q in range(replicas)]
    in_sum = jnp.concatenate([x[:, :span] for x in ffn_sums], axis=1)
    down_sum = jnp.concatenate([x[:, span:] for x in ffn_sums], axis=1)
    qkv_b, out_b = over_replicas(shard_b, 3 * D)
    qkv_a, out_a = over_replicas(shard_a, 3 * D)
    qkv_sum = jnp.stack([qkv_a, qkv_b], axis=1).reshape(qkv_weight.shape)
    out_sum = jnp.stack([out_a, out_b], axis=1)
    gain_all = jnp.stack(
        [jnp.stack([gain_grad_a, ffn_gain_grad]), jnp.stack([gain_grad_b, moe_gain_grad])]
    )
    table_all = jnp.stack([table_grad_a, table_grad_b])
    small = [gain_all, table_all, router_part]
    flat = jnp.concatenate([x.reshape(-1, BLK) for x in small], axis=0)
    for axis, count in (("rep", replicas), ("grp", groups)):
        for bit in range(count.bit_length() - 1):
            flat = flat + lax.ppermute(flat, axis, [(i, i ^ (1 << bit)) for i in range(count)])
    sizes = [x.size // BLK for x in small]
    cut = [flat[sum(sizes[:n]) : sum(sizes[: n + 1])].reshape(x.shape) for n, x in enumerate(small)]
    gain_sum, table_sum, router_sum = cut
    return (
        final_out[None], grad_tokens[None], qkv_sum, out_sum, in_sum, down_sum,
        gain_sum, table_sum, router_sum, expert_in_sum, expert_out_sum,
    )


def solution(mesh):
    return jax.shard_map(
        body,
        mesh=mesh,
        in_specs=(
            P("rep", "grp", None),
            P("rep", "grp"),
            P("rep", None, None),
            P("rep", "grp", None),
            P("grp", None, None, None),
            P("grp", None, None),
            P("grp", None),
            P("grp", None),
            P(),
            P(),
            P(),
            P("grp", None, None),
            P("grp", None, None),
            P("rep", "grp", None),
        ),
        out_specs=(
            P("rep", "grp", None),
            P("rep", "grp", None),
            P("grp", None, None, None),
            P("grp", None, None),
            P("grp", None),
            P("grp", None),
            P(),
            P(),
            P(),
            P("grp", None, None),
            P("grp", None, None),
        ),
        check_vma=False,
    )
```

time: 1220 us -> 800 us (0.66)
  waiting for transfers between devices: 653 us -> 222 us
  blocking collectives: 188 us -> 35.6 us
  Pallas kernels: 93.6 us -> 191 us
  matrix products: 170 us -> 104 us
  other arithmetic: 33.7 us -> 89.2 us
  local copies, waits for them, and re-layouts: 49.7 us -> 87.1 us
  starting transfers between devices: 8.75 us -> 45.9 us
    psum x1 -> x0, waiting for transfers between devices: 194 us -> none  [total(): return lax.psum(x.astype(BF16), 'rep').astype(F32)]
    reduce_scatter x6 -> x3, waiting for transfers between devices: 194 us -> 21.6 us  [the longest x1 17.6 us: scatter(): return lax.psum_scatter(x, 'grp', scatter_dimension=0, tiled=True)]
    pallas_call x0 -> x4, Pallas kernels: none -> 117 us  [the longest x2 82.7 us: expert_gradients(): pl.pallas_call(expert_kernel, name=f'expert_gradients_{part}', grid=(coun...]
    all_gather x10 -> x9, waiting for transfers between devices: 213 us -> 115 us  [the longest x1 28 us: body(): ffn_quarter = gather(ffn_own)]
    all_gather x5 -> x0, blocking collectives: 75.7 us -> none  [the longest x2 31.7 us: attend_back(): delta_all = lax.all_gather(delta, 'grp', axis=0)]
    ppermute x0 -> x32, waiting for transfers between devices: none -> 62.7 us  [the longest x23 38.9 us: from_replica(): return lax.ppermute(x, 'rep', [(i, i ^ k) for i in range(replicas)])]
    dot_general x6 -> x0, matrix products: 45.3 us -> none  [each(): lax.dot_general(a, b, (((ca,), (cb,)), ((0,), (0,))), preferred_element_t...]
    psum x1 -> x0, blocking collectives: 40 us -> none  [body(): lax.psum((gain_all, table_all, router_part), ('rep', 'grp'))]
  transfers between devices with their start and end apart: 19 -> 47, of which waited for: 15 -> 28; matrix products, arithmetic and copies ran while one was open for 13% -> 27% of each run, Pallas kernels for 4% -> 24%
where the time goes in v2:
time: 800 us; the launch traced here: 791 us
  waiting for transfers between devices  222 us (28%)
  Pallas kernels  191 us (24%)
  matrix products  104 us (13%)
  other arithmetic  89.2 us (11%)
  local copies, waits for them, and re-layouts  87.1 us (11%)
  starting transfers between devices  45.9 us (6%)
  blocking collectives  35.6 us (4%)
  between operations  16.2 us (2%)
    dot_general x30, matrix products, mm(): lax.dot_general(a, b, (((ca,), (cb,)), ((), ())), preferred_element_type=...  96.5 us
    pallas_call x2, Pallas kernels, expert_gradients(): pl.pallas_call(expert_kernel, name=f'expert_gradients_{part}', grid=(coun...  82.7 us
    pallas_call x2, Pallas kernels, attention_backward(): pl.pallas_call(bwd_kernel, name='attention_backward', out_shape=[jax.Shap...  60.2 us
    ppermute x23, waiting for transfers between devices, from_replica(): return lax.ppermute(x, 'rep', [(i, i ^ k) for i in range(replicas)])  38.9 us
    unnamed x199, local copies, waits for them, and re-layouts  37 us
    all_to_all x1, blocking collectives, exchange(): lax.all_to_all(x.reshape(groups, per_group * slots, D), 'grp', split_axis...  35.6 us
    all_gather x1, waiting for transfers between devices, body(): ffn_quarter = gather(ffn_own)  28 us
    ppermute x23, starting transfers between devices, from_replica(): return lax.ppermute(x, 'rep', [(i, i ^ k) for i in range(replicas)])  26.6 us
  transfers between devices with their start and end apart: 47, of which 28 were waited for; matrix products, arithmetic and copies ran while one was open for 27% of the time, Pallas kernels for 24%

profile of v2, /device:TPU:0, one launch (start us, length us, event | category | flops | bytes accessed | tf_op | source)
XLA Modules:
  0.0 790.5 jit_solution(288709695356845196)
XLA Ops:
  13.1 23.7 %all-gather.23.cloned.1.call-done = bf16[192,3072]{1,0:T(8,128)(2,1)} async-done(((bf16[24,3072]{1,0:T(8,128)(2,1)}), bf16[192,3072]{1,0:T(8,128)(2,1)}) %all-gather.23.cloned.1.call-update) | async-done | bytes 1179664 | tf_op jit(solution)/shard_map/all_gather | solution.py:559
  42.4 28.0 %all-gather.15.cloned.1.call-done = bf16[768,1536]{1,0:T(8,128)(2,1)} async-done(((bf16[96,1536]{1,0:T(8,128)(2,1)}), bf16[768,1536]{1,0:T(8,128)(2,1)}) %all-gather.15.cloned.1.call-update) | async-done | bytes 2359312 | tf_op jit(solution)/shard_map/all_gather | solution.py:582
  89.4 21.5 %all-gather.25.cloned.1.call-done = bf16[2112,768]{1,0:T(8,128)(2,1)} async-done(((bf16[264,768]{1,0:T(8,128)(2,1)}), bf16[2112,768]{1,0:T(8,128)(2,1)}) %all-gather.25.cloned.1.call-update) | async-done | bytes 3244048 | tf_op jit(solution)/shard_map/all_gather | solution.py:586
  126.9 6.7 convolution_convert_fusion.10.v_ref
  138.9 6.9 attention_forward.2
  186.6 11.7 %collective-permute-done.9 = bf16[8,24,1536]{2,1,0:T(8,128)(2,1)} collective-permute-done((bf16[8,24,1536]{2,1,0:T(8,128)(2,1)}, bf16[8,24,1536]{2,1,0:T(8,128)(2,1)}, u32[]{:S(2)}, u32[]{:S(2)}) %collective-permute-start.9) | collective-permute-done | bytes 589856 | tf_op jit(solution)/shard_map/ppermute | solution.py:541
  202.9 11.0 %ffn_forward.1 = (f32[256,768]{1,0:T(8,128)}, bf16[256,768]{1,0:T(8,128)(2,1)}, bf16[256,3072]{1,0:T(8,128)(2,1)}, f32[256,3072]{1,0:T(8,128)}) custom-call(f32[256,768]{1,0:T(8,128)} %convert_add_fusion.5.x_ref, f32[1,768]{1,0:T(1,128)} %get-tuple-element.292.gain_ref, bf16[2,768,768]{2,1,0:T(8,128)(2,1)} %pad_maximum_fusion.4.own_ref, ...), custom_call_target="tpu_custom_call" | custom-call | flops 2415919104 | bytes 18874368 | tf_op jit(solution)/shard_map/ffn_forward/pallas_call | solution.py:368
  237.9 23.3 %all-gather.17.cloned.1.call-done = bf16[2048,768]{1,0:T(8,128)(2,1)} async-done(((bf16[256,768]{1,0:T(8,128)(2,1)}), bf16[2048,768]{1,0:T(8,128)(2,1)}) %all-gather.17.cloned.1.call-update) | async-done | bytes 3145744 | tf_op jit(solution)/shard_map/all_gather | solution.py:685
  269.1 6.6 convolution_convert_fusion.8.v_ref
  275.7 5.6 convolution_convert_fusion.9.k_ref
  281.3 6.9 attention_forward.3
  290.2 5.7 all-to-all-done
  299.6 35.6 %all_to_all.20 = bf16[8,96,768]{2,1,0:T(8,128)(2,1)} all-to-all(bf16[8,96,768]{2,1,0:T(8,128)(2,1)S(1)} %select_convert_fusion.1), channel_id=1, replica_groups=mesh['rep'=4,'grp'=8] {'grp'}, dimensions={0} | all-to-all | bytes 2359296 | tf_op jit(solution)/shard_map/all_to_all | solution.py:651
  337.5 23.4 %expert_rows.1 = (bf16[1,768,768]{2,1,0:T(8,128)(2,1)}, f32[1,768,768]{2,1,0:T(8,128)}, f32[1,768,128]{2,1,0:T(8,128)}) custom-call(bf16[1,768,768]{2,1,0:T(8,128)(2,1)} %bitcast.323, bf16[1,768,768]{2,1,0:T(8,128)(2,1)} %multiply_convert_fusion.2.dye_ref, bf16[1,768,768]{2,1,0:T(8,128)(2,1)} %bitcast.320, bf16[1,768,3072]{2,1,0:T(8,128)(2,1)} %win_ref.5, ...), custom_call_target="tpu_custom_call" | custom-call | flops 14495514624 | bytes 37748736 | tf_op jit(solution)/shard_map/expert_rows/pallas_call | solution.py:423
  369.6 6.7 fusion.6.qt_ref
  381.6 16.4 %all-to-all-done.2 = bf16[8,96,768]{2,1,0:T(8,128)(2,1)S(1)} async-done(((bf16[8,96,768]{2,1,0:T(8,128)(2,1)}), bf16[8,96,768]{2,1,0:T(8,128)(2,1)S(1)}, u32[]{:S(2)}, u32[]{:S(2)}) %all-to-all-start.2) | async-done | bytes 1179680 | tf_op jit(solution)/shard_map/all_to_all | solution.py:651
  398.0 18.8 %all-gather.19.cloned.1.call-done.rows_ref = bf16[1,3072,768]{2,1,0:T(8,128)(2,1)} async-done(((bf16[1,768,768]{2,1,0:T(8,128)(2,1)}), bf16[1,3072,768]{2,1,0:T(8,128)(2,1)}) %all-gather.19.cloned.1.call-update) | async-done | bytes 4718608 | tf_op jit(solution)/shard_map/all_gather | solution.py:662
  431.1 41.2 %expert_gradients_0.1 = (f32[1,768,3072]{2,1,0:T(8,128)}, f32[1,3072,768]{2,1,0:T(8,128)}) custom-call(bf16[1,3072,768]{2,1,0:T(8,128)(2,1)} %all-gather.19.cloned.1.call-done.rows_ref, bf16[1,3072,768]{2,1,0:T(8,128)(2,1)} %multiply_convert_fusion.dye_ref, bf16[1,768,3072]{2,1,0:T(8,128)(2,1)} %win_ref.5, bf16[1,3072,768]{2,1,0:T(8,128)(2,1)} %wout_ref.5), custom_call_target="tpu_custom_call" | custom-call | flops 28991029248 | bytes 75497472 | tf_op jit(solution)/shard_map/expert_gradients_0/pallas_call | solution.py:476
  490.1 30.1 %attention_backward.2 = (bf16[256,2304]{1,0:T(8,128)(2,1)}, f32[12,256]{1,0:T(8,128)}, f32[12,128]{1,0:T(8,128)}) custom-call(s32[16,16]{1,0:T(8,128)} %select_select_fusion.code_ref, s32[1]{0:T(128)} %bitcast.7.me_ref, bf16[768,2048]{1,0:T(8,128)(2,1)} %fusion.7.qt_ref, bf16[768,2048]{1,0:T(8,128)(2,1)} %convolution_convert_fusion.5.dt_ref, ...), custom_call_target="tpu_custom_call" | custom-call | flops 5637144576 | bytes 100663296 | tf_op jit(solution)/shard_map/attention_backward/pallas_call | solution.py:318
  553.1 41.5 %expert_gradients_1.1 = (f32[1,768,3072]{2,1,0:T(8,128)}, f32[1,3072,768]{2,1,0:T(8,128)}) custom-call(bf16[1,3072,768]{2,1,0:T(8,128)(2,1)} %all-gather.19.cloned.1.call-done.rows_ref, bf16[1,3072,768]{2,1,0:T(8,128)(2,1)} %multiply_convert_fusion.dye_ref, bf16[1,768,3072]{2,1,0:T(8,128)(2,1)} %win_ref.5, ...), custom_call_target="tpu_custom_call", output_to_operand_aliasing={{0}: (4, {}), {1}: (5, {})} | custom-call | flops 28991029248 | bytes 75497472 | tf_op jit(solution)/shard_map/expert_gradients_1/pallas_call | solution.py:476
  606.5 7.0 collective-permute-done.12
  624.8 6.7 convolution_convert_fusion.4.dt_ref
  631.5 30.1 %attention_backward.3 = (bf16[256,2304]{1,0:T(8,128)(2,1)}, f32[12,256]{1,0:T(8,128)}, f32[12,128]{1,0:T(8,128)}) custom-call(s32[16,16]{1,0:T(8,128)} %select_select_fusion.code_ref, s32[1]{0:T(128)} %bitcast.7.me_ref, bf16[768,2048]{1,0:T(8,128)(2,1)} %fusion.6.qt_ref, bf16[768,2048]{1,0:T(8,128)(2,1)} %convolution_convert_fusion.4.dt_ref, ...), custom_call_target="tpu_custom_call" | custom-call | flops 5637144576 | bytes 100663296 | tf_op jit(solution)/shard_map/attention_backward/pallas_call | solution.py:318
  747.8 17.6 %reduce-scatter.8.cloned.1.call-done = bf16[96,1536]{1,0:T(8,128)(2,1)} async-done(((bf16[768,1536]{1,0:T(8,128)(2,1)}), bf16[96,1536]{1,0:T(8,128)(2,1)}) %reduce-scatter.8.cloned.1.call-update) | async-done | bytes 294928 | tf_op jit(solution)/shard_map/reduce_scatter | solution.py:794
  (523 shorter events, 341.8 us)
Async XLA Ops:
  11.3 59.1 %all-gather.15.cloned.1.call-start = ((), (), s32[]{:S(2)}) async-start(), calls=%async_computation.7 | async-start | bytes 2654208 | tf_op jit(solution)/shard_map/all_gather | solution.py:582
  36.8 74.1 %all-gather.25.cloned.1.call-start = ((), (), s32[]{:S(2)}) async-start(), calls=%async_computation.15 | async-start | bytes 3649536 | tf_op jit(solution)/shard_map/all_gather | solution.py:586
  38.8 34.5 %collective-permute-start.2 = (bf16[8,24,1536]{2,1,0:T(8,128)(2,1)S(1)}, bf16[8,24,1536]{2,1,0:T(8,128)(2,1)S(1)}, u32[]{:S(2)}, u32[]{:S(2)}) collective-permute-start(bf16[8,24,1536]{2,1,0:T(8,128)(2,1)S(1)} %constant_dynamic-slice_fusion.5), channel_id=1, source_target_pairs={{0,24},{8,16},{16,8},{24,0},{1,25},{9,17},{17,9},{25,1},{2,26},{10... | collective-permute-start | bytes 1769480 | tf_op jit(solution)/shard_map/ppermute | solution.py:541
  41.3 32.1 %collective-permute-start.1 = (bf16[8,24,1536]{2,1,0:T(8,128)(2,1)S(1)}, bf16[8,24,1536]{2,1,0:T(8,128)(2,1)S(1)}, u32[]{:S(2)}, u32[]{:S(2)}) collective-permute-start(bf16[8,24,1536]{2,1,0:T(8,128)(2,1)S(1)} %constant_dynamic-slice_fusion.5), channel_id=1, source_target_pairs={{0,16},{8,24},{16,0},{24,8},{1,17},{9,25},{17,1},{25,9},{2,18},{10... | collective-permute-start | bytes 1769480 | tf_op jit(solution)/shard_map/ppermute | solution.py:541
  41.8 31.5 %collective-permute-start = (bf16[8,24,1536]{2,1,0:T(8,128)(2,1)S(1)}, bf16[8,24,1536]{2,1,0:T(8,128)(2,1)S(1)}, u32[]{:S(2)}, u32[]{:S(2)}) collective-permute-start(bf16[8,24,1536]{2,1,0:T(8,128)(2,1)S(1)} %constant_dynamic-slice_fusion.5), channel_id=1, source_target_pairs={{0,8},{8,0},{16,24},{24,16},{1,9},{9,1},{17,25},{25,17},{2,10},{10... | collective-permute-start | bytes 1769480 | tf_op jit(solution)/shard_map/ppermute | solution.py:541
  70.4 78.1 %all-gather.27.cloned.1.call-start = ((), (), s32[]{:S(2)}) async-start(), calls=%async_computation.16 | async-start | bytes 1327104 | tf_op jit(solution)/shard_map/all_gather | solution.py:559
  85.9 62.6 %collective-permute-start.6 = (bf16[768,768]{1,0:T(8,128)(2,1)}, bf16[768,768]{1,0:T(8,128)(2,1)S(1)}, u32[]{:S(2)}, u32[]{:S(2)}) collective-permute-start(bf16[768,768]{1,0:T(8,128)(2,1)} %get-tuple-element.241), channel_id=1, source_target_pairs={{0,24},{8,16},{16,8},{24,0},{1,25},{9,17},{17,9},{25,1},{2,26},{10... | collective-permute-start | bytes 3538952 | tf_op jit(solution)/shard_map/ppermute | solution.py:541
  88.3 60.2 %collective-permute-start.5 = (bf16[768,768]{1,0:T(8,128)(2,1)}, bf16[768,768]{1,0:T(8,128)(2,1)S(1)}, u32[]{:S(2)}, u32[]{:S(2)}) collective-permute-start(bf16[768,768]{1,0:T(8,128)(2,1)} %get-tuple-element.241), channel_id=1, source_target_pairs={{0,16},{8,24},{16,0},{24,8},{1,17},{9,25},{17,1},{25,9},{2,18},{10... | collective-permute-start | bytes 3538952 | tf_op jit(solution)/shard_map/ppermute | solution.py:541
  88.9 59.6 %collective-permute-start.4 = (bf16[768,768]{1,0:T(8,128)(2,1)}, bf16[768,768]{1,0:T(8,128)(2,1)}, u32[]{:S(2)}, u32[]{:S(2)}) collective-permute-start(bf16[768,768]{1,0:T(8,128)(2,1)} %get-tuple-element.241), channel_id=1, source_target_pairs={{0,8},{8,0},{16,24},{24,16},{1,9},{9,1},{17,25},{25,17},{2,10},{10... | collective-permute-start | bytes 3538952 | tf_op jit(solution)/shard_map/ppermute | solution.py:541
  119.4 141.8 %all-gather.17.cloned.1.call-start = ((), (), s32[]{:S(2)}) async-start(), calls=%async_computation.8 | async-start | bytes 3538944 | tf_op jit(solution)/shard_map/all_gather | solution.py:685
  153.3 47.8 %collective-permute-start.7 = (bf16[3,768,768]{2,1,0:T(8,128)(2,1)}, bf16[3,768,768]{2,1,0:T(8,128)(2,1)S(1)}, u32[]{:S(2)}, u32[]{:S(2)}) collective-permute-start(bf16[3,768,768]{2,1,0:T(8,128)(2,1)} %pad_maximum_fusion.3.peer_ref), channel_id=1, source_target_pairs={{0,1},{1,0},{2,3},{3,2},{4,5},{5,4},{6,7},{7,6},{8,9},{9,8},{10,11... | collective-permute-start | bytes 10616840 | tf_op jit(solution)/shard_map/ppermute | solution.py:544
  262.9 32.9 %all-to-all-start = ((bf16[8,96,768]{2,1,0:T(8,128)(2,1)}), bf16[8,96,768]{2,1,0:T(8,128)(2,1)S(1)}, u32[]{:S(2)}, u32[]{:S(2)}) async-start(bf16[8,96,768]{2,1,0:T(8,128)(2,1)} %bitcast.346), calls=%async_computation | async-start | bytes 2359296 | tf_op jit(solution)/shard_map/all_to_all | solution.py:651
  266.5 131.5 %all-gather.21.cloned.1.call-start = ((), (), s32[]{:S(2)}) async-start(), calls=%async_computation.10 | async-start | bytes 5898240 | tf_op jit(solution)/shard_map/all_gather | solution.py:662
  296.9 119.9 %all-gather.19.cloned.1.call-start = ((), (), s32[]{:S(2)}) async-start(), calls=%async_computation.9 | async-start | bytes 5898240 | tf_op jit(solution)/shard_map/all_gather | solution.py:662
  365.1 32.9 %all-to-all-start.2 = ((bf16[8,96,768]{2,1,0:T(8,128)(2,1)}), bf16[8,96,768]{2,1,0:T(8,128)(2,1)S(1)}, u32[]{:S(2)}, u32[]{:S(2)}) async-start(bf16[8,96,768]{2,1,0:T(8,128)(2,1)} %select_convert_fusion), calls=%async_computation.2 | async-start | bytes 2359296 | tf_op jit(solution)/shard_map/all_to_all | solution.py:651
  368.7 103.6 %all-gather.29.cloned.1.call-start = ((), (), s32[]{:S(2)}) async-start(), calls=%async_computation.17 | async-start | bytes 3981312 | tf_op jit(solution)/shard_map/all_gather | solution.py:617
  479.8 45.3 %all-to-all-start.3 = ((bf16[8,96,768]{2,1,0:T(8,128)(2,1)}), bf16[8,96,768]{2,1,0:T(8,128)(2,1)}, u32[]{:S(2)}, u32[]{:S(2)}) async-start(bf16[8,96,768]{2,1,0:T(8,128)(2,1)} %bitcast.345), calls=%async_computation.3 | async-start | bytes 2359296 | tf_op jit(solution)/shard_map/all_to_all | solution.py:651
  484.6 110.0 %all-gather.31.cloned.1.call-start = ((), (), s32[]{:S(2)}) async-start(), calls=%async_computation.18 | async-start | bytes 3981312 | tf_op jit(solution)/shard_map/all_gather | solution.py:617
  547.8 124.2 %reduce-scatter.4.cloned.1.call-start = ((), (), s32[]{:S(2)}) async-start(), calls=%async_computation.11 | async-start | bytes 5308416 | tf_op jit(solution)/shard_map/reduce_scatter | solution.py:790
  598.4 130.1 %reduce-scatter.6.cloned.1.call-start = ((), (), s32[]{:S(2)}) async-start(), calls=%async_computation.12 | async-start | bytes 5308416 | tf_op jit(solution)/shard_map/reduce_scatter | solution.py:809
  616.8 50.2 %collective-permute-start.15 = (bf16[768,768]{1,0:T(8,128)(2,1)}, bf16[768,768]{1,0:T(8,128)(2,1)}, u32[]{:S(2)}, u32[]{:S(2)}) collective-permute-start(bf16[768,768]{1,0:T(8,128)(2,1)} %get-tuple-element.230), channel_id=1, source_target_pairs={{0,24},{8,16},{16,8},{24,0},{1,25},{9,17},{17,9},{25,1},{2,26},{10... | collective-permute-start | bytes 3538952 | tf_op jit(solution)/shard_map/ppermute | solution.py:541
  618.1 53.2 %collective-permute-start.14 = (bf16[768,768]{1,0:T(8,128)(2,1)}, bf16[768,768]{1,0:T(8,128)(2,1)}, u32[]{:S(2)}, u32[]{:S(2)}) collective-permute-start(bf16[768,768]{1,0:T(8,128)(2,1)} %get-tuple-element.231), channel_id=1, source_target_pairs={{0,16},{8,24},{16,0},{24,8},{1,17},{9,25},{17,1},{25,9},{2,18},{10... | collective-permute-start | bytes 3538952 | tf_op jit(solution)/shard_map/ppermute | solution.py:541
  619.0 53.1 %collective-permute-start.13 = (bf16[768,768]{1,0:T(8,128)(2,1)}, bf16[768,768]{1,0:T(8,128)(2,1)}, u32[]{:S(2)}, u32[]{:S(2)}) collective-permute-start(bf16[768,768]{1,0:T(8,128)(2,1)} %get-tuple-element.232), channel_id=1, source_target_pairs={{0,8},{8,0},{16,24},{24,16},{1,9},{9,1},{17,25},{25,17},{2,10},{10... | collective-permute-start | bytes 3538952 | tf_op jit(solution)/shard_map/ppermute | solution.py:541
  672.1 93.3 %reduce-scatter.8.cloned.1.call-start = ((), (), s32[]{:S(2)}) async-start(), calls=%async_computation.13 | async-start | bytes 2654208 | tf_op jit(solution)/shard_map/reduce_scatter | solution.py:794
  (110 other events, 1607.0 us)
Sparse Core Ops, SparseCore 0:
  11.4 25.3 all-gather.22
  39.0 31.3 all-gather.14
  72.6 38.1 all-gather.24
  119.5 21.4 all-gather.26
  218.5 42.7 all-gather.16
  297.0 60.8 all-gather.20
  359.7 57.0 all-gather.18
  424.7 41.4 all-gather.28
  548.0 42.4 all-gather.30
  598.5 55.9 reduce-scatter.3
  672.2 56.2 reduce-scatter.5
  730.7 34.6 reduce-scatter.7

commit v3 on v2

--- a/solution.py
+++ b/solution.py
@@ -111,7 +111,7 @@
 
 
 def fwd_kernel(
-    code_ref, me_ref, qt_ref, k_ref, v_ref, gap_ref, far_ref, segc_ref, segr_ref,
+    code_ref, me_ref, qt_ref, kv_ref, gap_ref, far_ref, segc_ref, segr_ref,
     ctxt_ref, ctxb_ref, lse_ref, tile_ref, m_ref, l_ref, acc_ref,
 ):
     fill_tiles(gap_ref, far_ref, tile_ref)
@@ -131,7 +131,8 @@
                 ok = seg_ok(segc_ref, segr_ref, i, j, 128)
             for p in range(PAIRS):
                 cols = slice(128 * p, 128 * p + 128)
-                s = mm(k_ref[keys, cols], pair_diag(qt_ref, p, qoff), 1, 0)
+                vcols = slice(D + 128 * p, D + 128 * p + 128)
+                s = mm(kv_ref[keys, cols], pair_diag(qt_ref, p, qoff), 1, 0)
                 if near:
                     s = jnp.where(ok, s + pair_tiles(tile_ref, p, [off]), NEG)
                 else:
@@ -144,7 +145,7 @@
                 l_ref[p : p + 1, :] = l_ref[p : p + 1, :] * shrink + jnp.sum(
                     w, axis=0, keepdims=True
                 )
-                o = mm(v_ref[keys, cols], w.astype(BF16), 0, 0)
+                o = mm(kv_ref[keys, vcols], w.astype(BF16), 0, 0)
                 o = jnp.concatenate([o[:64, :128], o[64:, 128:]], axis=1)
                 acc_ref[p] = acc_ref[p] * shrink + o
 
@@ -179,7 +180,7 @@
 
 
 def bwd_kernel(
-    code_ref, me_ref, qt_ref, dt_ref, k_ref, v_ref, stat_ref, gap_ref, far_ref, segc_ref, segr_ref,
+    code_ref, me_ref, qt_ref, dt_ref, kv_ref, stat_ref, gap_ref, far_ref, segc_ref, segr_ref,
     dqkv_ref, dgap_ref, dfar_ref,
     tile_ref, near_ref, facc_ref, dq_ref, dk_ref, dv_ref,
 ):
@@ -208,14 +209,15 @@
             ok = seg_ok(segc_ref, segr_ref, i, j, 256)
         for p in range(PAIRS):
             cols = slice(128 * p, 128 * p + 128)
+            vcols = slice(D + 128 * p, D + 128 * p + 128)
             qd, od = pair_diag(qt_ref, p, qoff), pair_diag(dt_ref, p, qoff)
-            s = mm(k_ref[keys, cols], qd, 1, 0)
+            s = mm(kv_ref[keys, cols], qd, 1, 0)
             lse = lanes(0, p, i)
             if near:
                 w = jnp.exp(jnp.where(ok, s + pair_tiles(tile_ref, p, offs) - lse, NEG))
             else:
                 w = jnp.exp(s + (far_ref[p : p + 1, :] - lse))
-            dp = mm(v_ref[keys, cols], od, 1, 0)
+            dp = mm(kv_ref[keys, vcols], od, 1, 0)
             ds = w * (dp - lanes(HEADS, p, i))
             dsb = ds.astype(BF16)
             if by_key:
@@ -223,7 +225,7 @@
                 dk_ref[p, own] += mm(dsb, qd, 1, 1)
             if by_query:
                 qi = i - 2 * me
-                o = mm(k_ref[keys, cols], dsb, 0, 0)
+                o = mm(kv_ref[keys, cols], dsb, 0, 0)
                 dq_ref[qi, p] += jnp.concatenate([o[:64, :128], o[64:, 128:]], axis=1)
                 if near:
                     for n in range(2):
@@ -286,8 +288,8 @@
     return pl.BlockSpec(memory_space=pltpu.SMEM)
 
 
-def attention_forward(code, me, qt, keys, values, gap, far, segc, segr):
-    length = keys.shape[0]
+def attention_forward(code, me, qt, kv, gap, far, segc, segr):
+    length = kv.shape[0]
     return pl.pallas_call(
         fwd_kernel,
         name="attention_forward",
@@ -296,7 +298,7 @@
             jax.ShapeDtypeStruct((ROWS, D), BF16),
             jax.ShapeDtypeStruct((HEADS, ROWS), F32),
         ],
-        in_specs=[smem(), smem()] + [vmem()] * 7,
+        in_specs=[smem(), smem()] + [vmem()] * 6,
         out_specs=[vmem()] * 3,
         scratch_shapes=[
             pltpu.VMEM((HEADS, 128, 512), F32),
@@ -310,11 +312,11 @@
             bytes_accessed=32 * length * D,
             transcendentals=HEADS * ROWS * length // 2,
         ),
-    )(code, me, qt, keys, values, gap, far, segc, segr)
-
-
-def attention_backward(code, me, qt, dt, keys, values, stats, gap, far, segc, segr):
-    length = keys.shape[0]
+    )(code, me, qt, kv, gap, far, segc, segr)
+
+
+def attention_backward(code, me, qt, dt, kv, stats, gap, far, segc, segr):
+    length = kv.shape[0]
     return pl.pallas_call(
         bwd_kernel,
         name="attention_backward",
@@ -323,7 +325,7 @@
             jax.ShapeDtypeStruct((HEADS, 256), F32),
             jax.ShapeDtypeStruct((HEADS, 128), F32),
         ],
-        in_specs=[smem(), smem()] + [vmem()] * 9,
+        in_specs=[smem(), smem()] + [vmem()] * 8,
         out_specs=[vmem()] * 3,
         scratch_shapes=[
             pltpu.VMEM((HEADS, 128, 512), F32),
@@ -339,19 +341,16 @@
             bytes_accessed=64 * length * D,
             transcendentals=HEADS * ROWS * length,
         ),
-    )(code, me, qt, dt, keys, values, stats, gap, far, segc, segr)
-
-
-def ffn_kernel(x_ref, gain_ref, own_ref, peer_ref, other_ref, out_ref, norm_ref, hidden_ref, slope_ref):
+    )(code, me, qt, dt, kv, stats, gap, far, segc, segr)
+
+
+def ffn_kernel(x_ref, gain_ref, *refs):
+    weights, (out_ref, norm_ref, hidden_ref, slope_ref) = refs[:-4], refs[-4:]
     x = x_ref[...]
     normed = norm_rows(x, gain_ref[...]).astype(BF16)
     norm_ref[...] = normed
     total = x
-    piece = own_ref.shape[2] // 2
-    peers = peer_ref.shape[0]
-    weights = [own_ref.at[0], own_ref.at[1]]
-    for k in range(peers):
-        weights += [peer_ref.at[k], other_ref.at[k]]
+    piece = weights[0].shape[1] // 2
     for n, ref in enumerate(weights):
         at = slice(n * piece, n * piece + piece)
         hidden, slope = gelu_pair(mm(normed, ref[:, :piece], 1, 0))
@@ -362,13 +361,13 @@
     out_ref[...] = total
 
 
-def ffn_forward(x, gain, own, peers, others):
+def ffn_forward(x, gain, pieces):
     count = x.shape[0]
-    width = own.shape[2] // 2 * (2 + 2 * peers.shape[0])
+    width = sum(w.shape[1] // 2 for w in pieces)
     return pl.pallas_call(
         ffn_kernel,
         name="ffn_forward",
-        in_specs=[vmem()] * 5,
+        in_specs=[vmem()] * (2 + len(pieces)),
         out_specs=[vmem()] * 4,
         out_shape=[
             jax.ShapeDtypeStruct((count, D), F32),
@@ -380,7 +379,7 @@
         cost_estimate=pl.CostEstimate(
             flops=4 * count * D * width, bytes_accessed=8 * D * width, transcendentals=count * width
         ),
-    )(x, gain[None, :], own, peers, others)
+    )(x, gain[None, :], *pieces)
 
 
 def gelu_pair(u):
@@ -469,10 +468,12 @@
 def expert_gradients(rows, dye, w_in, w_out, part, earlier):
     count, total, _ = rows.shape
     width, block = w_in.shape[2], 512
-    steps = width // block // 2
+    blocks = width // block
+    edges = (0, blocks // 2, blocks - blocks // 6, blocks)
+    first, steps = edges[part], edges[part + 1] - edges[part]
     whole = pl.BlockSpec((1, total, D), lambda e, i: (e, 0, 0))
-    by_in = pl.BlockSpec((1, D, block), lambda e, i: (e, 0, i + part * steps))
-    by_out = pl.BlockSpec((1, block, D), lambda e, i: (e, i + part * steps, 0))
+    by_in = pl.BlockSpec((1, D, block), lambda e, i: (e, 0, i + first))
+    by_out = pl.BlockSpec((1, block, D), lambda e, i: (e, i + first, 0))
     return pl.pallas_call(
         expert_kernel,
         name=f"expert_gradients_{part}",
@@ -486,9 +487,9 @@
         input_output_aliases={4 + n: n for n in range(len(earlier))},
         compiler_params=pltpu.CompilerParams(vmem_limit_bytes=VMEM_LIMIT),
         cost_estimate=pl.CostEstimate(
-            flops=4 * count * total * D * width,
-            bytes_accessed=32 * count * D * width,
-            transcendentals=count * total * width // 2,
+            flops=8 * count * total * D * block * steps,
+            bytes_accessed=64 * count * D * block * steps,
+            transcendentals=count * total * block * steps,
         ),
     )(rows, dye, w_in, w_out, *earlier)
 
@@ -578,18 +579,20 @@
     piece = span // 2
     ffn_own = [lax.dynamic_slice_in_dim(w, mine * span, span, 1) for w in (ffn_in, ffn_out)]
     ffn_own = jnp.concatenate([w[:, h * piece : h * piece + piece] for h in range(2) for w in ffn_own], axis=1)
+    seg_row = jnp.pad(segments.astype(BF16), ((0, 7), (0, ffn_own.shape[1] - rows)))
+    ffn_own = jnp.concatenate([ffn_own, seg_row], axis=0)
     ffn_own, quarter_first = lax.optimization_barrier((ffn_own, quarter_first))
-    ffn_quarter = gather(ffn_own)
-    seg_row = jnp.pad(segments.astype(BF16), ((0, 7), (0, D - rows)))
-    tokens_own = jnp.concatenate([tokens[0], seg_row], axis=0)
-    tokens_own, ffn_quarter = lax.optimization_barrier((tokens_own, ffn_quarter))
-    tokens_all = lax.all_gather(tokens_own, "grp", axis=0)
-    ffn_mine = [lax.dynamic_slice_in_dim(ffn_quarter, n * span, span, 1) for n in (core, 1 - core)]
+    ffn_quarter = lax.all_gather(ffn_own, "grp", axis=0)
+    seg_all = ffn_quarter[:, ffn_in.shape[0], :rows].astype(jnp.int32).reshape(-1)
+    tokens_own, ffn_quarter = lax.optimization_barrier((tokens[0], ffn_quarter))
+    x_all = gather(tokens_own)
+    ffn_mine = [
+        lax.dynamic_slice(ffn_quarter, (0, 0, n * span), (groups, ffn_in.shape[0], span)).reshape(-1, span)
+        for n in (core, 1 - core)
+    ]
     ffn_peers = [from_replica(ffn_mine[0], k) for k in range(1, replicas)]
 
-    quarter_second = layer_quarter(1, tokens_all)
-    x_all = tokens_all[:, :rows].reshape(-1, D)
-    seg_all = tokens_all[:, rows, :rows].astype(jnp.int32).reshape(-1)
+    quarter_second = layer_quarter(1, x_all)
     code = block_codes(seg_all, block_sets[0])
     shared = (seg_all[:, None], seg_all.reshape(-1, BLK))
     w_qkv, w_out = [w_first[0]], [w_first[1]]
@@ -597,16 +600,15 @@
     def attend(residual, normed, normed_all, layer):
         w = w_qkv[layer]
         qt = mm(w[:, :D], normed, 0, 1).astype(BF16) * jnp.asarray(0.125, BF16)
-        keys = mm(normed_all, w[:, D : 2 * D], 1, 0).astype(BF16)
-        values = mm(normed_all, w[:, 2 * D :], 1, 0).astype(BF16)
+        kv = mm(normed_all, w[:, D:], 1, 0).astype(BF16)
         gap, far = bias_inputs(rel_bias[layer])
-        ctxt, ctxb, lse = attention_forward(code, me, qt, keys, values, gap, far, *shared)
+        ctxt, ctxb, lse = attention_forward(code, me, qt, kv, gap, far, *shared)
         branch = mm(ctxb, w_out[layer], 1, 0)
-        saved = (residual, normed, normed_all, keys, values, ctxt, ctxb, lse, gap, far)
+        saved = (residual, normed, normed_all, kv, ctxt, ctxb, lse, gap, far)
         return residual + branch, saved
 
     def attend_back(grad_out, saved, layer, qt_all, held, cover):
-        residual, normed, normed_all, keys, values, ctxt, ctxb, lse, gap, far = saved
+        residual, normed, normed_all, kv, ctxt, ctxb, lse, gap, far = saved
         w, wo = w_qkv[layer], w_out[layer]
         grad_low = grad_out.astype(BF16)
         dctx_own = mm(wo, grad_low, 1, 1).astype(BF16)
@@ -621,9 +623,9 @@
         dt_all = mm(wo, grad_all, 1, 1).astype(BF16)
         dt_all, held = lax.optimization_barrier((dt_all, held))
         dqkv, dgap, dfar = attention_backward(
-            code, me, qt_all, dt_all, keys, values, stats_all, gap, far, *shared
+            code, me, qt_all, dt_all, kv, stats_all, gap, far, *shared
         )
-        out_part = mm(ctxb, grad_low, 0, 0)
+        out_part = mm(ctxb, grad_low, 0, 0) if layer else None
         qkv_part = mm(normed, dqkv, 0, 0)
         normed_grad = mm(dqkv, w, 1, 1)
         _, pull_back = jax.vjp(norm_rows, residual, norm_gains[layer, 0])
@@ -661,6 +663,9 @@
     def all_replicas(x):
         return lax.all_gather(x, "rep", axis=1, tiled=True)
 
+    x_all, cot_own = lax.optimization_barrier((x_all, cotangent[0]))
+    cot_rows = by_expert(exchange(mm(both, cot_own, 0, 0).astype(BF16)))
+
     stream = tokens[0].astype(F32)
     own_a = norm_rows(stream, norm_gains[0, 0]).astype(BF16)
     all_a = norm_rows(x_all.astype(F32), norm_gains[0, 0]).astype(BF16)
@@ -668,26 +673,23 @@
     first_out, quarter_second, ffn_peers = lax.optimization_barrier(
         (first_out, quarter_second, ffn_peers)
     )
-    ffn_peers = jnp.stack(ffn_peers)
-    ffn_others = from_sibling(ffn_peers)
-    after_ffn, normed_ffn, hidden_ffn, slope_ffn = ffn_forward(
-        first_out, norm_gains[0, 1], jnp.stack(ffn_mine), ffn_peers, ffn_others
-    )
-
+    ffn_others = [from_sibling(x) for x in ffn_peers]
+    pieces = ffn_mine + [x for pair in zip(ffn_peers, ffn_others) for x in pair]
+    after_ffn, normed_ffn, hidden_ffn, slope_ffn = ffn_forward(first_out, norm_gains[0, 1], pieces)
+    after_ffn, cot_rows = lax.optimization_barrier((after_ffn, cot_rows))
+
+    own_b = norm_rows(after_ffn, norm_gains[1, 0]).astype(BF16)
+    own_b, quarter_second = lax.optimization_barrier((own_b, quarter_second))
     w_second = layer_weights(quarter_second)
     w_qkv.append(w_second[0])
     w_out.append(w_second[1])
-    own_b = norm_rows(after_ffn, norm_gains[1, 0]).astype(BF16)
-    pieces = ffn_mine + [x[k] for k in range(replicas - 1) for x in (ffn_peers, ffn_others)]
     full_in = jnp.concatenate([x[:, :piece] for x in pieces], axis=1)
     full_down = jnp.concatenate([x[:, piece:] for x in pieces], axis=1)
-    all_b, cot_own, full_in, full_down = lax.optimization_barrier(
-        (gather(own_b), cotangent[0], full_in, full_down)
-    )
-    cot_rows = by_expert(exchange(mm(both, cot_own, 0, 0).astype(BF16)))
+    all_b, cot_rows, full_in, full_down = lax.optimization_barrier(
+        (gather(own_b), cot_rows, full_in, full_down)
+    )
+    cot_all = all_replicas(cot_rows)
     second_out, saved_b = attend(after_ffn, own_b, all_b, 1)
-    second_out, cot_rows = lax.optimization_barrier((second_out, cot_rows))
-    cot_all = all_replicas(cot_rows)
     normed_moe = norm_rows(second_out, norm_gains[1, 1]).astype(BF16)
     normed_wide = normed_moe.astype(F32)
     router_wide = router.astype(F32)
@@ -727,8 +729,11 @@
         mm(w_qkv[n][:, :D], all_rows, 0, 1).astype(BF16) * jnp.asarray(0.125, BF16)
         for n, all_rows in enumerate((all_a, all_b))
     ]
-    back_grad, rows_all, cot_all, queries_all = lax.optimization_barrier(
-        (exchange(by_source(rows_grad)), all_replicas(rows_e), cot_all, queries_all)
+    rows_e, cot_all = lax.optimization_barrier((rows_e, cot_all))
+    rows_all = all_replicas(rows_e)
+    dye_all = gated(rows_all, cot_all)
+    back_grad, queries_all, dye_all = lax.optimization_barrier(
+        (exchange(by_source(rows_grad)), queries_all, dye_all)
     )
     back_slots = scalars_of(back_grad.reshape(experts_all, slots, D)).reshape(1, -1)
     back_grad = back_grad.reshape(experts_all * slots, D)
@@ -748,7 +753,6 @@
         picked = [mm(pick[k], returned, 1, 0) for k in range(2)]
         return second_out + gate_probs[:, 0:1] * picked[0] + gate_probs[:, 1:2] * picked[1]
 
-    dye_all = gated(rows_all, cot_all)
 
     def expert_half(part, earlier):
         def run(sent):
@@ -784,16 +788,15 @@
     ffn_got = [from_replica(ffn_parts[k], k) for k in range(1, replicas)]
     back_a = attend_back(grad_first, saved_a, 0, queries_all[0], (), expert_half(1, expert_sums))
     grad_tokens, qkv_part_a, out_part_a, gain_grad_a, table_grad_a, grad_all_a, _, expert_sums = back_a
-    expert_in_sum, expert_out_sum = expert_sums
-    parts_b, _ = lax.optimization_barrier((packed([qkv_part_b, out_part_b]), grad_all_a))
-    parts_a = packed([qkv_part_a, out_part_a])
+    out_part_a = mm(saved_a[5], grad_first.astype(BF16), 0, 0)
+    parts_b, _ = lax.optimization_barrier((packed([qkv_part_b, out_part_b, out_part_a]), grad_all_a))
+    parts_a = qkv_part_a.astype(BF16)
     shard_b = lax.psum_scatter(parts_b, "grp", scatter_dimension=0, tiled=True)
     parts_a, shard_b, ffn_got = lax.optimization_barrier((parts_a, shard_b, ffn_got))
-
-    def scatter(x):
-        return lax.psum_scatter(x, "grp", scatter_dimension=0, tiled=True)
-
-    def over_replicas(x, cut):
+    shard_a = lax.psum_scatter(parts_a, "grp", scatter_dimension=0, tiled=True)
+    expert_in_sum, expert_out_sum = expert_half(2, expert_sums)(parts_a)
+
+    def over_replicas(x):
         half = x.shape[0] // 2
 
         def add(v, mask):
@@ -803,25 +806,38 @@
         top, low = x[:half], x[half:]
         for a, b in zip(first, first[::-1]):
             top, low = add(top, a), add(low, b)
-        x = jnp.concatenate([top, low], axis=0).astype(F32)
-        return x[:, :cut], x[:, cut:]
-
-    shard_a = lax.psum_scatter(parts_a, "grp", scatter_dimension=0, tiled=True)
+        return jnp.concatenate([top, low], axis=0).astype(F32)
+
     ffn_total = ffn_parts[0].astype(F32)
     for x in ffn_got:
         ffn_total = ffn_total + x.astype(F32)
-    down_half, in_half = ffn_total[:, :piece], ffn_total[:, piece:]
-    ffn_total = jnp.concatenate(
-        [jnp.where(core == h, x, 0.0) for x in (in_half, down_half) for h in range(2)], axis=1
-    )
-    shard_a, ffn_total = lax.optimization_barrier((shard_a, ffn_total.astype(BF16)))
-    ffn_shard = scatter(ffn_total)
-    ffn_sums = jnp.stack([ffn_shard] + [from_replica(ffn_shard, k) for k in range(1, replicas)])
-    ffn_sums = [lax.dynamic_index_in_dim(ffn_sums, mine ^ q, 0, False).astype(F32) for q in range(replicas)]
+    ffn_total = ffn_total.astype(BF16)
+    shard_a, ffn_total = lax.optimization_barrier((shard_a, ffn_total))
+    same_core = [list(range(c, groups, 2)) for c in range(2)]
+    band = lax.psum_scatter(
+        ffn_total, "grp", scatter_dimension=0, tiled=True, axis_index_groups=same_core
+    )
+    band = band.reshape(2, -1, band.shape[1])
+    kept = lax.dynamic_index_in_dim(band, core, 0, False)
+    other = from_sibling(lax.dynamic_index_in_dim(band, 1 - core, 0, False))
+    low, high = jnp.where(core == 0, kept, other), jnp.where(core == 0, other, kept)
+    ffn_shard = jnp.concatenate([low[:, piece:], high[:, piece:], low[:, :piece], high[:, :piece]], axis=1)
+    ffn_peers = [ffn_shard] + [from_replica(ffn_shard, k) for k in range(1, replicas)]
+
+    def quarter_of(q):
+        x = ffn_peers[0]
+        for k in range(1, replicas):
+            x = jnp.where(mine ^ k == q, ffn_peers[k], x)
+        return x.astype(F32)
+
+    ffn_sums = [quarter_of(q) for q in range(replicas)]
     in_sum = jnp.concatenate([x[:, :span] for x in ffn_sums], axis=1)
     down_sum = jnp.concatenate([x[:, span:] for x in ffn_sums], axis=1)
-    qkv_b, out_b = over_replicas(shard_b, 3 * D)
-    qkv_a, out_a = over_replicas(shard_a, 3 * D)
+    total_b = shard_b.astype(F32)
+    for k in range(1, replicas):
+        total_b = total_b + from_replica(shard_b, k).astype(F32)
+    qkv_b, out_b, out_a = total_b[:, : 3 * D], total_b[:, 3 * D : 4 * D], total_b[:, 4 * D :]
+    qkv_a = over_replicas(shard_a)
     qkv_sum = jnp.stack([qkv_a, qkv_b], axis=1).reshape(qkv_weight.shape)
     out_sum = jnp.stack([out_a, out_b], axis=1)
     gain_all = jnp.stack(

time: 800 us -> 714 us (0.89)
  waiting for transfers between devices: 222 us -> 172 us
  other arithmetic: 89.2 us -> 57 us
  blocking collectives: 35.6 us -> 50 us
  local copies, waits for them, and re-layouts: 87.1 us -> 75.9 us
  matrix products: 104 us -> 93.7 us
  Pallas kernels: 191 us -> 199 us
    all_gather x1, waiting for transfers between devices: 23.3 us -> 0.01 us  [body(): gather(own_b)]
    all_to_all x3, waiting for transfers between devices: 22.1 us -> 2.91 us  [exchange(): lax.all_to_all(x.reshape(groups, per_group * slots, D), 'grp', split_axis...]
    all_to_all x1, blocking collectives: 35.6 us -> 50 us  [exchange(): lax.all_to_all(x.reshape(groups, per_group * slots, D), 'grp', split_axis...]
    reduce_scatter x1, waiting for transfers between devices: 17.6 us -> 5.66 us  [body(): lax.psum_scatter(ffn_total, 'grp', scatter_dimension=0, tiled=True, axis_...]
    all_gather x2, waiting for transfers between devices: 18.8 us -> 7.31 us  [all_replicas(): return lax.all_gather(x, 'rep', axis=1, tiled=True)]
    ppermute x23 -> x22, waiting for transfers between devices: 38.9 us -> 49.6 us  [from_replica(): return lax.ppermute(x, 'rep', [(i, i ^ k) for i in range(replicas)])]
    another operation x6 -> x2, other arithmetic: 9.3 us -> 0.76 us  [the longest x1 3.25 us: body(): ffn_peers = jnp.stack(ffn_peers)]
    dot_general x30 -> x28, matrix products: 96.5 us -> 88.7 us  [mm(): lax.dot_general(a, b, (((ca,), (cb,)), ((), ())), preferred_element_type=...]
  transfers between devices with their start and end apart: 47 -> 49, of which waited for: 28 -> 27; matrix products, arithmetic and copies ran while one was open for 27% -> 24% of each run, Pallas kernels for 24% -> 28%
where the time goes in v3:
time: 714 us; the launch traced here: 710 us
  Pallas kernels  199 us (28%)
  waiting for transfers between devices  172 us (24%)
  matrix products  93.7 us (13%)
  local copies, waits for them, and re-layouts  75.9 us (11%)
  other arithmetic  57 us (8%)
  blocking collectives  50 us (7%)
  starting transfers between devices  45.2 us (6%)
  between operations  16.9 us (2%)
    dot_general x28, matrix products, mm(): lax.dot_general(a, b, (((ca,), (cb,)), ((), ())), preferred_element_type=...  88.7 us
    pallas_call x3, Pallas kernels, expert_gradients(): pl.pallas_call(expert_kernel, name=f'expert_gradients_{part}', grid=(coun...  87.4 us
    pallas_call x2, Pallas kernels, attention_backward(): pl.pallas_call(bwd_kernel, name='attention_backward', out_shape=[jax.Shap...  62.6 us
    all_to_all x1, blocking collectives, exchange(): lax.all_to_all(x.reshape(groups, per_group * slots, D), 'grp', split_axis...  50 us
    ppermute x22, waiting for transfers between devices, from_replica(): return lax.ppermute(x, 'rep', [(i, i ^ k) for i in range(replicas)])  49.6 us
    unnamed x248, local copies, waits for them, and re-layouts  30.8 us
    all_gather x1, waiting for transfers between devices, body(): ffn_quarter = lax.all_gather(ffn_own, 'grp', axis=0)  27.4 us
    all_gather x2, waiting for transfers between devices, layer_quarter(): return lax.all_gather(part, 'grp', axis=0)  26.8 us
  transfers between devices with their start and end apart: 49, of which 27 were waited for; matrix products, arithmetic and copies ran while one was open for 24% of the time, Pallas kernels for 28%

profile of v3, /device:TPU:0, one launch (start us, length us, event | category | flops | bytes accessed | tf_op | source)
XLA Modules:
  0.0 709.8 jit_solution(14546084532239851848)
XLA Ops:
  13.8 23.0 %all-gather.23.cloned.1.call-done = bf16[192,3072]{1,0:T(8,128)(2,1)} async-done(((bf16[24,3072]{1,0:T(8,128)(2,1)}), bf16[192,3072]{1,0:T(8,128)(2,1)}) %all-gather.23.cloned.1.call-update) | async-done | bytes 1179664 | tf_op jit(solution)/shard_map/all_gather | solution.py:560
  44.7 27.4 %all-gather.25.cloned.1.call-done = bf16[832,1536]{1,0:T(8,128)(2,1)} async-done(((bf16[104,1536]{1,0:T(8,128)(2,1)}), bf16[832,1536]{1,0:T(8,128)(2,1)}) %all-gather.25.cloned.1.call-update) | async-done | bytes 2555920 | tf_op jit(solution)/shard_map/all_gather | solution.py:585
  90.7 20.4 %all-gather.15.cloned.1.call-done = bf16[2048,768]{1,0:T(8,128)(2,1)} async-done(((bf16[256,768]{1,0:T(8,128)(2,1)}), bf16[2048,768]{1,0:T(8,128)(2,1)}) %all-gather.15.cloned.1.call-update) | async-done | bytes 3145744 | tf_op jit(solution)/shard_map/all_gather | solution.py:588
  119.6 8.7 %convolution_convert_fusion.1.kv_ref = bf16[2048,1536]{1,0:T(8,128)(2,1)} fusion(bf16[768,3072]{1,0:T(8,128)(2,1)} %bitcast.275, bf16[2048,768]{1,0:T(8,128)(2,1)S(1)} %copy-done.26, f32[768]{0:T(1024)S(1)} %get-tuple-element.221, f32[2048]{0:T(1024)S(1)} %add_rsqrt_fusion), kind=kOutput, calls=%fused_computation.4 | convolution fusion | flops 4841275392 | bytes 11807744 | tf_op jit(solution)/shard_map/dot_general | solution.py:29
  128.3 6.8 attention_forward.2
  150.6 11.0 %ffn_forward.1 = (f32[256,768]{1,0:T(8,128)}, bf16[256,768]{1,0:T(8,128)(2,1)}, bf16[256,3072]{1,0:T(8,128)(2,1)}, f32[256,3072]{1,0:T(8,128)}) custom-call(f32[256,768]{1,0:T(8,128)} %convert_add_fusion.4.x_ref, f32[1,768]{1,0:T(1,128)} %get-tuple-element.305.gain_ref, bf16[768,768]{1,0:T(8,128)(2,1)} %bitcast.272, bf16[768,768]{1,0:T(8,128)(2,1)} %bitcast.267, ...), custom_call_target="tpu_custom_call" | custom-call | flops 2415919104 | bytes 18874368 | tf_op jit(solution)/shard_map/ffn_forward/pallas_call | solution.py:367
  184.5 6.2 collective-permute-done.12
  190.6 11.9 %collective-permute-done.11 = bf16[8,24,1536]{2,1,0:T(8,128)(2,1)S(1)} collective-permute-done((bf16[8,24,1536]{2,1,0:T(8,128)(2,1)S(1)}, bf16[8,24,1536]{2,1,0:T(8,128)(2,1)S(1)}, u32[]{:S(2)}, u32[]{:S(2)}) %collective-permute-start.11) | collective-permute-done | bytes 589856 | tf_op jit(solution)/shard_map/ppermute | solution.py:542
  219.8 8.6 %convolution_convert_fusion.kv_ref = bf16[2048,1536]{1,0:T(8,128)(2,1)} fusion(bf16[2048,768]{1,0:T(8,128)(2,1)S(1)} %copy-done.106, bf16[768,3072]{1,0:T(8,128)(2,1)} %bitcast.50), kind=kOutput, calls=%fused_computation.3 | convolution fusion | flops 4834983936 | bytes 11796480 | tf_op jit(solution)/shard_map/dot_general | solution.py:29
  228.4 7.3 %attention_forward.3 = (f32[768,256]{1,0:T(8,128)}, bf16[256,768]{1,0:T(8,128)(2,1)}, f32[12,256]{1,0:T(8,128)}) custom-call(s32[16,16]{1,0:T(8,128)} %select_select_fusion.code_ref, s32[1]{0:T(128)} %bitcast.7.me_ref, bf16[768,256]{1,0:T(8,128)(2,1)} %fusion.22.qt_ref, bf16[2048,1536]{1,0:T(8,128)(2,1)} %convolution_convert_fusion.kv_ref, ...), custom_call_target="tpu_custom_call" | custom-call | flops 3221225472 | bytes 50331648 | tf_op jit(solution)/shard_map/attention_forward/pallas_call | solution.py:293
  240.7 50.0 %all_to_all.20 = bf16[8,96,768]{2,1,0:T(8,128)(2,1)} all-to-all(bf16[8,96,768]{2,1,0:T(8,128)(2,1)S(1)} %select_convert_fusion.1), channel_id=1, replica_groups=mesh['rep'=4,'grp'=8] {'grp'}, dimensions={0} | all-to-all | bytes 2359296 | tf_op jit(solution)/shard_map/all_to_all | solution.py:653
  293.8 24.0 %expert_rows.1 = (bf16[1,768,768]{2,1,0:T(8,128)(2,1)}, f32[1,768,768]{2,1,0:T(8,128)}, f32[1,768,128]{2,1,0:T(8,128)}) custom-call(bf16[1,768,768]{2,1,0:T(8,128)(2,1)} %bitcast.286, bf16[1,768,768]{2,1,0:T(8,128)(2,1)} %multiply_convert_fusion.2.dye_ref, bf16[1,768,768]{2,1,0:T(8,128)(2,1)} %bitcast.282, bf16[1,768,3072]{2,1,0:T(8,128)(2,1)} %win_ref.7, ...), custom_call_target="tpu_custom_call" | custom-call | flops 14495514624 | bytes 37748736 | tf_op jit(solution)/shard_map/expert_rows/pallas_call | solution.py:422
  325.8 7.1 fusion.7.qt_ref
  338.2 7.3 %all-gather.21.cloned.1.call-done.rows_ref = bf16[1,3072,768]{2,1,0:T(8,128)(2,1)} async-done(((bf16[1,768,768]{2,1,0:T(8,128)(2,1)}), bf16[1,3072,768]{2,1,0:T(8,128)(2,1)}) %all-gather.21.cloned.1.call-update) | async-done | bytes 4718608 | tf_op jit(solution)/shard_map/all_gather | solution.py:664
  361.6 40.9 %expert_gradients_0.1 = (f32[1,768,3072]{2,1,0:T(8,128)}, f32[1,3072,768]{2,1,0:T(8,128)}) custom-call(bf16[1,3072,768]{2,1,0:T(8,128)(2,1)} %all-gather.21.cloned.1.call-done.rows_ref, bf16[1,3072,768]{2,1,0:T(8,128)(2,1)} %multiply_convert_fusion.dye_ref, bf16[1,768,3072]{2,1,0:T(8,128)(2,1)} %win_ref.7, bf16[1,3072,768]{2,1,0:T(8,128)(2,1)} %wout_ref.7), custom_call_target="tpu_custom_call" | custom-call | flops 28991029248 | bytes 75497472 | tf_op jit(solution)/shard_map/expert_gradients_0/pallas_call | solution.py:477
  419.9 31.3 %attention_backward.2 = (bf16[256,2304]{1,0:T(8,128)(2,1)}, f32[12,256]{1,0:T(8,128)}, f32[12,128]{1,0:T(8,128)}) custom-call(s32[16,16]{1,0:T(8,128)} %select_select_fusion.code_ref, s32[1]{0:T(128)} %bitcast.7.me_ref, bf16[768,2048]{1,0:T(8,128)(2,1)} %fusion.8.qt_ref, bf16[768,2048]{1,0:T(8,128)(2,1)} %convolution_convert_fusion.7.dt_ref, ...), custom_call_target="tpu_custom_call" | custom-call | flops 5637144576 | bytes 100663296 | tf_op jit(solution)/shard_map/attention_backward/pallas_call | solution.py:320
  484.7 29.2 %expert_gradients_1.1 = (f32[1,768,3072]{2,1,0:T(8,128)}, f32[1,3072,768]{2,1,0:T(8,128)}) custom-call(bf16[1,3072,768]{2,1,0:T(8,128)(2,1)} %all-gather.21.cloned.1.call-done.rows_ref, bf16[1,3072,768]{2,1,0:T(8,128)(2,1)} %multiply_convert_fusion.dye_ref, bf16[1,768,3072]{2,1,0:T(8,128)(2,1)} %win_ref.7, ...), custom_call_target="tpu_custom_call", output_to_operand_aliasing={{0}: (4, {}), {1}: (5, {})} | custom-call | flops 19327352832 | bytes 50331648 | tf_op jit(solution)/shard_map/expert_gradients_1/pallas_call | solution.py:477
  513.9 5.7 all-gather.31.cloned.1.call-done
  530.7 7.7 %collective-permute-done.14 = bf16[4,768,768]{2,1,0:T(8,128)(2,1)S(1)} collective-permute-done((bf16[4,768,768]{2,1,0:T(8,128)(2,1)S(1)}, bf16[4,768,768]{2,1,0:T(8,128)(2,1)S(1)}, u32[]{:S(2)}, u32[]{:S(2)}) %collective-permute-start.14) | collective-permute-done | bytes 4718624 | tf_op jit(solution)/shard_map/ppermute | solution.py:545
  553.5 31.3 %attention_backward.3 = (bf16[256,2304]{1,0:T(8,128)(2,1)}, f32[12,256]{1,0:T(8,128)}, f32[12,128]{1,0:T(8,128)}) custom-call(s32[16,16]{1,0:T(8,128)} %select_select_fusion.code_ref, s32[1]{0:T(128)} %bitcast.7.me_ref, bf16[768,2048]{1,0:T(8,128)(2,1)} %fusion.7.qt_ref, bf16[768,2048]{1,0:T(8,128)(2,1)} %convolution_convert_fusion.6.dt_ref, ...), custom_call_target="tpu_custom_call" | custom-call | flops 5637144576 | bytes 100663296 | tf_op jit(solution)/shard_map/attention_backward/pallas_call | solution.py:320
  589.1 7.7 %collective-permute-done.16 = bf16[768,768]{1,0:T(8,128)(2,1)} collective-permute-done((bf16[768,768]{1,0:T(8,128)(2,1)}, bf16[768,768]{1,0:T(8,128)(2,1)}, u32[]{:S(2)}, u32[]{:S(2)}) %collective-permute-start.16) | collective-permute-done | bytes 1179680 | tf_op jit(solution)/shard_map/ppermute | solution.py:542
  630.1 17.4 %expert_gradients_2.1 = (f32[1,768,3072]{2,1,0:T(8,128)}, f32[1,3072,768]{2,1,0:T(8,128)}) custom-call(bf16[1,3072,768]{2,1,0:T(8,128)(2,1)} %all-gather.21.cloned.1.call-done.rows_ref, bf16[1,3072,768]{2,1,0:T(8,128)(2,1)} %multiply_convert_fusion.dye_ref, bf16[1,768,3072]{2,1,0:T(8,128)(2,1)} %win_ref.7, ...), custom_call_target="tpu_custom_call", output_to_operand_aliasing={{0}: (4, {}), {1}: (5, {})} | custom-call | flops 9663676416 | bytes 25165824 | tf_op jit(solution)/shard_map/expert_gradients_2/pallas_call | solution.py:477
  655.2 6.4 collective-permute-done.23
  692.9 6.7 collective-permute-done.27
  (564 shorter events, 289.2 us)
Async XLA Ops:
  7.2 29.6 %all-gather.23.cloned.1.call-start = ((), (), s32[]{:S(2)}) async-start(), calls=%async_computation.14 | async-start | bytes 1327104 | tf_op jit(solution)/shard_map/all_gather | solution.py:560
  11.3 60.8 %all-gather.25.cloned.1.call-start = ((), (), s32[]{:S(2)}) async-start(), calls=%async_computation.15 | async-start | bytes 2875392 | tf_op jit(solution)/shard_map/all_gather | solution.py:585
  36.8 74.3 %all-gather.15.cloned.1.call-start = ((), (), s32[]{:S(2)}) async-start(), calls=%async_computation.7 | async-start | bytes 3538944 | tf_op jit(solution)/shard_map/all_gather | solution.py:588
  40.9 31.3 %collective-permute-start.2 = (bf16[8,24,1536]{2,1,0:T(8,128)(2,1)S(1)}, bf16[8,24,1536]{2,1,0:T(8,128)(2,1)S(1)}, u32[]{:S(2)}, u32[]{:S(2)}) collective-permute-start(bf16[8,24,1536]{2,1,0:T(8,128)(2,1)S(1)} %constant_dynamic-slice_fusion.6), channel_id=1, source_target_pairs={{0,24},{8,16},{16,8},{24,0},{1,25},{9,17},{17,9},{25,1},{2,26},{10... | collective-permute-start | bytes 1769480 | tf_op jit(solution)/shard_map/ppermute | solution.py:542
  72.1 71.0 %all-gather.27.cloned.1.call-start = ((), (), s32[]{:S(2)}) async-start(), calls=%async_computation.16 | async-start | bytes 1327104 | tf_op jit(solution)/shard_map/all_gather | solution.py:560
  84.9 52.9 %collective-permute-start.6 = (bf16[768,768]{1,0:T(8,128)(2,1)S(1)}, bf16[768,768]{1,0:T(8,128)(2,1)}, u32[]{:S(2)}, u32[]{:S(2)}) collective-permute-start(bf16[768,768]{1,0:T(8,128)(2,1)S(1)} %bitcast.269), channel_id=1, source_target_pairs={{0,24},{8,16},{16,8},{24,0},{1,25},{9,17},{17,9},{25,1},{2,26},{10... | collective-permute-start | bytes 3538952 | tf_op jit(solution)/shard_map/ppermute | solution.py:542
  87.1 52.2 %collective-permute-start.5 = (bf16[768,768]{1,0:T(8,128)(2,1)S(1)}, bf16[768,768]{1,0:T(8,128)(2,1)}, u32[]{:S(2)}, u32[]{:S(2)}) collective-permute-start(bf16[768,768]{1,0:T(8,128)(2,1)S(1)} %bitcast.270), channel_id=1, source_target_pairs={{0,16},{8,24},{16,0},{24,8},{1,17},{9,25},{17,1},{25,9},{2,18},{10... | collective-permute-start | bytes 3538952 | tf_op jit(solution)/shard_map/ppermute | solution.py:542
  87.7 51.7 %collective-permute-start.4 = (bf16[768,768]{1,0:T(8,128)(2,1)S(1)}, bf16[768,768]{1,0:T(8,128)(2,1)}, u32[]{:S(2)}, u32[]{:S(2)}) collective-permute-start(bf16[768,768]{1,0:T(8,128)(2,1)S(1)} %bitcast.271), channel_id=1, source_target_pairs={{0,8},{8,0},{16,24},{24,16},{1,9},{9,1},{17,25},{25,17},{2,10},{10... | collective-permute-start | bytes 3538952 | tf_op jit(solution)/shard_map/ppermute | solution.py:542
  112.9 48.7 %all-to-all-start = ((bf16[8,96,768]{2,1,0:T(8,128)(2,1)}), bf16[8,96,768]{2,1,0:T(8,128)(2,1)S(1)}, u32[]{:S(2)}, u32[]{:S(2)}) async-start(bf16[8,96,768]{2,1,0:T(8,128)(2,1)} %bitcast.312), calls=%async_computation | async-start | bytes 2359296 | tf_op jit(solution)/shard_map/all_to_all | solution.py:653
  116.4 99.0 %all-gather.17.cloned.1.call-start = ((), (), s32[]{:S(2)}) async-start(), calls=%async_computation.8 | async-start | bytes 3538944 | tf_op jit(solution)/shard_map/all_gather | solution.py:689
  166.5 124.3 %all-gather.19.cloned.1.call-start = ((), (), s32[]{:S(2)}) async-start(), calls=%async_computation.9 | async-start | bytes 5898240 | tf_op jit(solution)/shard_map/all_gather | solution.py:664
  215.4 130.1 %all-gather.21.cloned.1.call-start = ((), (), s32[]{:S(2)}) async-start(), calls=%async_computation.10 | async-start | bytes 5898240 | tf_op jit(solution)/shard_map/all_gather | solution.py:664
  322.2 32.9 %all-to-all-start.2 = ((bf16[8,96,768]{2,1,0:T(8,128)(2,1)}), bf16[8,96,768]{2,1,0:T(8,128)(2,1)S(1)}, u32[]{:S(2)}, u32[]{:S(2)}) async-start(bf16[8,96,768]{2,1,0:T(8,128)(2,1)} %select_convert_fusion), calls=%async_computation.2 | async-start | bytes 2359296 | tf_op jit(solution)/shard_map/all_to_all | solution.py:653
  325.7 76.7 %all-gather.29.cloned.1.call-start = ((), (), s32[]{:S(2)}) async-start(), calls=%async_computation.17 | async-start | bytes 3981312 | tf_op jit(solution)/shard_map/all_gather | solution.py:619
  409.9 46.1 %all-to-all-start.3 = ((bf16[8,96,768]{2,1,0:T(8,128)(2,1)}), bf16[8,96,768]{2,1,0:T(8,128)(2,1)}, u32[]{:S(2)}, u32[]{:S(2)}) async-start(bf16[8,96,768]{2,1,0:T(8,128)(2,1)} %bitcast.311), calls=%async_computation.3 | async-start | bytes 2359296 | tf_op jit(solution)/shard_map/all_to_all | solution.py:653
  414.3 105.3 %all-gather.31.cloned.1.call-start = ((), (), s32[]{:S(2)}) async-start(), calls=%async_computation.18 | async-start | bytes 3981312 | tf_op jit(solution)/shard_map/all_gather | solution.py:619
  478.2 118.6 %reduce-scatter.4.cloned.1.call-start = ((), (), s32[]{:S(2)}) async-start(), calls=%async_computation.11 | async-start | bytes 6635520 | tf_op jit(solution)/shard_map/reduce_scatter | solution.py:794
  523.3 128.3 %reduce-scatter.6.cloned.1.call-start = ((), (), s32[]{:S(2)}) async-start(), calls=%async_computation.12 | async-start | bytes 3981312 | tf_op jit(solution)/shard_map/reduce_scatter | solution.py:796
  542.2 47.0 %collective-permute-start.17 = (bf16[768,768]{1,0:T(8,128)(2,1)}, bf16[768,768]{1,0:T(8,128)(2,1)}, u32[]{:S(2)}, u32[]{:S(2)}) collective-permute-start(bf16[768,768]{1,0:T(8,128)(2,1)} %get-tuple-element.246), channel_id=1, source_target_pairs={{0,24},{8,16},{16,8},{24,0},{1,25},{9,17},{17,9},{25,1},{2,26},{10... | collective-permute-start | bytes 3538952 | tf_op jit(solution)/shard_map/ppermute | solution.py:542
  544.5 52.3 %collective-permute-start.16 = (bf16[768,768]{1,0:T(8,128)(2,1)}, bf16[768,768]{1,0:T(8,128)(2,1)}, u32[]{:S(2)}, u32[]{:S(2)}) collective-permute-start(bf16[768,768]{1,0:T(8,128)(2,1)} %get-tuple-element.247), channel_id=1, source_target_pairs={{0,16},{8,24},{16,0},{24,8},{1,17},{9,25},{17,1},{25,9},{2,18},{10... | collective-permute-start | bytes 3538952 | tf_op jit(solution)/shard_map/ppermute | solution.py:542
  545.1 51.7 %collective-permute-start.15 = (bf16[768,768]{1,0:T(8,128)(2,1)}, bf16[768,768]{1,0:T(8,128)(2,1)}, u32[]{:S(2)}, u32[]{:S(2)}) collective-permute-start(bf16[768,768]{1,0:T(8,128)(2,1)} %get-tuple-element.248), channel_id=1, source_target_pairs={{0,8},{8,0},{16,24},{24,16},{1,9},{9,1},{17,25},{25,17},{2,10},{10... | collective-permute-start | bytes 3538952 | tf_op jit(solution)/shard_map/ppermute | solution.py:542
  596.9 82.7 %reduce-scatter.8.cloned.1.call-start = ((), (), s32[]{:S(2)}) async-start(), calls=%async_computation.13 | async-start | bytes 1474560 | tf_op jit(solution)/shard_map/reduce_scatter | solution.py:817
  628.4 33.2 %collective-permute-start.23 = (bf16[96,3840]{1,0:T(8,128)(2,1)}, bf16[96,3840]{1,0:T(8,128)(2,1)S(1)}, u32[]{:S(2)}, u32[]{:S(2)}) collective-permute-start(bf16[96,3840]{1,0:T(8,128)(2,1)} %reduce-scatter.4.cloned.1.call-done), channel_id=1, source_target_pairs={{0,16},{8,24},{16,0},{24,8},{1,17},{9,25},{17,1},{25,9},{2,18},{10... | collective-permute-start | bytes 2211848 | tf_op jit(solution)/shard_map/ppermute | solution.py:542
  629.7 33.5 %collective-permute-start.22 = (bf16[96,3840]{1,0:T(8,128)(2,1)}, bf16[96,3840]{1,0:T(8,128)(2,1)}, u32[]{:S(2)}, u32[]{:S(2)}) collective-permute-start(bf16[96,3840]{1,0:T(8,128)(2,1)} %reduce-scatter.4.cloned.1.call-done), channel_id=1, source_target_pairs={{0,8},{8,0},{16,24},{24,16},{1,9},{9,1},{17,25},{25,17},{2,10},{10... | collective-permute-start | bytes 2211848 | tf_op jit(solution)/shard_map/ppermute | solution.py:542
  (137 other events, 1558.1 us)
Sparse Core Ops, SparseCore 0:
  11.4 25.3 all-gather.22
  39.0 33.0 all-gather.24
  73.8 37.3 all-gather.14
  113.2 29.9 all-gather.26
  166.6 44.1 all-gather.16
  215.5 62.1 all-gather.18
  290.9 54.5 all-gather.20
  361.7 38.8 all-gather.28
  478.4 41.1 all-gather.30
  523.4 64.9 reduce-scatter.3
  597.0 43.8 reduce-scatter.5
  651.8 27.7 reduce-scatter.7

commit v4 on v3

--- a/solution.py
+++ b/solution.py
@@ -469,7 +469,7 @@
     count, total, _ = rows.shape
     width, block = w_in.shape[2], 512
     blocks = width // block
-    edges = (0, blocks // 2, blocks - blocks // 6, blocks)
+    edges = (0, blocks // 2, blocks // 2 + blocks // 6, blocks)
     first, steps = edges[part], edges[part + 1] - edges[part]
     whole = pl.BlockSpec((1, total, D), lambda e, i: (e, 0, 0))
     by_in = pl.BlockSpec((1, D, block), lambda e, i: (e, 0, i + first))
@@ -625,13 +625,11 @@
         dqkv, dgap, dfar = attention_backward(
             code, me, qt_all, dt_all, kv, stats_all, gap, far, *shared
         )
-        out_part = mm(ctxb, grad_low, 0, 0) if layer else None
-        qkv_part = mm(normed, dqkv, 0, 0)
         normed_grad = mm(dqkv, w, 1, 1)
         _, pull_back = jax.vjp(norm_rows, residual, norm_gains[layer, 0])
         residual_grad, gain_grad = pull_back(normed_grad)
         table_grad = bias_back(dgap, dfar)
-        return grad_out + residual_grad, qkv_part, out_part, gain_grad, table_grad, grad_all, held, covered
+        return grad_out + residual_grad, dqkv, gain_grad, table_grad, grad_all, held, covered
 
     experts_all = router.shape[1]
     per_group = experts_all // groups
@@ -754,15 +752,15 @@
         return second_out + gate_probs[:, 0:1] * picked[0] + gate_probs[:, 1:2] * picked[1]
 
 
-    def expert_half(part, earlier):
+    def expert_half(part, earlier, extra=()):
         def run(sent):
-            rows_in, _ = lax.optimization_barrier((rows_all, sent))
+            rows_in, _, _ = lax.optimization_barrier((rows_all, sent, extra))
             return tuple(expert_gradients(rows_in, dye_all, expert_in, expert_out, part, earlier))
 
         return run
 
     back_b = attend_back(grad_second, saved_b, 1, queries_all[1], made_rows, expert_half(0, ()))
-    grad_ffn, qkv_part_b, out_part_b, gain_grad_b, table_grad_b, _, made_held, expert_sums = back_b
+    grad_ffn, dqkv_b, gain_grad_b, table_grad_b, _, made_held, expert_sums = back_b
     final_out = finish(made_held)
     grad_ffn, final_out = lax.optimization_barrier((grad_ffn, final_out))
     down_low = grad_ffn.astype(BF16)
@@ -781,16 +779,29 @@
         at = k * span + which * piece
         return packed([x[:, at : at + piece] for x in (down_part, in_part)])
 
-    theirs = from_sibling(jnp.stack([halves(k, 1) for k in range(replicas)]))
+    their_half = jnp.stack([halves(k, 1) for k in range(replicas)])
+    theirs = from_sibling(their_half)
     ffn_parts = [
         (halves(k, 0).astype(F32) + theirs[k].astype(F32)).astype(BF16) for k in range(replicas)
     ]
+
+    def cover_a(sent):
+        dq, _ = lax.optimization_barrier((dqkv_b, sent))
+        part_b = packed(
+            [
+                mm(own_b, dq, 0, 0),
+                mm(saved_b[5], grad_second.astype(BF16), 0, 0),
+                mm(saved_a[5], grad_first.astype(BF16), 0, 0),
+            ]
+        )
+        return expert_half(1, expert_sums, their_half)(sent), part_b, ffn_parts
+
+    back_a = attend_back(grad_first, saved_a, 0, queries_all[0], (), cover_a)
+    grad_tokens, dqkv_a, gain_grad_a, table_grad_a, grad_all_a, _, covered_a = back_a
+    expert_sums, parts_b, ffn_parts = covered_a
     ffn_got = [from_replica(ffn_parts[k], k) for k in range(1, replicas)]
-    back_a = attend_back(grad_first, saved_a, 0, queries_all[0], (), expert_half(1, expert_sums))
-    grad_tokens, qkv_part_a, out_part_a, gain_grad_a, table_grad_a, grad_all_a, _, expert_sums = back_a
-    out_part_a = mm(saved_a[5], grad_first.astype(BF16), 0, 0)
-    parts_b, _ = lax.optimization_barrier((packed([qkv_part_b, out_part_b, out_part_a]), grad_all_a))
-    parts_a = qkv_part_a.astype(BF16)
+    parts_b, _ = lax.optimization_barrier((parts_b, grad_all_a))
+    parts_a = mm(own_a, dqkv_a, 0, 0).astype(BF16)
     shard_b = lax.psum_scatter(parts_b, "grp", scatter_dimension=0, tiled=True)
     parts_a, shard_b, ffn_got = lax.optimization_barrier((parts_a, shard_b, ffn_got))
     shard_a = lax.psum_scatter(parts_a, "grp", scatter_dimension=0, tiled=True)
@@ -846,6 +857,7 @@
     table_all = jnp.stack([table_grad_a, table_grad_b])
     small = [gain_all, table_all, router_part]
     flat = jnp.concatenate([x.reshape(-1, BLK) for x in small], axis=0)
+    flat, expert_out_sum, ffn_total = lax.optimization_barrier((flat, expert_out_sum, ffn_total))
     for axis, count in (("rep", replicas), ("grp", groups)):
         for bit in range(count.bit_length() - 1):
             flat = flat + lax.ppermute(flat, axis, [(i, i ^ (1 << bit)) for i in range(count)])

time: 714 us -> 694 us (0.972)
  waiting for transfers between devices: 172 us -> 152 us
    reduce_scatter x1, waiting for transfers between devices: 0.01 us -> 9.73 us  [body(): shard_b = lax.psum_scatter(parts_b, 'grp', scatter_dimension=0, tiled=True)]
    ppermute x22, waiting for transfers between devices: 49.6 us -> 40.5 us  [from_replica(): return lax.ppermute(x, 'rep', [(i, i ^ k) for i in range(replicas)])]
    ppermute x7, waiting for transfers between devices: 10.2 us -> 1.42 us  [from_sibling(): return lax.ppermute(x, 'grp', [(i, i ^ 1) for i in range(groups)])]
    unnamed x248 -> x242, local copies, waits for them, and re-layouts: 30.8 us -> 28 us
  transfers between devices with their start and end apart: 49 -> 49, of which waited for: 27 -> 23; matrix products, arithmetic and copies ran while one was open for 24% -> 26% of each run, Pallas kernels for 28% -> 28%
where the time goes in v4:
time: 694 us; the launch traced here: 687 us
  Pallas kernels  195 us (28%)
  waiting for transfers between devices  152 us (22%)
  matrix products  96 us (14%)
  local copies, waits for them, and re-layouts  76.4 us (11%)
  other arithmetic  61.5 us (9%)
  blocking collectives  45.4 us (7%)
  starting transfers between devices  43.8 us (6%)
  between operations  16.6 us (2%)
    dot_general x28, matrix products, mm(): lax.dot_general(a, b, (((ca,), (cb,)), ((), ())), preferred_element_type=...  90.4 us
    pallas_call x3, Pallas kernels, expert_gradients(): pl.pallas_call(expert_kernel, name=f'expert_gradients_{part}', grid=(coun...  87.1 us
    pallas_call x2, Pallas kernels, attention_backward(): pl.pallas_call(bwd_kernel, name='attention_backward', out_shape=[jax.Shap...  59.6 us
    all_to_all x1, blocking collectives, exchange(): lax.all_to_all(x.reshape(groups, per_group * slots, D), 'grp', split_axis...  45.4 us
    ppermute x22, waiting for transfers between devices, from_replica(): return lax.ppermute(x, 'rep', [(i, i ^ k) for i in range(replicas)])  40.5 us
    unnamed x242, local copies, waits for them, and re-layouts  28 us
    all_gather x1, waiting for transfers between devices, body(): ffn_quarter = lax.all_gather(ffn_own, 'grp', axis=0)  27.4 us
    all_gather x2, waiting for transfers between devices, layer_quarter(): return lax.all_gather(part, 'grp', axis=0)  26.8 us
  transfers between devices with their start and end apart: 49, of which 23 were waited for; matrix products, arithmetic and copies ran while one was open for 26% of the time, Pallas kernels for 28%

profile of v4, /device:TPU:0, one launch (start us, length us, event | category | flops | bytes accessed | tf_op | source)
XLA Modules:
  0.0 687.2 jit_solution(8219245693769503359)
XLA Ops:
  13.8 23.0 %all-gather.23.cloned.1.call-done = bf16[192,3072]{1,0:T(8,128)(2,1)} async-done(((bf16[24,3072]{1,0:T(8,128)(2,1)}), bf16[192,3072]{1,0:T(8,128)(2,1)}) %all-gather.23.cloned.1.call-update) | async-done | bytes 1179664 | tf_op jit(solution)/shard_map/all_gather | solution.py:560
  44.7 27.4 %all-gather.25.cloned.1.call-done = bf16[832,1536]{1,0:T(8,128)(2,1)} async-done(((bf16[104,1536]{1,0:T(8,128)(2,1)}), bf16[832,1536]{1,0:T(8,128)(2,1)}) %all-gather.25.cloned.1.call-update) | async-done | bytes 2555920 | tf_op jit(solution)/shard_map/all_gather | solution.py:585
  90.7 20.4 %all-gather.15.cloned.1.call-done = bf16[2048,768]{1,0:T(8,128)(2,1)} async-done(((bf16[256,768]{1,0:T(8,128)(2,1)}), bf16[2048,768]{1,0:T(8,128)(2,1)}) %all-gather.15.cloned.1.call-update) | async-done | bytes 3145744 | tf_op jit(solution)/shard_map/all_gather | solution.py:588
  119.6 8.7 %convolution_convert_fusion.1.kv_ref = bf16[2048,1536]{1,0:T(8,128)(2,1)} fusion(bf16[768,3072]{1,0:T(8,128)(2,1)} %bitcast.275, bf16[2048,768]{1,0:T(8,128)(2,1)S(1)} %copy-done.25, f32[768]{0:T(1024)S(1)} %get-tuple-element.237, f32[2048]{0:T(1024)S(1)} %add_rsqrt_fusion), kind=kOutput, calls=%fused_computation.4 | convolution fusion | flops 4841275392 | bytes 11807744 | tf_op jit(solution)/shard_map/dot_general | solution.py:29
  128.3 6.8 attention_forward.2
  150.6 10.9 %ffn_forward.1 = (f32[256,768]{1,0:T(8,128)}, bf16[256,768]{1,0:T(8,128)(2,1)}, bf16[256,3072]{1,0:T(8,128)(2,1)}, f32[256,3072]{1,0:T(8,128)}) custom-call(f32[256,768]{1,0:T(8,128)} %convert_add_fusion.4.x_ref, f32[1,768]{1,0:T(1,128)} %get-tuple-element.322.gain_ref, bf16[768,768]{1,0:T(8,128)(2,1)} %bitcast.272, bf16[768,768]{1,0:T(8,128)(2,1)} %bitcast.267, ...), custom_call_target="tpu_custom_call" | custom-call | flops 2415919104 | bytes 18874368 | tf_op jit(solution)/shard_map/ffn_forward/pallas_call | solution.py:367
  184.2 6.1 collective-permute-done.12
  190.4 11.9 %collective-permute-done.11 = bf16[8,24,1536]{2,1,0:T(8,128)(2,1)S(1)} collective-permute-done((bf16[8,24,1536]{2,1,0:T(8,128)(2,1)S(1)}, bf16[8,24,1536]{2,1,0:T(8,128)(2,1)S(1)}, u32[]{:S(2)}, u32[]{:S(2)}) %collective-permute-start.11) | collective-permute-done | bytes 589856 | tf_op jit(solution)/shard_map/ppermute | solution.py:542
  219.4 8.6 %convolution_convert_fusion.kv_ref = bf16[2048,1536]{1,0:T(8,128)(2,1)} fusion(bf16[2048,768]{1,0:T(8,128)(2,1)S(1)} %copy-done.103, bf16[768,3072]{1,0:T(8,128)(2,1)} %bitcast.50), kind=kOutput, calls=%fused_computation.3 | convolution fusion | flops 4834983936 | bytes 11796480 | tf_op jit(solution)/shard_map/dot_general | solution.py:29
  228.0 6.8 attention_forward.3
  239.9 45.4 %all_to_all.20 = bf16[8,96,768]{2,1,0:T(8,128)(2,1)} all-to-all(bf16[8,96,768]{2,1,0:T(8,128)(2,1)S(1)} %select_convert_fusion.1), channel_id=1, replica_groups=mesh['rep'=4,'grp'=8] {'grp'}, dimensions={0} | all-to-all | bytes 2359296 | tf_op jit(solution)/shard_map/all_to_all | solution.py:651
  288.3 23.8 %expert_rows.1 = (bf16[1,768,768]{2,1,0:T(8,128)(2,1)}, f32[1,768,768]{2,1,0:T(8,128)}, f32[1,768,128]{2,1,0:T(8,128)}) custom-call(bf16[1,768,768]{2,1,0:T(8,128)(2,1)} %bitcast.286, bf16[1,768,768]{2,1,0:T(8,128)(2,1)} %multiply_convert_fusion.2.dye_ref, bf16[1,768,768]{2,1,0:T(8,128)(2,1)} %bitcast.282, bf16[1,768,3072]{2,1,0:T(8,128)(2,1)} %win_ref.7, ...), custom_call_target="tpu_custom_call" | custom-call | flops 14495514624 | bytes 37748736 | tf_op jit(solution)/shard_map/expert_rows/pallas_call | solution.py:422
  320.1 7.1 %fusion.7.qt_ref = bf16[768,2048]{1,0:T(8,128)(2,1)} fusion(bf16[768,3072]{1,0:T(8,128)(2,1)} %bitcast.277, bf16[2048,768]{1,0:T(8,128)(2,1)} %all-gather.15.cloned.1.call-done, f32[768]{0:T(1024)S(1)} %get-tuple-element.237, f32[2048]{0:T(1024)S(1)} %copy-done.90), kind=kOutput, calls=%fused_computation.23 | convolution fusion | flops 2425356288 | bytes 7482368 | tf_op jit(solution)/shard_map/dot_general | solution.py:29
  327.2 5.5 fusion.8.qt_ref
  332.7 7.8 %all-gather.21.cloned.1.call-done.rows_ref = bf16[1,3072,768]{2,1,0:T(8,128)(2,1)} async-done(((bf16[1,768,768]{2,1,0:T(8,128)(2,1)}), bf16[1,3072,768]{2,1,0:T(8,128)(2,1)}) %all-gather.21.cloned.1.call-update) | async-done | bytes 4718608 | tf_op jit(solution)/shard_map/all_gather | solution.py:662
  355.9 40.7 %expert_gradients_0.1 = (f32[1,768,3072]{2,1,0:T(8,128)}, f32[1,3072,768]{2,1,0:T(8,128)}) custom-call(bf16[1,3072,768]{2,1,0:T(8,128)(2,1)} %all-gather.21.cloned.1.call-done.rows_ref, bf16[1,3072,768]{2,1,0:T(8,128)(2,1)} %multiply_convert_fusion.dye_ref, bf16[1,768,3072]{2,1,0:T(8,128)(2,1)} %win_ref.7, bf16[1,3072,768]{2,1,0:T(8,128)(2,1)} %wout_ref.7), custom_call_target="tpu_custom_call" | custom-call | flops 28991029248 | bytes 75497472 | tf_op jit(solution)/shard_map/expert_gradients_0/pallas_call | solution.py:477
  413.9 29.8 %attention_backward.2 = (bf16[256,2304]{1,0:T(8,128)(2,1)}, f32[12,256]{1,0:T(8,128)}, f32[12,128]{1,0:T(8,128)}) custom-call(s32[16,16]{1,0:T(8,128)} %select_select_fusion.code_ref, s32[1]{0:T(128)} %bitcast.7.me_ref, bf16[768,2048]{1,0:T(8,128)(2,1)} %fusion.8.qt_ref, bf16[768,2048]{1,0:T(8,128)(2,1)} %convolution_convert_fusion.7.dt_ref, ...), custom_call_target="tpu_custom_call" | custom-call | flops 5637144576 | bytes 100663296 | tf_op jit(solution)/shard_map/attention_backward/pallas_call | solution.py:320
  484.9 17.1 %expert_gradients_1.1 = (f32[1,768,3072]{2,1,0:T(8,128)}, f32[1,3072,768]{2,1,0:T(8,128)}) custom-call(bf16[1,3072,768]{2,1,0:T(8,128)(2,1)} %all-gather.21.cloned.1.call-done.rows_ref, bf16[1,3072,768]{2,1,0:T(8,128)(2,1)} %multiply_convert_fusion.dye_ref, bf16[1,768,3072]{2,1,0:T(8,128)(2,1)} %win_ref.7, ...), custom_call_target="tpu_custom_call", output_to_operand_aliasing={{0}: (4, {}), {1}: (5, {})} | custom-call | flops 9663676416 | bytes 25165824 | tf_op jit(solution)/shard_map/expert_gradients_1/pallas_call | solution.py:477
  518.2 7.1 %convolution_convert_fusion.6.dt_ref = bf16[768,2048]{1,0:T(8,128)(2,1)} fusion(bf16[2048,768]{1,0:T(8,128)(2,1)} %bitcast.291, bf16[768,3072]{1,0:T(8,128)(2,1)} %bitcast.279), kind=kOutput, calls=%fused_computation.18 | convolution fusion | flops 2417491968 | bytes 7471104 | tf_op jit(solution)/shard_map/dot_general | solution.py:29
  527.8 29.8 %attention_backward.3 = (bf16[256,2304]{1,0:T(8,128)(2,1)}, f32[12,256]{1,0:T(8,128)}, f32[12,128]{1,0:T(8,128)}) custom-call(s32[16,16]{1,0:T(8,128)} %select_select_fusion.code_ref, s32[1]{0:T(128)} %bitcast.7.me_ref, bf16[768,2048]{1,0:T(8,128)(2,1)} %fusion.7.qt_ref, bf16[768,2048]{1,0:T(8,128)(2,1)} %convolution_convert_fusion.6.dt_ref, ...), custom_call_target="tpu_custom_call" | custom-call | flops 5637144576 | bytes 100663296 | tf_op jit(solution)/shard_map/attention_backward/pallas_call | solution.py:320
  561.9 7.7 %collective-permute-done.16 = bf16[768,768]{1,0:T(8,128)(2,1)} collective-permute-done((bf16[768,768]{1,0:T(8,128)(2,1)}, bf16[768,768]{1,0:T(8,128)(2,1)}, u32[]{:S(2)}, u32[]{:S(2)}) %collective-permute-start.16) | collective-permute-done | bytes 1179680 | tf_op jit(solution)/shard_map/ppermute | solution.py:542
  569.7 9.7 %reduce-scatter.4.cloned.1.call-done = bf16[96,3840]{1,0:T(8,128)(2,1)} async-done(((bf16[768,3840]{1,0:T(8,128)(2,1)}), bf16[96,3840]{1,0:T(8,128)(2,1)}) %reduce-scatter.4.cloned.1.call-update) | async-done | bytes 737296 | tf_op jit(solution)/shard_map/reduce_scatter | solution.py:805
  596.8 29.2 %expert_gradients_2.1 = (f32[1,768,3072]{2,1,0:T(8,128)}, f32[1,3072,768]{2,1,0:T(8,128)}) custom-call(bf16[1,3072,768]{2,1,0:T(8,128)(2,1)} %all-gather.21.cloned.1.call-done.rows_ref, bf16[1,3072,768]{2,1,0:T(8,128)(2,1)} %multiply_convert_fusion.dye_ref, bf16[1,768,3072]{2,1,0:T(8,128)(2,1)} %win_ref.7, ...), custom_call_target="tpu_custom_call", output_to_operand_aliasing={{0}: (4, {}), {1}: (5, {})} | custom-call | flops 19327352832 | bytes 50331648 | tf_op jit(solution)/shard_map/expert_gradients_2/pallas_call | solution.py:477
  646.8 5.9 collective-permute-done.33
  (558 shorter events, 273.3 us)
Async XLA Ops:
  11.3 60.8 %all-gather.25.cloned.1.call-start = ((), (), s32[]{:S(2)}) async-start(), calls=%async_computation.15 | async-start | bytes 2875392 | tf_op jit(solution)/shard_map/all_gather | solution.py:585
  36.8 74.3 %all-gather.15.cloned.1.call-start = ((), (), s32[]{:S(2)}) async-start(), calls=%async_computation.7 | async-start | bytes 3538944 | tf_op jit(solution)/shard_map/all_gather | solution.py:588
  40.9 31.3 %collective-permute-start.2 = (bf16[8,24,1536]{2,1,0:T(8,128)(2,1)S(1)}, bf16[8,24,1536]{2,1,0:T(8,128)(2,1)S(1)}, u32[]{:S(2)}, u32[]{:S(2)}) collective-permute-start(bf16[8,24,1536]{2,1,0:T(8,128)(2,1)S(1)} %constant_dynamic-slice_fusion.6), channel_id=1, source_target_pairs={{0,24},{8,16},{16,8},{24,0},{1,25},{9,17},{17,9},{25,1},{2,26},{10... | collective-permute-start | bytes 1769480 | tf_op jit(solution)/shard_map/ppermute | solution.py:542
  72.1 71.0 %all-gather.27.cloned.1.call-start = ((), (), s32[]{:S(2)}) async-start(), calls=%async_computation.16 | async-start | bytes 1327104 | tf_op jit(solution)/shard_map/all_gather | solution.py:560
  84.9 52.9 %collective-permute-start.6 = (bf16[768,768]{1,0:T(8,128)(2,1)S(1)}, bf16[768,768]{1,0:T(8,128)(2,1)}, u32[]{:S(2)}, u32[]{:S(2)}) collective-permute-start(bf16[768,768]{1,0:T(8,128)(2,1)S(1)} %bitcast.269), channel_id=1, source_target_pairs={{0,24},{8,16},{16,8},{24,0},{1,25},{9,17},{17,9},{25,1},{2,26},{10... | collective-permute-start | bytes 3538952 | tf_op jit(solution)/shard_map/ppermute | solution.py:542
  87.1 52.2 %collective-permute-start.5 = (bf16[768,768]{1,0:T(8,128)(2,1)S(1)}, bf16[768,768]{1,0:T(8,128)(2,1)}, u32[]{:S(2)}, u32[]{:S(2)}) collective-permute-start(bf16[768,768]{1,0:T(8,128)(2,1)S(1)} %bitcast.270), channel_id=1, source_target_pairs={{0,16},{8,24},{16,0},{24,8},{1,17},{9,25},{17,1},{25,9},{2,18},{10... | collective-permute-start | bytes 3538952 | tf_op jit(solution)/shard_map/ppermute | solution.py:542
  87.7 51.7 %collective-permute-start.4 = (bf16[768,768]{1,0:T(8,128)(2,1)S(1)}, bf16[768,768]{1,0:T(8,128)(2,1)}, u32[]{:S(2)}, u32[]{:S(2)}) collective-permute-start(bf16[768,768]{1,0:T(8,128)(2,1)S(1)} %bitcast.271), channel_id=1, source_target_pairs={{0,8},{8,0},{16,24},{24,16},{1,9},{9,1},{17,25},{25,17},{2,10},{10... | collective-permute-start | bytes 3538952 | tf_op jit(solution)/shard_map/ppermute | solution.py:542
  112.9 48.6 %all-to-all-start = ((bf16[8,96,768]{2,1,0:T(8,128)(2,1)}), bf16[8,96,768]{2,1,0:T(8,128)(2,1)S(1)}, u32[]{:S(2)}, u32[]{:S(2)}) async-start(bf16[8,96,768]{2,1,0:T(8,128)(2,1)} %bitcast.312), calls=%async_computation | async-start | bytes 2359296 | tf_op jit(solution)/shard_map/all_to_all | solution.py:651
  116.4 98.6 %all-gather.17.cloned.1.call-start = ((), (), s32[]{:S(2)}) async-start(), calls=%async_computation.8 | async-start | bytes 3538944 | tf_op jit(solution)/shard_map/all_gather | solution.py:687
  166.4 118.9 %all-gather.19.cloned.1.call-start = ((), (), s32[]{:S(2)}) async-start(), calls=%async_computation.9 | async-start | bytes 5898240 | tf_op jit(solution)/shard_map/all_gather | solution.py:662
  215.1 125.4 %all-gather.21.cloned.1.call-start = ((), (), s32[]{:S(2)}) async-start(), calls=%async_computation.10 | async-start | bytes 5898240 | tf_op jit(solution)/shard_map/all_gather | solution.py:662
  316.5 32.9 %all-to-all-start.2 = ((bf16[8,96,768]{2,1,0:T(8,128)(2,1)}), bf16[8,96,768]{2,1,0:T(8,128)(2,1)S(1)}, u32[]{:S(2)}, u32[]{:S(2)}) async-start(bf16[8,96,768]{2,1,0:T(8,128)(2,1)} %select_convert_fusion), calls=%async_computation.2 | async-start | bytes 2359296 | tf_op jit(solution)/shard_map/all_to_all | solution.py:651
  320.1 76.6 %all-gather.29.cloned.1.call-start = ((), (), s32[]{:S(2)}) async-start(), calls=%async_computation.17 | async-start | bytes 3981312 | tf_op jit(solution)/shard_map/all_gather | solution.py:619
  404.1 44.4 %all-to-all-start.3 = ((bf16[8,96,768]{2,1,0:T(8,128)(2,1)}), bf16[8,96,768]{2,1,0:T(8,128)(2,1)}, u32[]{:S(2)}, u32[]{:S(2)}) async-start(bf16[8,96,768]{2,1,0:T(8,128)(2,1)} %bitcast.311), calls=%async_computation.3 | async-start | bytes 2359296 | tf_op jit(solution)/shard_map/all_to_all | solution.py:651
  408.5 101.8 %all-gather.31.cloned.1.call-start = ((), (), s32[]{:S(2)}) async-start(), calls=%async_computation.18 | async-start | bytes 3981312 | tf_op jit(solution)/shard_map/all_gather | solution.py:619
  468.6 110.7 %reduce-scatter.4.cloned.1.call-start = ((), (), s32[]{:S(2)}) async-start(), calls=%async_computation.11 | async-start | bytes 6635520 | tf_op jit(solution)/shard_map/reduce_scatter | solution.py:805
  514.2 111.8 %reduce-scatter.6.cloned.1.call-start = ((), (), s32[]{:S(2)}) async-start(), calls=%async_computation.12 | async-start | bytes 3981312 | tf_op jit(solution)/shard_map/reduce_scatter | solution.py:807
  514.7 47.2 %collective-permute-start.15 = (bf16[768,768]{1,0:T(8,128)(2,1)}, bf16[768,768]{1,0:T(8,128)(2,1)}, u32[]{:S(2)}, u32[]{:S(2)}) collective-permute-start(bf16[768,768]{1,0:T(8,128)(2,1)} %get-tuple-element.147), channel_id=1, source_target_pairs={{0,8},{8,0},{16,24},{24,16},{1,9},{9,1},{17,25},{25,17},{2,10},{10... | collective-permute-start | bytes 3538952 | tf_op jit(solution)/shard_map/ppermute | solution.py:542
  516.2 53.4 %collective-permute-start.16 = (bf16[768,768]{1,0:T(8,128)(2,1)}, bf16[768,768]{1,0:T(8,128)(2,1)}, u32[]{:S(2)}, u32[]{:S(2)}) collective-permute-start(bf16[768,768]{1,0:T(8,128)(2,1)} %get-tuple-element.148), channel_id=1, source_target_pairs={{0,16},{8,24},{16,0},{24,8},{1,17},{9,25},{17,1},{25,9},{2,18},{10... | collective-permute-start | bytes 3538952 | tf_op jit(solution)/shard_map/ppermute | solution.py:542
  517.7 52.0 %collective-permute-start.17 = (bf16[768,768]{1,0:T(8,128)(2,1)}, bf16[768,768]{1,0:T(8,128)(2,1)}, u32[]{:S(2)}, u32[]{:S(2)}) collective-permute-start(bf16[768,768]{1,0:T(8,128)(2,1)} %get-tuple-element.149), channel_id=1, source_target_pairs={{0,24},{8,16},{16,8},{24,0},{1,25},{9,17},{17,9},{25,1},{2,26},{10... | collective-permute-start | bytes 3538952 | tf_op jit(solution)/shard_map/ppermute | solution.py:542
  579.4 77.5 %reduce-scatter.8.cloned.1.call-start = ((), (), s32[]{:S(2)}) async-start(), calls=%async_computation.13 | async-start | bytes 1474560 | tf_op jit(solution)/shard_map/reduce_scatter | solution.py:828
  589.6 46.3 %collective-permute-start.24 = (bf16[96,3840]{1,0:T(8,128)(2,1)}, bf16[96,3840]{1,0:T(8,128)(2,1)S(1)}, u32[]{:S(2)}, u32[]{:S(2)}) collective-permute-start(bf16[96,3840]{1,0:T(8,128)(2,1)} %reduce-scatter.4.cloned.1.call-done), channel_id=1, source_target_pairs={{0,24},{8,16},{16,8},{24,0},{1,25},{9,17},{17,9},{25,1},{2,26},{10... | collective-permute-start | bytes 2211848 | tf_op jit(solution)/shard_map/ppermute | solution.py:542
  591.9 44.1 %collective-permute-start.23 = (bf16[96,3840]{1,0:T(8,128)(2,1)}, bf16[96,3840]{1,0:T(8,128)(2,1)}, u32[]{:S(2)}, u32[]{:S(2)}) collective-permute-start(bf16[96,3840]{1,0:T(8,128)(2,1)} %reduce-scatter.4.cloned.1.call-done), channel_id=1, source_target_pairs={{0,16},{8,24},{16,0},{24,8},{1,17},{9,25},{17,1},{25,9},{2,18},{10... | collective-permute-start | bytes 2211848 | tf_op jit(solution)/shard_map/ppermute | solution.py:542
  592.5 43.5 %collective-permute-start.22 = (bf16[96,3840]{1,0:T(8,128)(2,1)}, bf16[96,3840]{1,0:T(8,128)(2,1)}, u32[]{:S(2)}, u32[]{:S(2)}) collective-permute-start(bf16[96,3840]{1,0:T(8,128)(2,1)} %reduce-scatter.4.cloned.1.call-done), channel_id=1, source_target_pairs={{0,8},{8,0},{16,24},{24,16},{1,9},{9,1},{17,25},{25,17},{2,10},{10... | collective-permute-start | bytes 2211848 | tf_op jit(solution)/shard_map/ppermute | solution.py:542
  (134 other events, 1590.0 us)
Sparse Core Ops, SparseCore 0:
  11.4 25.3 all-gather.22
  39.0 33.0 all-gather.24
  73.8 37.3 all-gather.14
  113.2 29.9 all-gather.26
  166.5 42.2 all-gather.16
  215.2 60.2 all-gather.18
  285.4 55.0 all-gather.20
  356.1 39.5 all-gather.28
  468.8 41.5 all-gather.30
  514.4 64.9 reduce-scatter.3
  581.8 42.1 reduce-scatter.5
  628.7 28.1 reduce-scatter.7

commit v5 on v4

--- a/solution.py
+++ b/solution.py
@@ -607,7 +607,7 @@
         saved = (residual, normed, normed_all, kv, ctxt, ctxb, lse, gap, far)
         return residual + branch, saved
 
-    def attend_back(grad_out, saved, layer, qt_all, held, cover):
+    def attend_back(grad_out, saved, layer, qt_all, held, cover, late):
         residual, normed, normed_all, kv, ctxt, ctxb, lse, gap, far = saved
         w, wo = w_qkv[layer], w_out[layer]
         grad_low = grad_out.astype(BF16)
@@ -625,11 +625,12 @@
         dqkv, dgap, dfar = attention_backward(
             code, me, qt_all, dt_all, kv, stats_all, gap, far, *shared
         )
+        dqkv, done = lax.optimization_barrier((dqkv, late(held)))
         normed_grad = mm(dqkv, w, 1, 1)
         _, pull_back = jax.vjp(norm_rows, residual, norm_gains[layer, 0])
         residual_grad, gain_grad = pull_back(normed_grad)
         table_grad = bias_back(dgap, dfar)
-        return grad_out + residual_grad, dqkv, gain_grad, table_grad, grad_all, held, covered
+        return grad_out + residual_grad, dqkv, gain_grad, table_grad, grad_all, held, covered, done
 
     experts_all = router.shape[1]
     per_group = experts_all // groups
@@ -759,8 +760,14 @@
 
         return run
 
-    back_b = attend_back(grad_second, saved_b, 1, queries_all[1], made_rows, expert_half(0, ()))
-    grad_ffn, dqkv_b, gain_grad_b, table_grad_b, _, made_held, expert_sums = back_b
+    held_b = (made_rows, mm(saved_b[5], grad_second.astype(BF16), 0, 0).astype(BF16))
+
+    def late_b(held):
+        return lax.psum_scatter(held[1], "grp", scatter_dimension=0, tiled=True)
+
+    back_b = attend_back(grad_second, saved_b, 1, queries_all[1], held_b, expert_half(0, ()), late_b)
+    grad_ffn, dqkv_b, gain_grad_b, table_grad_b, _, held_b, expert_sums, shard_out = back_b
+    made_held = held_b[0]
     final_out = finish(made_held)
     grad_ffn, final_out = lax.optimization_barrier((grad_ffn, final_out))
     down_low = grad_ffn.astype(BF16)
@@ -790,14 +797,13 @@
         part_b = packed(
             [
                 mm(own_b, dq, 0, 0),
-                mm(saved_b[5], grad_second.astype(BF16), 0, 0),
                 mm(saved_a[5], grad_first.astype(BF16), 0, 0),
             ]
         )
         return expert_half(1, expert_sums, their_half)(sent), part_b, ffn_parts
 
-    back_a = attend_back(grad_first, saved_a, 0, queries_all[0], (), cover_a)
-    grad_tokens, dqkv_a, gain_grad_a, table_grad_a, grad_all_a, _, covered_a = back_a
+    back_a = attend_back(grad_first, saved_a, 0, queries_all[0], (), cover_a, lambda held: ())
+    grad_tokens, dqkv_a, gain_grad_a, table_grad_a, grad_all_a, _, covered_a, _ = back_a
     expert_sums, parts_b, ffn_parts = covered_a
     ffn_got = [from_replica(ffn_parts[k], k) for k in range(1, replicas)]
     parts_b, _ = lax.optimization_barrier((parts_b, grad_all_a))
@@ -844,6 +850,7 @@
     ffn_sums = [quarter_of(q) for q in range(replicas)]
     in_sum = jnp.concatenate([x[:, :span] for x in ffn_sums], axis=1)
     down_sum = jnp.concatenate([x[:, span:] for x in ffn_sums], axis=1)
+    shard_b = jnp.concatenate([shard_b[:, : 3 * D], shard_out, shard_b[:, 3 * D :]], axis=1)
     total_b = shard_b.astype(F32)
     for k in range(1, replicas):
         total_b = total_b + from_replica(shard_b, k).astype(F32)

time: 694 us -> 692 us (level)
  waiting for transfers between devices: 152 us -> 145 us
    reduce_scatter x1, waiting for transfers between devices: 9.73 us -> 0.01 us  [body(): shard_b = lax.psum_scatter(parts_b, 'grp', scatter_dimension=0, tiled=True)]
    unnamed x242 -> x244, local copies, waits for them, and re-layouts: 28 us -> 28.7 us
  transfers between devices with their start and end apart: 49 -> 50, of which waited for: 23 -> 24; matrix products, arithmetic and copies ran while one was open for 26% -> 27% of each run, Pallas kernels for 28% -> 29%
where the time goes in v5:
time: 692 us; the launch traced here: 683 us
  Pallas kernels  195 us (28%)
  waiting for transfers between devices  145 us (21%)
  matrix products  94.7 us (14%)
  local copies, waits for them, and re-layouts  79.9 us (12%)
  other arithmetic  63.4 us (9%)
  starting transfers between devices  45.2 us (7%)
  blocking collectives  43.5 us (6%)
  between operations  16.3 us (2%)
    dot_general x28, matrix products, mm(): lax.dot_general(a, b, (((ca,), (cb,)), ((), ())), preferred_element_type=...  89 us
    pallas_call x3, Pallas kernels, expert_gradients(): pl.pallas_call(expert_kernel, name=f'expert_gradients_{part}', grid=(coun...  87.2 us
    pallas_call x2, Pallas kernels, attention_backward(): pl.pallas_call(bwd_kernel, name='attention_backward', out_shape=[jax.Shap...  59.2 us
    all_to_all x1, blocking collectives, exchange(): lax.all_to_all(x.reshape(groups, per_group * slots, D), 'grp', split_axis...  43.5 us
    ppermute x22, waiting for transfers between devices, from_replica(): return lax.ppermute(x, 'rep', [(i, i ^ k) for i in range(replicas)])  39.8 us
    unnamed x244, local copies, waits for them, and re-layouts  28.7 us
    all_gather x1, waiting for transfers between devices, body(): ffn_quarter = lax.all_gather(ffn_own, 'grp', axis=0)  27.4 us
    all_gather x2, waiting for transfers between devices, layer_quarter(): return lax.all_gather(part, 'grp', axis=0)  26.8 us
  transfers between devices with their start and end apart: 50, of which 24 were waited for; matrix products, arithmetic and copies ran while one was open for 27% of the time, Pallas kernels for 29%

profile of v5, /device:TPU:0, one launch (start us, length us, event | category | flops | bytes accessed | tf_op | source)
XLA Modules:
  0.0 682.5 jit_solution(16870256218120847504)
XLA Ops:
  13.8 23.0 %all-gather.23.cloned.1.call-done = bf16[192,3072]{1,0:T(8,128)(2,1)} async-done(((bf16[24,3072]{1,0:T(8,128)(2,1)}), bf16[192,3072]{1,0:T(8,128)(2,1)}) %all-gather.23.cloned.1.call-update) | async-done | bytes 1179664 | tf_op jit(solution)/shard_map/all_gather | solution.py:560
  44.7 27.4 %all-gather.25.cloned.1.call-done = bf16[832,1536]{1,0:T(8,128)(2,1)} async-done(((bf16[104,1536]{1,0:T(8,128)(2,1)}), bf16[832,1536]{1,0:T(8,128)(2,1)}) %all-gather.25.cloned.1.call-update) | async-done | bytes 2555920 | tf_op jit(solution)/shard_map/all_gather | solution.py:585
  90.7 20.4 %all-gather.15.cloned.1.call-done = bf16[2048,768]{1,0:T(8,128)(2,1)} async-done(((bf16[256,768]{1,0:T(8,128)(2,1)}), bf16[2048,768]{1,0:T(8,128)(2,1)}) %all-gather.15.cloned.1.call-update) | async-done | bytes 3145744 | tf_op jit(solution)/shard_map/all_gather | solution.py:588
  119.6 8.7 %convolution_convert_fusion.1.kv_ref = bf16[2048,1536]{1,0:T(8,128)(2,1)} fusion(bf16[768,3072]{1,0:T(8,128)(2,1)} %bitcast.275, bf16[2048,768]{1,0:T(8,128)(2,1)S(1)} %copy-done.23, f32[768]{0:T(1024)S(1)} %get-tuple-element.243, f32[2048]{0:T(1024)S(1)} %add_rsqrt_fusion), kind=kOutput, calls=%fused_computation.4 | convolution fusion | flops 4841275392 | bytes 11807744 | tf_op jit(solution)/shard_map/dot_general | solution.py:29
  128.3 6.8 attention_forward.2
  150.6 10.9 %ffn_forward.1 = (f32[256,768]{1,0:T(8,128)}, bf16[256,768]{1,0:T(8,128)(2,1)}, bf16[256,3072]{1,0:T(8,128)(2,1)}, f32[256,3072]{1,0:T(8,128)}) custom-call(f32[256,768]{1,0:T(8,128)} %convert_add_fusion.4.x_ref, f32[1,768]{1,0:T(1,128)} %get-tuple-element.328.gain_ref, bf16[768,768]{1,0:T(8,128)(2,1)} %bitcast.272, bf16[768,768]{1,0:T(8,128)(2,1)} %bitcast.267, ...), custom_call_target="tpu_custom_call" | custom-call | flops 2415919104 | bytes 18874368 | tf_op jit(solution)/shard_map/ffn_forward/pallas_call | solution.py:367
  184.5 6.1 collective-permute-done.12
  190.6 11.9 %collective-permute-done.11 = bf16[8,24,1536]{2,1,0:T(8,128)(2,1)S(1)} collective-permute-done((bf16[8,24,1536]{2,1,0:T(8,128)(2,1)S(1)}, bf16[8,24,1536]{2,1,0:T(8,128)(2,1)S(1)}, u32[]{:S(2)}, u32[]{:S(2)}) %collective-permute-start.11) | collective-permute-done | bytes 589856 | tf_op jit(solution)/shard_map/ppermute | solution.py:542
  219.8 8.6 %convolution_convert_fusion.kv_ref = bf16[2048,1536]{1,0:T(8,128)(2,1)} fusion(bf16[2048,768]{1,0:T(8,128)(2,1)S(1)} %copy-done.104, bf16[768,3072]{1,0:T(8,128)(2,1)} %bitcast.50), kind=kOutput, calls=%fused_computation.3 | convolution fusion | flops 4834983936 | bytes 11796480 | tf_op jit(solution)/shard_map/dot_general | solution.py:29
  228.5 6.8 attention_forward.3
  240.3 43.5 %all_to_all.20 = bf16[8,96,768]{2,1,0:T(8,128)(2,1)} all-to-all(bf16[8,96,768]{2,1,0:T(8,128)(2,1)S(1)} %select_convert_fusion.1), channel_id=1, replica_groups=mesh['rep'=4,'grp'=8] {'grp'}, dimensions={0} | all-to-all | bytes 2359296 | tf_op jit(solution)/shard_map/all_to_all | solution.py:652
  286.8 23.6 %expert_rows.1 = (bf16[1,768,768]{2,1,0:T(8,128)(2,1)}, f32[1,768,768]{2,1,0:T(8,128)}, f32[1,768,128]{2,1,0:T(8,128)}) custom-call(bf16[1,768,768]{2,1,0:T(8,128)(2,1)} %bitcast.288, bf16[1,768,768]{2,1,0:T(8,128)(2,1)} %multiply_convert_fusion.2.dye_ref, bf16[1,768,768]{2,1,0:T(8,128)(2,1)} %bitcast.282, bf16[1,768,3072]{2,1,0:T(8,128)(2,1)} %win_ref.7, ...), custom_call_target="tpu_custom_call" | custom-call | flops 14495514624 | bytes 37748736 | tf_op jit(solution)/shard_map/expert_rows/pallas_call | solution.py:422
  318.8 7.1 %fusion.7.qt_ref = bf16[768,2048]{1,0:T(8,128)(2,1)} fusion(bf16[768,3072]{1,0:T(8,128)(2,1)} %bitcast.277, bf16[2048,768]{1,0:T(8,128)(2,1)} %all-gather.15.cloned.1.call-done, f32[768]{0:T(1024)S(1)} %get-tuple-element.243, f32[2048]{0:T(1024)S(1)} %copy-done.91), kind=kOutput, calls=%fused_computation.23 | convolution fusion | flops 2425356288 | bytes 7482368 | tf_op jit(solution)/shard_map/dot_general | solution.py:29
  325.9 5.4 fusion.8.qt_ref
  331.2 8.3 %all-gather.21.cloned.1.call-done.rows_ref = bf16[1,3072,768]{2,1,0:T(8,128)(2,1)} async-done(((bf16[1,768,768]{2,1,0:T(8,128)(2,1)}), bf16[1,3072,768]{2,1,0:T(8,128)(2,1)}) %all-gather.21.cloned.1.call-update) | async-done | bytes 4718608 | tf_op jit(solution)/shard_map/all_gather | solution.py:663
  340.8 5.4 multiply_convert_fusion.dye_ref
  356.2 40.9 %expert_gradients_0.1 = (f32[1,768,3072]{2,1,0:T(8,128)}, f32[1,3072,768]{2,1,0:T(8,128)}) custom-call(bf16[1,3072,768]{2,1,0:T(8,128)(2,1)} %all-gather.21.cloned.1.call-done.rows_ref, bf16[1,3072,768]{2,1,0:T(8,128)(2,1)} %multiply_convert_fusion.dye_ref, bf16[1,768,3072]{2,1,0:T(8,128)(2,1)} %win_ref.7, bf16[1,3072,768]{2,1,0:T(8,128)(2,1)} %wout_ref.7), custom_call_target="tpu_custom_call" | custom-call | flops 28991029248 | bytes 75497472 | tf_op jit(solution)/shard_map/expert_gradients_0/pallas_call | solution.py:477
  416.3 29.7 %attention_backward.2 = (bf16[256,2304]{1,0:T(8,128)(2,1)}, f32[12,256]{1,0:T(8,128)}, f32[12,128]{1,0:T(8,128)}) custom-call(s32[16,16]{1,0:T(8,128)} %select_select_fusion.code_ref, s32[1]{0:T(128)} %bitcast.7.me_ref, bf16[768,2048]{1,0:T(8,128)(2,1)} %fusion.8.qt_ref, bf16[768,2048]{1,0:T(8,128)(2,1)} %convolution_convert_fusion.7.dt_ref, ...), custom_call_target="tpu_custom_call" | custom-call | flops 5637144576 | bytes 100663296 | tf_op jit(solution)/shard_map/attention_backward/pallas_call | solution.py:320
  487.1 17.1 %expert_gradients_1.1 = (f32[1,768,3072]{2,1,0:T(8,128)}, f32[1,3072,768]{2,1,0:T(8,128)}) custom-call(bf16[1,3072,768]{2,1,0:T(8,128)(2,1)} %all-gather.21.cloned.1.call-done.rows_ref, bf16[1,3072,768]{2,1,0:T(8,128)(2,1)} %multiply_convert_fusion.dye_ref, bf16[1,768,3072]{2,1,0:T(8,128)(2,1)} %win_ref.7, ...), custom_call_target="tpu_custom_call", output_to_operand_aliasing={{0}: (4, {}), {1}: (5, {})} | custom-call | flops 9663676416 | bytes 25165824 | tf_op jit(solution)/shard_map/expert_gradients_1/pallas_call | solution.py:477
  520.3 7.0 %convolution_convert_fusion.6.dt_ref = bf16[768,2048]{1,0:T(8,128)(2,1)} fusion(bf16[2048,768]{1,0:T(8,128)(2,1)} %bitcast.293, bf16[768,3072]{1,0:T(8,128)(2,1)} %bitcast.279), kind=kOutput, calls=%fused_computation.18 | convolution fusion | flops 2417491968 | bytes 7471104 | tf_op jit(solution)/shard_map/dot_general | solution.py:29
  529.7 29.5 %attention_backward.3 = (bf16[256,2304]{1,0:T(8,128)(2,1)}, f32[12,256]{1,0:T(8,128)}, f32[12,128]{1,0:T(8,128)}) custom-call(s32[16,16]{1,0:T(8,128)} %select_select_fusion.code_ref, s32[1]{0:T(128)} %bitcast.7.me_ref, bf16[768,2048]{1,0:T(8,128)(2,1)} %fusion.7.qt_ref, bf16[768,2048]{1,0:T(8,128)(2,1)} %convolution_convert_fusion.6.dt_ref, ...), custom_call_target="tpu_custom_call" | custom-call | flops 5637144576 | bytes 100663296 | tf_op jit(solution)/shard_map/attention_backward/pallas_call | solution.py:320
  563.6 8.1 %collective-permute-done.16 = bf16[768,768]{1,0:T(8,128)(2,1)} collective-permute-done((bf16[768,768]{1,0:T(8,128)(2,1)}, bf16[768,768]{1,0:T(8,128)(2,1)}, u32[]{:S(2)}, u32[]{:S(2)}) %collective-permute-start.16) | collective-permute-done | bytes 1179680 | tf_op jit(solution)/shard_map/ppermute | solution.py:542
  591.7 29.2 %expert_gradients_2.1 = (f32[1,768,3072]{2,1,0:T(8,128)}, f32[1,3072,768]{2,1,0:T(8,128)}) custom-call(bf16[1,3072,768]{2,1,0:T(8,128)(2,1)} %all-gather.21.cloned.1.call-done.rows_ref, bf16[1,3072,768]{2,1,0:T(8,128)(2,1)} %multiply_convert_fusion.dye_ref, bf16[1,768,3072]{2,1,0:T(8,128)(2,1)} %win_ref.7, ...), custom_call_target="tpu_custom_call", output_to_operand_aliasing={{0}: (4, {}), {1}: (5, {})} | custom-call | flops 19327352832 | bytes 50331648 | tf_op jit(solution)/shard_map/expert_gradients_2/pallas_call | solution.py:477
  641.8 5.6 collective-permute-done.33
  (566 shorter events, 275.3 us)
Async XLA Ops:
  11.3 60.8 %all-gather.25.cloned.1.call-start = ((), (), s32[]{:S(2)}) async-start(), calls=%async_computation.17 | async-start | bytes 2875392 | tf_op jit(solution)/shard_map/all_gather | solution.py:585
  36.8 74.3 %all-gather.15.cloned.1.call-start = ((), (), s32[]{:S(2)}) async-start(), calls=%async_computation.8 | async-start | bytes 3538944 | tf_op jit(solution)/shard_map/all_gather | solution.py:588
  72.1 71.0 %all-gather.27.cloned.1.call-start = ((), (), s32[]{:S(2)}) async-start(), calls=%async_computation.18 | async-start | bytes 1327104 | tf_op jit(solution)/shard_map/all_gather | solution.py:560
  84.9 52.9 %collective-permute-start.6 = (bf16[768,768]{1,0:T(8,128)(2,1)S(1)}, bf16[768,768]{1,0:T(8,128)(2,1)}, u32[]{:S(2)}, u32[]{:S(2)}) collective-permute-start(bf16[768,768]{1,0:T(8,128)(2,1)S(1)} %bitcast.269), channel_id=1, source_target_pairs={{0,24},{8,16},{16,8},{24,0},{1,25},{9,17},{17,9},{25,1},{2,26},{10... | collective-permute-start | bytes 3538952 | tf_op jit(solution)/shard_map/ppermute | solution.py:542
  87.1 52.2 %collective-permute-start.5 = (bf16[768,768]{1,0:T(8,128)(2,1)S(1)}, bf16[768,768]{1,0:T(8,128)(2,1)}, u32[]{:S(2)}, u32[]{:S(2)}) collective-permute-start(bf16[768,768]{1,0:T(8,128)(2,1)S(1)} %bitcast.270), channel_id=1, source_target_pairs={{0,16},{8,24},{16,0},{24,8},{1,17},{9,25},{17,1},{25,9},{2,18},{10... | collective-permute-start | bytes 3538952 | tf_op jit(solution)/shard_map/ppermute | solution.py:542
  87.7 51.7 %collective-permute-start.4 = (bf16[768,768]{1,0:T(8,128)(2,1)S(1)}, bf16[768,768]{1,0:T(8,128)(2,1)}, u32[]{:S(2)}, u32[]{:S(2)}) collective-permute-start(bf16[768,768]{1,0:T(8,128)(2,1)S(1)} %bitcast.271), channel_id=1, source_target_pairs={{0,8},{8,0},{16,24},{24,16},{1,9},{9,1},{17,25},{25,17},{2,10},{10... | collective-permute-start | bytes 3538952 | tf_op jit(solution)/shard_map/ppermute | solution.py:542
  112.9 48.7 %all-to-all-start = ((bf16[8,96,768]{2,1,0:T(8,128)(2,1)}), bf16[8,96,768]{2,1,0:T(8,128)(2,1)S(1)}, u32[]{:S(2)}, u32[]{:S(2)}) async-start(bf16[8,96,768]{2,1,0:T(8,128)(2,1)} %bitcast.314), calls=%async_computation | async-start | bytes 2359296 | tf_op jit(solution)/shard_map/all_to_all | solution.py:652
  116.4 99.0 %all-gather.17.cloned.1.call-start = ((), (), s32[]{:S(2)}) async-start(), calls=%async_computation.9 | async-start | bytes 3538944 | tf_op jit(solution)/shard_map/all_gather | solution.py:688
  166.5 117.4 %all-gather.19.cloned.1.call-start = ((), (), s32[]{:S(2)}) async-start(), calls=%async_computation.10 | async-start | bytes 5898240 | tf_op jit(solution)/shard_map/all_gather | solution.py:663
  215.5 124.1 %all-gather.21.cloned.1.call-start = ((), (), s32[]{:S(2)}) async-start(), calls=%async_computation.11 | async-start | bytes 5898240 | tf_op jit(solution)/shard_map/all_gather | solution.py:663
  315.1 32.9 %all-to-all-start.2 = ((bf16[8,96,768]{2,1,0:T(8,128)(2,1)}), bf16[8,96,768]{2,1,0:T(8,128)(2,1)S(1)}, u32[]{:S(2)}, u32[]{:S(2)}) async-start(bf16[8,96,768]{2,1,0:T(8,128)(2,1)} %select_convert_fusion), calls=%async_computation.2 | async-start | bytes 2359296 | tf_op jit(solution)/shard_map/all_to_all | solution.py:652
  318.7 78.4 %all-gather.29.cloned.1.call-start = ((), (), s32[]{:S(2)}) async-start(), calls=%async_computation.19 | async-start | bytes 3981312 | tf_op jit(solution)/shard_map/all_gather | solution.py:619
  404.6 41.7 %all-to-all-start.3 = ((bf16[8,96,768]{2,1,0:T(8,128)(2,1)}), bf16[8,96,768]{2,1,0:T(8,128)(2,1)S(1)}, u32[]{:S(2)}, u32[]{:S(2)}) async-start(bf16[8,96,768]{2,1,0:T(8,128)(2,1)} %bitcast.313), calls=%async_computation.4 | async-start | bytes 2359296 | tf_op jit(solution)/shard_map/all_to_all | solution.py:652
  408.3 40.8 %reduce-scatter.5.cloned.1.call-start = ((), (), s32[]{:S(2)}) async-start(), calls=%async_computation.12 | async-start | bytes 1327104 | tf_op jit(solution)/shard_map/reduce_scatter | solution.py:766
  409.0 103.8 %all-gather.31.cloned.1.call-start = ((), (), s32[]{:S(2)}) async-start(), calls=%async_computation.20 | async-start | bytes 3981312 | tf_op jit(solution)/shard_map/all_gather | solution.py:619
  469.6 102.1 %reduce-scatter.7.cloned.1.call-start = ((), (), s32[]{:S(2)}) async-start(), calls=%async_computation.13 | async-start | bytes 5308416 | tf_op jit(solution)/shard_map/reduce_scatter | solution.py:811
  516.6 104.3 %reduce-scatter.9.cloned.1.call-start = ((), (), s32[]{:S(2)}) async-start(), calls=%async_computation.14 | async-start | bytes 3981312 | tf_op jit(solution)/shard_map/reduce_scatter | solution.py:813
  516.7 46.9 %collective-permute-start.15 = (bf16[768,768]{1,0:T(8,128)(2,1)}, bf16[768,768]{1,0:T(8,128)(2,1)}, u32[]{:S(2)}, u32[]{:S(2)}) collective-permute-start(bf16[768,768]{1,0:T(8,128)(2,1)} %get-tuple-element.152), channel_id=1, source_target_pairs={{0,8},{8,0},{16,24},{24,16},{1,9},{9,1},{17,25},{25,17},{2,10},{10... | collective-permute-start | bytes 3538952 | tf_op jit(solution)/shard_map/ppermute | solution.py:542
  518.2 53.4 %collective-permute-start.16 = (bf16[768,768]{1,0:T(8,128)(2,1)}, bf16[768,768]{1,0:T(8,128)(2,1)}, u32[]{:S(2)}, u32[]{:S(2)}) collective-permute-start(bf16[768,768]{1,0:T(8,128)(2,1)} %get-tuple-element.153), channel_id=1, source_target_pairs={{0,16},{8,24},{16,0},{24,8},{1,17},{9,25},{17,1},{25,9},{2,18},{10... | collective-permute-start | bytes 3538952 | tf_op jit(solution)/shard_map/ppermute | solution.py:542
  519.7 52.0 %collective-permute-start.17 = (bf16[768,768]{1,0:T(8,128)(2,1)}, bf16[768,768]{1,0:T(8,128)(2,1)}, u32[]{:S(2)}, u32[]{:S(2)}) collective-permute-start(bf16[768,768]{1,0:T(8,128)(2,1)} %get-tuple-element.154), channel_id=1, source_target_pairs={{0,24},{8,16},{16,8},{24,0},{1,25},{9,17},{17,9},{25,1},{2,26},{10... | collective-permute-start | bytes 3538952 | tf_op jit(solution)/shard_map/ppermute | solution.py:542
  571.7 81.2 %reduce-scatter.11.cloned.1.call-start = ((), (), s32[]{:S(2)}) async-start(), calls=%async_computation.15 | async-start | bytes 1474560 | tf_op jit(solution)/shard_map/reduce_scatter | solution.py:834
  584.6 46.4 %collective-permute-start.23 = (bf16[96,3840]{1,0:T(8,128)(2,1)}, bf16[96,3840]{1,0:T(8,128)(2,1)}, u32[]{:S(2)}, u32[]{:S(2)}) collective-permute-start(bf16[96,3840]{1,0:T(8,128)(2,1)} %pad_maximum_fusion.7), channel_id=1, source_target_pairs={{0,16},{8,24},{16,0},{24,8},{1,17},{9,25},{17,1},{25,9},{2,18},{10... | collective-permute-start | bytes 2211848 | tf_op jit(solution)/shard_map/ppermute | solution.py:542
  586.1 45.0 %collective-permute-start.22 = (bf16[96,3840]{1,0:T(8,128)(2,1)}, bf16[96,3840]{1,0:T(8,128)(2,1)}, u32[]{:S(2)}, u32[]{:S(2)}) collective-permute-start(bf16[96,3840]{1,0:T(8,128)(2,1)} %pad_maximum_fusion.7), channel_id=1, source_target_pairs={{0,8},{8,0},{16,24},{24,16},{1,9},{9,1},{17,25},{25,17},{2,10},{10... | collective-permute-start | bytes 2211848 | tf_op jit(solution)/shard_map/ppermute | solution.py:542
  586.8 44.3 %collective-permute-start.24 = (bf16[96,3840]{1,0:T(8,128)(2,1)}, bf16[96,3840]{1,0:T(8,128)(2,1)}, u32[]{:S(2)}, u32[]{:S(2)}) collective-permute-start(bf16[96,3840]{1,0:T(8,128)(2,1)} %pad_maximum_fusion.7), channel_id=1, source_target_pairs={{0,24},{8,16},{16,8},{24,0},{1,25},{9,17},{17,9},{25,1},{2,26},{10... | collective-permute-start | bytes 2211848 | tf_op jit(solution)/shard_map/ppermute | solution.py:542
  (136 other events, 1576.4 us)
Sparse Core Ops, SparseCore 0:
  11.4 25.3 all-gather.22
  39.0 33.0 all-gather.24
  73.8 37.3 all-gather.14
  113.2 29.9 all-gather.26
  166.6 40.7 all-gather.16
  215.6 59.4 all-gather.18
  284.0 55.5 all-gather.20
  354.8 39.8 all-gather.28
  411.4 37.6 reduce-scatter.4
  469.7 42.9 all-gather.30
  516.8 53.8 reduce-scatter.6
  572.8 42.1 reduce-scatter.8
  623.7 29.1 reduce-scatter.10
